TPU v7x, 32 devices: a whole 2x2x4 slice. The times are simulated.
32 devices in a mesh: seq: 2 (over y), rows: 16 (over z, x, core).
Axes of the slice: x: 2, y: 2, z: 4, core: 2. Of those that a mesh axis runs over, the one named last changes fastest.
Arguments:
- hidden: bfloat16 [16, 1024, 384], P('rows', 'seq'), may hold values from -6 to 6
- grad_out: bfloat16 [16, 1024, 384], P('rows', 'seq'), may hold values from -6 to 6
- grad_mask: int32 [16, 1024], P('rows', 'seq'), may hold values from 0 to 1, as said below
- w_query: bfloat16 [384, 384], replicated, may hold values from -0.4375 to 0.4375
- w_key: bfloat16 [384, 384], replicated, may hold values from -0.4375 to 0.4375
- w_value: bfloat16 [384, 384], replicated, may hold values from -0.3125 to 0.3125
- w_output: bfloat16 [384, 384], replicated, may hold values from -1.25 to 1.25
- rel_table: bfloat16 [512, 384], replicated, may hold values from -6 to 6
- w_pos_key: bfloat16 [384, 384], replicated, may hold values from -0.4375 to 0.4375
- w_pos_query: bfloat16 [384, 384], replicated, may hold values from -0.4375 to 0.4375
- attn_biases: bfloat16 [4, 384], replicated, may hold values from -1.796875 to 1.796875
- norm_gains: bfloat16 [2, 384], replicated, may hold values from 0.25 to 1.75
- norm_shifts: bfloat16 [2, 384], replicated, may hold values from -1.796875 to 1.796875
- w_inner: bfloat16 [384, 1536], replicated, may hold values from -0.3125 to 0.3125
- inner_bias: bfloat16 [1536], replicated, may hold values from -1.796875 to 1.796875
- w_outer: bfloat16 [1536, 384], replicated, may hold values from -0.15625 to 0.15625
- outer_bias: bfloat16 [384], replicated, may hold values from -1.796875 to 1.796875
Outputs:
- result: bfloat16 [16, 1024, 384], P('rows', 'seq')
- grad_hidden: bfloat16 [16, 1024, 384], P('rows', 'seq')
- grad_w_query: float32 [384, 384], P('rows')
- grad_w_key: float32 [384, 384], P('rows')
- grad_w_value: float32 [384, 384], P('rows')
- grad_w_output: float32 [384, 384], P('rows')
- grad_rel_table: float32 [512, 384], P(None, 'rows')
- grad_w_pos_key: float32 [384, 384], P('rows')
- grad_w_pos_query: float32 [384, 384], P('rows')
- grad_attn_biases: float32 [4, 384], P(None, 'rows')
- grad_norm_gains: float32 [2, 384], P(None, 'rows')
- grad_norm_shifts: float32 [2, 384], P(None, 'rows')
- grad_w_inner: float32 [384, 1536], P('rows')
- grad_inner_bias: float32 [1536], replicated
- grad_w_outer: float32 [1536, 384], P(None, 'rows')
- grad_outer_bias: float32 [384], P('rows')
Inputs may be any that keep to these rules, and one draw needn't show every extreme that they name: `grad_mask`: in every sequence a share of the positions is 1, taken as 1024 * p // 100 positions where the sequences' p run evenly from 5 to 40 over the 16 sequences in an order drawn from the seed; the marked positions are spread at random.
All inputs are finite; a program needn't handle non-finite values.
Results may differ from a plain program's by a relative error of at most 0.02.
Values may be sent and summed in bfloat16 or wider, within the bound.
No kernel may reach another device: no remote copies, remote signals or barrier semaphores. Data moves between devices by JAX's collectives and lax.ppermute only.
A program may use at most 128 MiB of HBM per device.

v0:
```python
from functools import partial
import math

import jax
import jax.numpy as jnp
import numpy as np
from jax import lax
from jax.experimental import pallas as pl
from jax.experimental.pallas import tpu as pltpu
from jax.sharding import PartitionSpec as P

HEADS = 6
PAIRS = HEADS // 2
TILE = 128
norm_eps = 1e-07
masked_score = -1e30
f32 = jnp.float32
bf16 = jnp.bfloat16
MiB = 1 << 20


def nn(left, right):
    return lax.dot_general(left, right, (((1,), (0,)), ((), ())), preferred_element_type=f32)


def nt(left, right):
    return lax.dot_general(left, right, (((1,), (1,)), ((), ())), preferred_element_type=f32)


def iota(shape, axis):
    return lax.broadcasted_iota(jnp.int32, shape, axis)


def where_bf16(mask, value):
    return jnp.where(mask, value.astype(f32), 0.0).astype(bf16)


def skew(block, first):
    return pltpu.roll(block, first, 1, stride=1, stride_axis=0)


def column_cut(columns):
    cut = columns // (4 * TILE) * (2 * TILE) + columns % (2 * TILE)
    return cut, (columns - cut) // 2


def store_halves(keep, send, first, value):
    value = value.astype(bf16)
    half = value.shape[0] // 2
    keep[:, first : first + value.shape[1]] = value[:half]
    send[:, first : first + value.shape[1]] = value[half:]


def store_parts(keep, send, first, value):
    cut, part = column_cut(keep.shape[1])
    bit = lax.axis_index("seq") % 2
    value = value.astype(bf16)
    half = value.shape[0] // 2
    ahead = min(max(cut - first, 0), value.shape[1])
    if ahead:
        keep[:, first : first + ahead] = value[:half, :ahead]
        send[:, first : first + ahead] = value[half:, :ahead]
    for c in range(ahead, value.shape[1], TILE):
        which, offset = divmod(first + c - cut, part)
        place = cut + jnp.bitwise_xor(which, bit) * part + offset
        cols = pl.ds(pl.multiple_of(place, TILE), TILE)
        keep[:, cols] = value[:half, c : c + TILE]
        send[:, cols] = value[half:, c : c + TILE]


def exchange(value, axis, bit):
    count = lax.axis_size(axis)
    return lax.ppermute(value, axis, [(i, i ^ bit) for i in range(count)])


def project_kernel(*refs):
    sources, outs, held, arrived = refs[:9], refs[9:20], refs[20:29], refs[29]
    q_out, k_out, v_out, pk_out, pk_rev_out, pq_rev_out, order_out = outs[:7]
    x_turned, rel_turned, w_pk_ordered, w_pq_ordered = outs[7:]
    places, x, w_query, w_key, w_value, rel, w_pos_key, w_pos_query, biases = held
    copies = [
        pltpu.make_async_copy(source, target, arrived.at[i])
        for i, (source, target) in enumerate(zip(sources, held))
    ]
    for copy in copies:
        copy.start()

    def split(out, value):
        for p in range(PAIRS):
            out[p] = value[:, p * TILE : (p + 1) * TILE].astype(bf16)

    width = order_out.shape[0]
    copies[0].wait()
    shard = jnp.bitwise_xor(places[:, 0:1], lax.axis_index("rows"))
    target = shard * places[0, 2] + places[:, 1:2]
    order_out[...] = jnp.where(iota((width, width), 1) == target, 1.0, 0.0).astype(bf16)
    for copy in copies[1:]:
        copy.wait()
    bias = biases[...].astype(f32)
    split(q_out, nn(x[...], w_query[...]) + bias[0:1])
    split(k_out, nn(x[...], w_key[...]))
    split(v_out, nn(x[...], w_value[...]) + bias[1:2])
    count = rel.shape[0]
    pos_keys = nn(rel[...], w_pos_key[...]).astype(bf16)
    pos_queries = (nn(rel[...], w_pos_query[...]) + bias[2:3]).astype(bf16)
    row, col = iota((count, count), 0), iota((count, count), 1)
    flip = jnp.where(col == count - 1 - row, 1.0, 0.0).astype(bf16)
    pick = jnp.where(col == jnp.minimum(count - row, count - 1), 1.0, 0.0).astype(bf16)
    split(pk_out, pos_keys)
    split(pk_rev_out, nn(flip, pos_keys))
    split(pq_rev_out, nn(pick, pos_queries))
    x_turned[...] = nt(order_out[...], x[...]).astype(bf16)
    rel_turned[...] = nt(order_out[...], rel[...]).astype(bf16)
    w_pk_ordered[...] = nn(order_out[...], w_pos_key[...]).astype(bf16)
    w_pq_ordered[...] = nn(order_out[...], w_pos_query[...]).astype(bf16)


def key_block_range(wb, blocks, tiles):
    low, high = max(0, blocks - 1 - wb), min(blocks - 1, tiles + blocks - 2 - wb)
    return low, high, max(low - 1, 0), min(high, blocks - 2)


def attend_kernel(q, k_own, v_own, pk_rev, pq_rev, w_key, w_value, biases, *refs, scale, n_seq):
    edges, refs = refs[:-6], refs[-6:]

    def one_pair(p, carry):
        attend_pair(
            p, q, k_own, v_own, pk_rev, pq_rev, w_key, w_value, biases, edges, *refs, scale, n_seq
        )
        return carry

    lax.fori_loop(0, PAIRS, one_pair, 0)


def attend_pair(
    p,
    q,
    k_own,
    v_own,
    pk_rev,
    pq_rev,
    w_key,
    w_value,
    biases,
    edges,
    context,
    probs,
    k,
    v,
    from_scr,
    score_scr,
    scale,
    n_seq,
):
    me_seq = lax.axis_index("seq")
    cols = pl.ds(pl.multiple_of(p * TILE, TILE), TILE)
    span, block = edges[0].shape[0], k_own.shape[1]
    k[p, span : span + block, :] = k_own[p]
    v[p, span : span + block, :] = v_own[p]
    bias = biases[1:2, cols].astype(f32)
    both = jnp.concatenate([w_key[:, cols], w_value[:, cols]], axis=1)
    sides = ((0, span + block),) if len(edges) == 1 else ((0,), (span + block,))
    for firsts, source in zip(sides, edges):
        product = nn(source[...], both)
        for first in firsts:
            k[p, first : first + span, :] = product[:, :TILE].astype(bf16)
            v[p, first : first + span, :] = (product[:, TILE:] + bias).astype(bf16)
    row, lane = iota((TILE, TILE), 0), iota((TILE, TILE), 1)
    eye = jnp.where(row == lane, 1.0, 0.0).astype(bf16)
    halves = (lane < TILE // 2, lane >= TILE // 2)
    tiles = q.shape[1] // TILE
    blocks = pk_rev.shape[1] // TILE + 1
    side = blocks // 2
    tables = []
    for h in range(2):
        table = pq_rev[p].astype(f32)
        half = iota((table.shape[0], TILE), 1) // (TILE // 2) == h
        tables.append(jnp.where(half, table, 0.0).astype(bf16))
    for wb in range(tiles + blocks - 1):
        low, high, first, last = key_block_range(wb, blocks, tiles)
        kb = k[p, wb * TILE : (wb + 1) * TILE, :]
        span = slice(first * TILE, (last + 1) * TILE)
        product = nt(kb, jnp.concatenate([tables[0][span], tables[1][span]], axis=0))
        for h in range(2):
            turned = {}
            for a in range(first, last + 1):
                at = (h * (last + 1 - first) + a - first) * TILE
                turned[a] = skew(product[:, at : at + TILE], 0)
            for e in range(low, high + 1):
                if e == 0:
                    term = turned[0]
                elif e == blocks - 1:
                    term = turned[blocks - 2]
                else:
                    term = jnp.where(lane >= row, turned[e], turned[e - 1])
                it, b = wb - (blocks - 1) + e, blocks - 1 - e
                from_scr[h, it, b * TILE : (b + 1) * TILE, :] = term.astype(bf16)
    before = jnp.where(me_seq == 0, masked_score, 0.0)
    after = jnp.where(me_seq == n_seq - 1, masked_score, 0.0)
    rate = scale * math.log2(math.e)
    chains = [(it, h) for it in range(tiles) for h in range(2)]
    stacked = jnp.concatenate(
        [where_bf16(halves[h], q[p, it * TILE : (it + 1) * TILE, :]) for it, h in chains], axis=0
    )
    product = nt(stacked, pk_rev[p])
    tops = []
    for n, (it, h) in enumerate(chains):
        rows = slice(n * TILE, (n + 1) * TILE)
        turned = [
            skew(product[rows, b * TILE : (b + 1) * TILE], 1) for b in range(blocks - 1)
        ]
        left = jnp.concatenate([stacked[rows], eye], axis=1)
        right = jnp.concatenate(
            [k[p, it * TILE : (it + blocks) * TILE, :], from_scr[h, it]], axis=1
        )
        content = nt(left, right)
        largest = None
        for b in range(blocks):
            score = content[:, b * TILE : (b + 1) * TILE]
            if b == 0:
                score = jnp.where(lane > row, score + turned[0], masked_score)
            elif b == blocks - 1:
                score = jnp.where(lane <= row, score + turned[b - 1], masked_score)
            else:
                score = score + jnp.where(lane > row, turned[b], turned[b - 1])
            if it + b < side:
                score = score + before
            if it + b >= side + tiles:
                score = score + after
            score_scr[n, :, b * TILE : (b + 1) * TILE] = score
            largest = score if largest is None else jnp.maximum(largest, score)
        tops.append(largest)
    tops = [jnp.max(top, axis=1, keepdims=True) for top in tops]
    totals = []
    for n in range(len(chains)):
        weight = jnp.exp2((score_scr[n] - tops[n]) * rate)
        score_scr[n] = weight
        total = weight[:, :TILE]
        for b in range(1, blocks):
            total = total + weight[:, b * TILE : (b + 1) * TILE]
        totals.append(total)
    inverses = [1.0 / jnp.sum(total, axis=1, keepdims=True) for total in totals]
    for n, (it, h) in enumerate(chains):
        probs[p, h, it] = (score_scr[n] * inverses[n]).astype(bf16)
    for it in range(tiles):
        both = jnp.concatenate([probs[p, 0, it], probs[p, 1, it]], axis=0)
        part = nn(both, v[p, it * TILE : (it + blocks) * TILE, :])
        context[it * TILE : (it + 1) * TILE, cols] = jnp.where(
            halves[0], part[:TILE], part[TILE:]
        ).astype(bf16)


def attend_back_kernel(
    q,
    k,
    v,
    pk,
    pq_rev,
    d_context,
    context,
    probs,
    dq_out,
    dk_out,
    dv_out,
    dpk_out,
    dpq_out,
    ds_scr,
    merged_scr,
    band_scr,
    turn_scr,
    shifted_scr,
    dv_scr,
    *,
    scale,
    p,
):
    row, lane = iota((TILE, TILE), 0), iota((TILE, TILE), 1)
    flip = jnp.where(row + lane == TILE - 1, 1.0, 0.0).astype(bf16)
    row2, lane2 = iota((2 * TILE, 2 * TILE), 0), iota((2 * TILE, 2 * TILE), 1)
    same = (row2 // TILE) == (lane2 // TILE)
    flip2 = jnp.where(
        same & (row2 % TILE + lane2 % TILE == TILE - 1), 1.0, 0.0
    ).astype(bf16)
    halves = (lane < TILE // 2, lane >= TILE // 2)
    row_halves = (row < TILE // 2, row >= TILE // 2)
    cols = slice(p * TILE, (p + 1) * TILE)
    tiles = q.shape[1] // TILE
    blocks = pk.shape[1] // TILE + 1
    keys = tiles + blocks - 1
    pairs = (blocks - 1) // 2

    def part(index):
        return slice(index * TILE, (index + 1) * TILE)

    def window(it):
        return slice(it * TILE, (it + blocks) * TILE)

    def split_rows(value):
        return jnp.concatenate([where_bf16(halves[h], value) for h in range(2)], axis=0)

    def split_turned(value):
        flat = value.astype(f32).T
        return [jnp.where(row_halves[h], flat, 0.0).astype(bf16) for h in range(2)]

    stacked_q = [split_rows(q[p, part(it), :]) for it in range(tiles)]
    for it in range(tiles):
        dct = d_context[part(it), cols]
        overlap = dct.astype(f32) * context[part(it), cols].astype(f32)
        delta = jnp.concatenate(
            [
                jnp.sum(jnp.where(halves[h], overlap, 0.0), axis=1, keepdims=True)
                for h in range(2)
            ],
            axis=0,
        )
        d_probs = nt(split_rows(dct), v[p, window(it), :])
        weights = jnp.concatenate([probs[p, 0, it], probs[p, 1, it]], axis=0)
        ds = weights.astype(f32) * (d_probs - delta) * scale
        ds_scr[it] = ds.astype(bf16)
        for h in range(2):
            for b in range(blocks - 1):
                merged = jnp.where(lane > row, ds[part(h), part(b)], ds[part(h), part(b + 1)])
                at = (it * 2 + h) * pairs + b // 2
                merged_scr[part(at), part(b % 2)] = merged.astype(bf16)
    flipped = nn(merged_scr[...], flip2)
    for it in range(tiles):
        for h in range(2):
            for b in range(blocks - 1):
                at = (it * 2 + h) * pairs + b // 2
                band_scr[part(it * 2 + h), part(blocks - 2 - b)] = skew(
                    flipped[part(at), part(b % 2)], 1
                ).astype(bf16)
    for it in range(tiles):
        for b in range(blocks):
            turn_scr[it, b] = nt(flip, ds_scr[it, :, part(b)]).astype(bf16)
    for it in range(tiles):
        both = slice(2 * it * TILE, 2 * (it + 1) * TILE)
        total = nn(
            jnp.concatenate([ds_scr[it], band_scr[both, :]], axis=1),
            jnp.concatenate([k[p, window(it), :], pk[p]], axis=0),
        )
        dq_out[part(it), :] = jnp.where(halves[0], total[:TILE], total[TILE:]).astype(bf16)
    turned = [split_turned(q[p, part(it), :]) for it in range(tiles)]
    dpk_out[...] = nn(jnp.concatenate(sum(turned, []), axis=1), band_scr[...]).astype(bf16)
    dv_scr[...] = jnp.zeros_like(dv_scr)
    for it in range(tiles):
        dv_scr[:, window(it)] += nn(
            jnp.concatenate(split_turned(d_context[part(it), cols]), axis=1),
            jnp.concatenate([probs[p, 0, it], probs[p, 1, it]], axis=0),
        )

    tables = []
    for h in range(2):
        table = pq_rev[p].astype(f32)
        half = iota((table.shape[0], TILE), 1) // (TILE // 2) == h
        tables.append(jnp.where(half, table, 0.0).astype(bf16))
    for wb in range(keys):
        low, high, first, last = key_block_range(wb, blocks, tiles)

        def source(e, h):
            if e < low or e > high:
                return jnp.zeros((TILE, TILE), f32)
            it, b = wb - (blocks - 1) + e, blocks - 1 - e
            return turn_scr[it, b, :, part(h)].astype(f32)

        for h in range(2):
            for a in range(blocks - 1):
                if first <= a <= last:
                    merged = jnp.where(lane + row >= TILE - 1, source(a, h), source(a + 1, h))
                    shifted_scr[part(2 * wb + h), part(a)] = skew(merged, 1).astype(bf16)
                else:
                    shifted_scr[part(2 * wb + h), part(a)] = jnp.zeros((TILE, TILE), bf16)
    lows = []
    for wb in range(keys):
        low, high, first, last = key_block_range(wb, blocks, tiles)
        left, right = [], []
        for e in range(low, high + 1):
            it, b = wb - (blocks - 1) + e, blocks - 1 - e
            left.append(turn_scr[it, b])
            right.append(stacked_q[it])
        span = slice(first * TILE, (last + 1) * TILE)
        for h in range(2):
            left.append(shifted_scr[part(2 * wb + h), span])
            right.append(tables[h][span])
        total = nn(jnp.concatenate(left, axis=1), jnp.concatenate(right, axis=0))
        lows.append(total.astype(bf16))
    natural = nn(flip, jnp.concatenate(lows, axis=1)).astype(bf16)
    for wb in range(keys):
        dk_out[part(wb), :] = natural[:, part(wb)]
    reverse = nn(flip, jnp.concatenate([k[p, part(wb), :] for wb in range(keys)], axis=1))
    turned = sum([split_turned(reverse[:, part(wb)]) for wb in range(keys)], [])
    dpq_out[...] = nn(jnp.concatenate(turned, axis=1), shifted_scr[...]).astype(bf16)
    for wb in range(keys):
        dv_out[part(wb), :] = dv_scr[:, part(wb)].T.astype(bf16)


def norm_parts(value):
    centre = value - jnp.mean(value, axis=1, keepdims=True)
    rate = lax.rsqrt(jnp.mean(centre * centre, axis=1, keepdims=True) + norm_eps)
    return centre * rate, rate


def norm_back(cotangent, normal, rate):
    return rate * (
        cotangent
        - jnp.mean(cotangent, axis=1, keepdims=True)
        - normal * jnp.mean(cotangent * normal, axis=1, keepdims=True)
    )


def middle_kernel(
    x,
    context,
    grad_out,
    mask,
    w_output,
    biases,
    gains,
    shifts,
    w_inner,
    inner_bias,
    w_outer,
    outer_bias,
    order,
    result,
    d_first_out,
    d_context,
    keep,
    send,
    rows_out,
    low_scr,
    active_scr,
    d_inner_scr,
    d_outer_scr,
    d_att_scr,
    *,
    step,
    share,
):
    tokens, width = x.shape
    units = w_inner.shape[1]
    bias = biases[3:4, :].astype(f32)
    gain_one, gain_two = gains[0:1, :].astype(f32), gains[1:2, :].astype(f32)
    shift_one, shift_two = shifts[0:1, :].astype(f32), shifts[1:2, :].astype(f32)
    in_bias = inner_bias[...].astype(f32).reshape(1, units)
    out_bias = outer_bias[...].astype(f32).reshape(1, width)
    diagonal = iota((TILE, TILE), 0) == iota((TILE, TILE), 1)
    sums = [jnp.zeros((1, width), f32) for _ in range(6)]

    def add(index, value):
        sums[index] = sums[index] + jnp.sum(value, axis=0, keepdims=True)

    parts = [slice(first, first + step) for first in range(0, tokens, step)]
    first_norm, slopes, second = [], [], []
    for rows in parts:
        attended = nn(context[rows, :], w_output[...]) + bias
        n_one, r_one = norm_parts(x[rows, :].astype(f32) + attended)
        normed = n_one * gain_one + shift_one
        low_scr[rows, :] = normed.astype(bf16)
        first_norm.append((n_one, r_one, normed))
    for rows in parts:
        inner = nn(low_scr[rows, :], w_inner[...]) + in_bias
        cumulative = 0.5 + 0.5 * lax.erf(inner * math.sqrt(0.5))
        active_scr[rows, :] = (inner * cumulative).astype(bf16)
        slopes.append(
            cumulative + inner * jnp.exp(-0.5 * inner * inner) * (1.0 / math.sqrt(2 * math.pi))
        )
    for rows, (_, _, normed) in zip(parts, first_norm):
        outer = nn(active_scr[rows, :], w_outer[...]) + out_bias
        n_two, r_two = norm_parts(normed + outer)
        result[rows, :] = (n_two * gain_two + shift_two).astype(bf16)
        columns = []
        for part in range(rows.start, rows.stop, TILE):
            line = mask[0:1, part : part + TILE].astype(f32)
            columns.append(jnp.sum(jnp.where(diagonal, line, 0.0), axis=1, keepdims=True))
        cotangent = grad_out[rows, :].astype(f32) * jnp.concatenate(columns, axis=0)
        add(0, cotangent * n_two)
        add(1, cotangent)
        d_second = norm_back(cotangent * gain_two, n_two, r_two)
        d_outer = d_second.astype(bf16)
        d_outer_scr[rows, :] = d_outer
        add(2, d_outer.astype(f32))
        second.append(d_second)
    for rows, slope in zip(parts, slopes):
        d_inner_scr[rows, :] = (nt(d_outer_scr[rows, :], w_outer[...]) * slope).astype(bf16)
    for rows, d_second, (n_one, r_one, _) in zip(parts, second, first_norm):
        d_normed = d_second + nt(d_inner_scr[rows, :], w_inner[...])
        add(3, d_normed * n_one)
        add(4, d_normed)
        d_first = norm_back(d_normed * gain_one, n_one, r_one)
        d_first_out[rows, :] = d_first
        d_att = d_first.astype(bf16)
        d_att_scr[rows, :] = d_att
        add(5, d_att.astype(f32))
    for rows in parts:
        d_context[rows, :] = nt(d_att_scr[rows, :], w_output[...]).astype(bf16)

    def put(first, left, right):
        turned = nt(order[...], left).astype(bf16)
        for c in range(0, right.shape[1], width):
            store_halves(keep, send, first + c, nn(turned, right[:, c : c + width]))

    put(0, low_scr[...], d_inner_scr)
    put(units, d_outer_scr[...], active_scr)
    line = nn(jnp.ones((8, tokens), bf16), d_inner_scr[...])[0:1]
    lines = [line[:, c : c + TILE] for c in range(0, units, TILE)]
    lines = jnp.concatenate(lines + [jnp.zeros((share - len(lines), TILE), f32)] * (share > len(lines)), axis=0)
    lines = jnp.concatenate([lines] * (width // share), axis=0)
    store_halves(keep, send, 2 * units, lines)
    zero = jnp.zeros((1, width), f32)
    table = [zero, zero, zero, sums[5], sums[3], sums[0], sums[4], sums[1], sums[2]]
    rows_out[...] = jnp.concatenate(table + [zero] * (16 - len(table)), axis=0)


def weight_grad_kernel(
    x_t, rel_t, w_pk_t, w_pq_t, order, rows, context, d_first, *refs, n_seq
):
    edges = refs[: 1 if n_seq == 2 else 2]
    backs, (keep, send) = refs[len(edges) : -2], refs[-2:]
    width, block = x_t.shape
    count = rel_t.shape[1]
    span = count // 2
    put = partial(store_parts, keep, send)

    def joined(index, rows=slice(None), axis=1):
        some = backs[PAIRS * index : PAIRS * (index + 1)]
        return jnp.concatenate([ref[rows, :] for ref in some], axis=axis)

    ord_ = order[...]
    dq = joined(0)
    put(0, nn(x_t[...], dq))
    turned = [nt(ord_, edge[...]).astype(bf16) for edge in edges] + [x_t[...]]
    if n_seq == 2:
        first = pl.multiple_of((1 - lax.axis_index("seq")) * (span + block), TILE)
        places = [pl.ds(first, span)]
    else:
        places = [slice(0, span), slice(span + block, 2 * span + block)]
    places.append(slice(span, span + block))
    left = jnp.concatenate(turned, axis=1)
    dk, dv = (jnp.concatenate([joined(i, r) for r in places], axis=0) for i in (1, 2))
    put(width, nn(left, dk))
    put(2 * width, nn(left, dv))
    context_t = nt(ord_, context[...]).astype(bf16)
    put(5 * width, nn(context_t, d_first[...].astype(bf16)))
    dpk, dpq = joined(3, axis=0), joined(4, axis=0)
    put(3 * width, nt(rel_t[...], dpk))
    row, col = iota((count, count), 0), iota((count, count), 1)
    pick = jnp.where(col == jnp.minimum(count - row, count - 1), 1.0, 0.0).astype(bf16)
    dpq_nat = nn(dpq, pick).astype(bf16)
    put(4 * width, nt(rel_t[...], dpq_nat))
    rel_grad = nn(w_pk_t[...], dpk)
    rel_grad = rel_grad + nn(w_pq_t[...], dpq_nat)
    put(6 * width, rel_grad)
    known = rows[...]
    sum_q = nn(jnp.ones((8, block), bf16), dq)[0:1]
    sum_v = nn(jnp.ones((8, dv.shape[0]), bf16), dv)[0:1]
    sum_p = nt(jnp.ones((8, count), bf16), dpq_nat)[0:1]
    place = iota(known.shape, 0)
    known = jnp.where(place == 0, sum_q, known)
    known = jnp.where(place == 1, sum_v, known)
    known = jnp.where(place == 2, sum_p, known)
    padded = jnp.concatenate([known, jnp.zeros((TILE - known.shape[0], width), f32)], axis=0)
    put(6 * width + count, nt(ord_, padded.astype(bf16)))


def input_grad_kernel(
    dq0, dq1, dq2, dk0, dk1, dk2, dv0, dv1, dv2, d_first, w_query, w_key, w_value, own, *outs
):
    span = outs[0].shape[0]
    block = own.shape[0]

    def joined(refs, rows):
        return jnp.concatenate([ref[rows, :] for ref in refs], axis=1)

    def halo(rows):
        return nt(joined((dk0, dk1, dk2), rows), w_key[...]) + nt(
            joined((dv0, dv1, dv2), rows), w_value[...]
        )

    if len(outs) == 1:
        first = pl.multiple_of((1 - lax.axis_index("seq")) * (span + block), TILE)
        outs[0][...] = halo(pl.ds(first, span)).astype(bf16)
    else:
        outs[0][...] = halo(slice(0, span)).astype(bf16)
        outs[1][...] = halo(slice(span + block, 2 * span + block)).astype(bf16)
    dq = jnp.concatenate([dq0[...], dq1[...], dq2[...]], axis=1)
    own[...] = halo(slice(span, span + block)) + d_first[...] + nt(dq, w_query[...])


def final_kernel(*refs, width, units, count):
    (g_q, g_k, g_v, g_o, g_rel, g_pk, g_pq, g_bias, g_gain, g_shift, g_in, g_out, g_ob, g_ib) = (
        refs[6:]
    )
    low = lax.axis_index("seq") % 2 == 0

    def joined(one, one_other, two, two_other):
        mine, other = two[...].astype(f32), two_other[...].astype(f32)
        return jnp.concatenate(
            [
                one[...].astype(f32) + one_other[...].astype(f32),
                jnp.where(low, mine, other),
                jnp.where(low, other, mine),
            ],
            axis=1,
        )

    mid = refs[0][...].astype(f32) + refs[1][...].astype(f32)
    rest = joined(*refs[2:6])
    g_in[...] = mid[:, :units]
    g_out[...] = mid[:, units : 2 * units]
    g_ib[...] = mid[: units // TILE, 2 * units :]
    for i, out in enumerate((g_q, g_k, g_v, g_pk, g_pq, g_o)):
        out[...] = rest[:, i * width : (i + 1) * width]
    g_rel[...] = rest[:, 6 * width : 6 * width + count]
    lines = rest[:, 6 * width + count :].T
    g_bias[...] = lines[0:4]
    g_gain[...] = lines[4:6]
    g_shift[...] = lines[6:8]
    g_ob[...] = lines[8:9]


def bit_reversed(value, bits):
    out = 0
    for _ in range(bits):
        out = out * 2 + value % 2
        value //= 2
    return out


def local(
    hidden,
    grad_out,
    grad_mask,
    w_query,
    w_key,
    w_value,
    w_output,
    rel_table,
    w_pos_key,
    w_pos_query,
    attn_biases,
    norm_gains,
    norm_shifts,
    w_inner,
    inner_bias,
    w_outer,
    outer_bias,
):
    count, block, width = hidden.shape
    tokens = count * block
    table = rel_table.shape[0]
    span = table // 2
    window = block + 2 * span
    units = w_inner.shape[1]
    head = width // HEADS
    scale = 1.0 / math.sqrt(3.0 * head)
    n_rows, n_seq = lax.axis_size("rows"), lax.axis_size("seq")
    row_bits, seq_bits = n_rows.bit_length() - 1, n_seq.bit_length() - 1
    share = width // n_rows
    tiles, blocks = block // TILE, table // TILE + 1
    me_seq = lax.axis_index("seq")
    x = hidden.reshape(tokens, width)
    shape = jax.ShapeDtypeStruct

    forward = [(i, i + 1) for i in range(n_seq - 1)]
    backward = [(i + 1, i) for i in range(n_seq - 1)]
    if n_seq == 2:
        start = (1 - me_seq) * (block - span)
        x_low = exchange(lax.dynamic_slice_in_dim(x, start, span, axis=0), "seq", 1)
        x_high = x_low
    else:
        x_low = lax.ppermute(x[block - span :], "seq", forward)
        x_high = lax.ppermute(x[:span], "seq", backward)

    outside = (x_low,) if n_seq == 2 else (x_low, x_high)
    places = np.zeros((width, 4), np.int32)
    for i in range(width):
        places[i] = (bit_reversed(i // share, row_bits), i % share, share, 0)

    loaded = (
        jnp.asarray(places),
        x,
        w_query,
        w_key,
        w_value,
        rel_table,
        w_pos_key,
        w_pos_query,
        attn_biases,
    )
    q3, k3, v3, pk3, pk_rev3, pq_rev3, order, x_t, rel_t, w_pk_t, w_pq_t = pl.pallas_call(
        project_kernel,
        out_shape=(
            shape((PAIRS, block, TILE), bf16),
            shape((PAIRS, block, TILE), bf16),
            shape((PAIRS, block, TILE), bf16),
            shape((PAIRS, table, TILE), bf16),
            shape((PAIRS, table, TILE), bf16),
            shape((PAIRS, table, TILE), bf16),
            shape((width, width), bf16),
            shape((width, tokens), bf16),
            shape((width, table), bf16),
            shape((width, width), bf16),
            shape((width, width), bf16),
        ),
        in_specs=[pl.BlockSpec(memory_space=pltpu.HBM)] * len(loaded),
        scratch_shapes=[pltpu.VMEM(a.shape, a.dtype) for a in loaded]
        + [pltpu.SemaphoreType.DMA((len(loaded),))],
        compiler_params=pltpu.CompilerParams(vmem_limit_bytes=12 * MiB),
        name="project",
    )(*(pltpu.with_memory_space_constraint(a, pltpu.HBM) for a in loaded))
    probs_shape = (PAIRS, 2, tiles, TILE, blocks * TILE)
    context, probs, k3, v3 = pl.pallas_call(
        partial(attend_kernel, scale=scale, n_seq=n_seq),
        out_shape=(
            shape((tokens, width), bf16),
            shape(probs_shape, bf16),
            shape((PAIRS, window, TILE), bf16),
            shape((PAIRS, window, TILE), bf16),
        ),
        scratch_shapes=[
            pltpu.VMEM((2, tiles, blocks * TILE, TILE), bf16),
            pltpu.VMEM((2 * tiles, TILE, blocks * TILE), f32),
        ],
        compiler_params=pltpu.CompilerParams(vmem_limit_bytes=20 * MiB),
        name="attend",
    )(q3, k3, v3, pk_rev3, pq_rev3, w_key, w_value, attn_biases, *outside)

    mid_cols = 2 * units + TILE
    result, d_first, d_context, mid_keep, mid_send, rows = pl.pallas_call(
        partial(middle_kernel, step=512, share=share),
        out_shape=(
            shape((tokens, width), bf16),
            shape((tokens, width), f32),
            shape((tokens, width), bf16),
            shape((width // 2, mid_cols), bf16),
            shape((width // 2, mid_cols), bf16),
            shape((16, width), f32),
        ),
        scratch_shapes=[
            pltpu.VMEM((tokens, width), bf16),
            pltpu.VMEM((tokens, units), bf16),
            pltpu.VMEM((tokens, units), bf16),
            pltpu.VMEM((tokens, width), bf16),
            pltpu.VMEM((tokens, width), bf16),
        ],
        compiler_params=pltpu.CompilerParams(vmem_limit_bytes=22 * MiB),
        name="middle",
    )(
        x,
        context,
        grad_out.reshape(tokens, width),
        grad_mask,
        w_output,
        attn_biases,
        norm_gains,
        norm_shifts,
        w_inner,
        inner_bias,
        w_outer,
        outer_bias,
        order,
    )

    def back(p, d_context):
        return pl.pallas_call(
            partial(attend_back_kernel, scale=scale, p=p),
            out_shape=(
                shape((block, TILE), bf16),
                shape((window, TILE), bf16),
                shape((window, TILE), bf16),
                shape((TILE, table), bf16),
                shape((TILE, table), bf16),
            ),
            scratch_shapes=[
                pltpu.VMEM((tiles, 2 * TILE, blocks * TILE), bf16),
                pltpu.VMEM((tiles * (blocks - 1) * TILE, 2 * TILE), bf16),
                pltpu.VMEM((2 * tiles * TILE, table), bf16),
                pltpu.VMEM((tiles, blocks, TILE, 2 * TILE), bf16),
                pltpu.VMEM((2 * window, table), bf16),
                pltpu.VMEM((TILE, window), f32),
            ],
            compiler_params=pltpu.CompilerParams(vmem_limit_bytes=20 * MiB),
            cost_estimate=pl.CostEstimate(
                flops=1000, bytes_accessed=1000, transcendentals=0
            ),
            name="attend_back",
        )(q3, k3, v3, pk3, pq_rev3, d_context, context, probs)

    def tied(first, second):
        return lax.optimization_barrier((first, second))

    def halves(total):
        return total[: total.shape[0] // 2], total[total.shape[0] // 2 :]

    def row_begin(total, step):
        keep, send = halves(total)
        return keep, exchange(send, "rows", 1 << step)

    def row_step(total, step):
        keep, received = row_begin(total, step)
        return keep + received

    def seq_step(total, step):
        return total + exchange(total, "seq", 1 << step)

    def opened(total):
        cut, part = column_cut(total.shape[1])
        one = row_step(total[:, :cut], 1)
        two = total[:, cut : cut + part] + exchange(total[:, cut + part :], "seq", 1)
        return one, two

    def finished(one, two, first=2):
        for step in range(first, row_bits + 1):
            if step < row_bits:
                one = row_step(one, step)
            two = row_step(two, step - 1)
        for step in range(seq_bits - 1):
            one = seq_step(one, step)
            two = seq_step(two, step + 1)
        return one, exchange(one, "seq", 1 << (seq_bits - 1)), two, exchange(two, "seq", 1)

    received = exchange(mid_send, "rows", 1)
    back0 = back(0, d_context)
    mid_keep, dq0 = tied(mid_keep, back0[0])
    mid = mid_keep + received
    mid, d_context = tied(mid, d_context)
    keep, send = halves(mid)
    back1 = back(1, d_context)
    received = exchange(send, "rows", 2)
    back2 = back(2, d_context)
    dq1, dq2 = back1[0], back2[0]
    mid = keep + received
    dq = (dq0, dq1, dq2)
    dk, dv, dpk, dpq = ((back0[i], back1[i], back2[i]) for i in range(1, 5))

    rest_cols = 6 * width + table + TILE
    rest_keep, rest_send = pl.pallas_call(
        partial(weight_grad_kernel, n_seq=n_seq),
        out_shape=(
            shape((width // 2, rest_cols), bf16),
            shape((width // 2, rest_cols), bf16),
        ),
        compiler_params=pltpu.CompilerParams(vmem_limit_bytes=20 * MiB),
        cost_estimate=pl.CostEstimate(flops=1000, bytes_accessed=1000, transcendentals=0),
        name="weight_grad",
    )(x_t, rel_t, w_pk_t, w_pq_t, order, rows, context, d_first, *outside, *dq, *dk, *dv, *dpk, *dpq)

    rest_send, d_first = tied(rest_send, d_first)
    edge = shape((span, width), bf16)
    loaded = (d_first, w_query, w_key, w_value)
    own, *edges = pl.pallas_call(
        input_grad_kernel,
        out_shape=(shape((tokens, width), f32),) + (edge,) * (1 if n_seq == 2 else 2),
        compiler_params=pltpu.CompilerParams(vmem_limit_bytes=12 * MiB),
        cost_estimate=pl.CostEstimate(flops=1000, bytes_accessed=1000, transcendentals=0),
        name="input_grad",
    )(*dq, *dk, *dv, *(pltpu.with_memory_space_constraint(a, pltpu.HBM) for a in loaded))
    rest_keep, own = tied(rest_keep, own)
    rest = rest_keep + exchange(rest_send, "rows", 1)
    rest, mid = tied(rest, mid)
    rest_one, rest_two = opened(rest)
    rest_one, rest_two, edges = lax.optimization_barrier((rest_one, rest_two, edges))
    nothing = jnp.zeros((block - span, width), f32)
    if n_seq == 2:
        arrived = exchange(edges[0], "seq", 1).astype(f32)
        own = own + jnp.where(
            me_seq == 0,
            jnp.concatenate([nothing, arrived], axis=0),
            jnp.concatenate([arrived, nothing], axis=0),
        )
    else:
        from_next = lax.ppermute(edges[0], "seq", backward).astype(f32)
        from_prev = lax.ppermute(edges[1], "seq", forward).astype(f32)
        own = (
            own
            + jnp.concatenate([nothing, from_next], axis=0)
            + jnp.concatenate([from_prev, nothing], axis=0)
        )
    grad_hidden = own.astype(bf16)

    rest = finished(rest_one, rest_two)
    for step in range(2, row_bits):
        mid = row_step(mid, step)
    for step in range(seq_bits - 1):
        mid = seq_step(mid, step)
    mid = (mid, exchange(mid, "seq", 1 << (seq_bits - 1)))

    square = shape((share, width), f32)
    grads = pl.pallas_call(
        partial(final_kernel, width=width, units=units, count=table),
        out_shape=(
            square,
            square,
            square,
            square,
            shape((share, table), f32),
            square,
            square,
            shape((4, share), f32),
            shape((2, share), f32),
            shape((2, share), f32),
            shape((share, units), f32),
            shape((share, units), f32),
            shape((1, share), f32),
            shape((units // TILE, TILE), f32),
        ),
        compiler_params=pltpu.CompilerParams(vmem_limit_bytes=12 * MiB),
        name="final",
    )(*mid, *rest)
    return (
        result.reshape(count, block, width),
        grad_hidden.reshape(count, block, width),
        *grads[:4],
        grads[4].T,
        *grads[5:11],
        grads[13].reshape(units),
        grads[11].T,
        grads[12].reshape(share),
    )


def solution(mesh):
    in_specs = (
        P("rows", "seq", None),
        P("rows", "seq", None),
        P("rows", "seq"),
    ) + (P(),) * 14
    out_specs = (
        P("rows", "seq", None),
        P("rows", "seq", None),
        P("rows", None),
        P("rows", None),
        P("rows", None),
        P("rows", None),
        P(None, "rows"),
        P("rows", None),
        P("rows", None),
        P(None, "rows"),
        P(None, "rows"),
        P(None, "rows"),
        P("rows", None),
        P(),
        P(None, "rows"),
        P("rows"),
    )
    return jax.shard_map(local, mesh=mesh, in_specs=in_specs, out_specs=out_specs, check_vma=False)
```

profile of v0, /device:TPU:0, one launch (start us, length us, event | category | flops | bytes accessed | tf_op | source)
XLA Modules:
  0.0 83.3 jit_solution(2252483668091941840)
XLA Ops:
  0.7 1.0 %dynamic-slice_bitcast_fusion = bf16[256,384]{1,0:T(8,128)(2,1)S(1)} fusion(bf16[1,512,384]{2,1,0:T(8,128)(2,1)} %param.18, s32[]{:T(128)S(6)} %select_n.11), kind=kLoop, calls=%fused_computation.6 | loop fusion | bytes 393220 | tf_op jit(solution)/shard_map/dynamic_slice | solution.py:669
  1.6 3.0 %collective-permute-start = (bf16[256,384]{1,0:T(8,128)(2,1)S(1)}, bf16[256,384]{1,0:T(8,128)(2,1)S(1)}, u32[]{:S(2)}, u32[]{:S(2)}) collective-permute-start(bf16[256,384]{1,0:T(8,128)(2,1)S(1)} %dynamic-slice_bitcast_fusion), channel_id=1, source_target_pairs={{0,16},{16,0},{1,17},{17,1},{2,18},{18,2},{3,19},{19,3},{4,20},{20... | collective-permute-start | bytes 589832 | tf_op jit(solution)/shard_map/ppermute | solution.py:73
  4.7 4.5 %project.1 = (bf16[3,512,128]{2,1,0:T(8,128)(2,1)S(1)}, bf16[3,512,128]{2,1,0:T(8,128)(2,1)S(1)}, bf16[3,512,128]{2,1,0:T(8,128)(2,1)S(1)}, bf16[3,512,128]{2,1,...) custom-call(s32[384,4]{1,0:T(8,128)} %constant.19.clone.refs_0_, ...), custom_call_target="tpu_custom_call" | custom-call | tf_op jit(solution)/shard_map/project/pallas_call | solution.py:691
  9.6 8.7 %attend.1 = (bf16[512,384]{1,0:T(8,128)(2,1)S(1)}, bf16[3,2,4,128,640]{4,3,2,1,0:T(8,128)(2,1)S(1)}, bf16[3,1024,128]{2,1,0:T(8,128)(2,1)S(1)}, bf16[3,1024,128]{2,1,0:T(8,128)(2,1)S(1)}) custom-call(bf16[3,512,128]{2,1,0:T(8,128)(2,1)S(1)} %get-tuple-element.83.q, bf16[3,512,128]{2,1,0:T(8,128)(2,1)S(1)} %get-tuple-element.84.k_own, ...), custom_call_target="tpu_custom_call" | custom-call | tf_op jit(solution)/shard_map/attend/pallas_call | solution.py:713
  18.4 8.0 %middle.1 = (bf16[512,384]{1,0:T(8,128)(2,1)}, f32[512,384]{1,0:T(8,128)S(1)}, bf16[512,384]{1,0:T(8,128)(2,1)S(1)}, bf16[192,3200]{1,0:T(8,128)(2,1)S(1)}, bf16...) custom-call(bf16[512,384]{1,0:T(8,128)(2,1)S(1)} %bitcast.12, bf16[512,384]{1,0:T(8,128)(2,1)S(1)} %get-tuple-element.88.context, ...), custom_call_target="tpu_custom_call" | custom-call | tf_op jit(solution)/shard_map/middle/pallas_call | solution.py:730
  26.6 3.9 %attend_back.3 = (bf16[512,128]{1,0:T(8,128)(2,1)S(1)}, bf16[1024,128]{1,0:T(8,128)(2,1)S(1)}, bf16[1024,128]{1,0:T(8,128)(2,1)S(1)}, bf16[128,512]{1,0:T(8,128)(2,1)S(1)}, bf16[128,512]{1,0:T(8,128)(2,1)S(1)}) custom-call(bf16[3,512,128]{2,1,0:T(8,128)(2,1)S(1)} %get-tuple-element.83.q, bf16[3,1024,128]{2,1,0:T(8,128)(2,1)S(1)} %get-tuple-element.98.k, ...), custom_call_target="tpu_custom_call" | custom-call | flops 1000 | bytes 1000 | tf_op jit(solution)/shard_map/attend_back/pallas_call | solution.py:766
  30.8 1.8 %collective-permute-start.3 = (bf16[96,3200]{1,0:T(8,128)(2,1)S(1)}, bf16[96,3200]{1,0:T(8,128)(2,1)S(1)}, u32[]{:S(2)}, u32[]{:S(2)}) collective-permute-start(bf16[96,3200]{1,0:T(8,128)(2,1)S(1)} %slice.64), channel_id=1, source_target_pairs={{0,2},{1,3},{2,0},{3,1},{4,6},{5,7},{6,4},{7,5},{8,10},{9,11},{10,... | collective-permute-start | bytes 1843208 | tf_op jit(solution)/shard_map/ppermute | solution.py:73
  32.6 4.1 %attend_back.5 = (bf16[512,128]{1,0:T(8,128)(2,1)S(1)}, bf16[1024,128]{1,0:T(8,128)(2,1)S(1)}, bf16[1024,128]{1,0:T(8,128)(2,1)S(1)}, bf16[128,512]{1,0:T(8,128)(2,1)S(1)}, bf16[128,512]{1,0:T(8,128)(2,1)S(1)}) custom-call(bf16[3,512,128]{2,1,0:T(8,128)(2,1)S(1)} %get-tuple-element.83.q, bf16[3,1024,128]{2,1,0:T(8,128)(2,1)S(1)} %get-tuple-element.98.k, ...), custom_call_target="tpu_custom_call" | custom-call | flops 1000 | bytes 1000 | tf_op jit(solution)/shard_map/attend_back/pallas_call | solution.py:766
  36.7 3.9 %attend_back.4 = (bf16[512,128]{1,0:T(8,128)(2,1)S(1)}, bf16[1024,128]{1,0:T(8,128)(2,1)S(1)}, bf16[1024,128]{1,0:T(8,128)(2,1)S(1)}, bf16[128,512]{1,0:T(8,128)(2,1)S(1)}, bf16[128,512]{1,0:T(8,128)(2,1)S(1)}) custom-call(bf16[3,512,128]{2,1,0:T(8,128)(2,1)S(1)} %get-tuple-element.83.q, bf16[3,1024,128]{2,1,0:T(8,128)(2,1)S(1)} %get-tuple-element.98.k, ...), custom_call_target="tpu_custom_call" | custom-call | flops 1000 | bytes 1000 | tf_op jit(solution)/shard_map/attend_back/pallas_call | solution.py:766
  40.6 3.3 %weight_grad.1 = (bf16[192,2944]{1,0:T(8,128)(2,1)S(1)}, bf16[192,2944]{1,0:T(8,128)(2,1)S(1)}) custom-call(bf16[384,512]{1,0:T(8,128)(2,1)S(1)} %get-tuple-element.91.x_t, bf16[384,512]{1,0:T(8,128)(2,1)S(1)} %get-tuple-element.92.rel_t, bf16[384,384]{1,0:T(8,128)(2,1)S(1)} %get-tuple-element.93.w_pk_t, bf16[384,384]{1,0:T(8,128)(2,1)S(1)} %get-tuple-element.94.w_pq_t, ...), custom_call_target="tpu_custom_call" | custom-call | flops 1000 | bytes 1000 | tf_op jit(solution)/shard_map/weight_grad/pallas_call | solution.py:838
  44.1 2.5 %input_grad.1 = (f32[512,384]{1,0:T(8,128)S(1)}, bf16[256,384]{1,0:T(8,128)(2,1)S(1)}) custom-call(bf16[512,128]{1,0:T(8,128)(2,1)S(1)} %get-tuple-element.104.refs_1_.dq0, bf16[512,128]{1,0:T(8,128)(2,1)S(1)} %get-tuple-element.108.refs_2_.dq1, bf16[512,128]{1,0:T(8,128)(2,1)S(1)} %get-tuple-element.109.refs_3_.dq2, ...), custom_call_target="tpu_custom_call" | custom-call | flops 1000 | bytes 1000 | tf_op jit(solution)/shard_map/input_grad/pallas_call | solution.py:852
  46.6 0.5 collective-permute-done.3
  47.5 1.8 %collective-permute-start.4 = (bf16[96,1408]{1,0:T(8,128)(2,1)S(1)}, bf16[96,1408]{1,0:T(8,128)(2,1)S(1)}, u32[]{:S(2)}, u32[]{:S(2)}) collective-permute-start(bf16[96,1408]{1,0:T(8,128)(2,1)S(1)} %slice.66), channel_id=1, source_target_pairs={{0,2},{1,3},{2,0},{3,1},{4,6},{5,7},{6,4},{7,5},{8,10},{9,11},{10,... | collective-permute-start | bytes 811016 | tf_op jit(solution)/shard_map/ppermute | solution.py:73
  49.3 1.6 %collective-permute-start.5 = (bf16[192,768]{1,0:T(8,128)(2,1)S(1)}, bf16[192,768]{1,0:T(8,128)(2,1)S(1)}, u32[]{:S(2)}, u32[]{:S(2)}) collective-permute-start(bf16[192,768]{1,0:T(8,128)(2,1)S(1)} %slice.68), channel_id=1, source_target_pairs={{0,16},{16,0},{1,17},{17,1},{2,18},{18,2},{3,19},{19,3},{4,20},{20... | collective-permute-start | bytes 884744 | tf_op jit(solution)/shard_map/ppermute | solution.py:73
  50.9 1.6 %collective-permute-start.7 = (bf16[48,3200]{1,0:T(8,128)(2,1)S(1)}, bf16[48,3200]{1,0:T(8,128)(2,1)S(1)}, u32[]{:S(2)}, u32[]{:S(2)}) collective-permute-start(bf16[48,3200]{1,0:T(8,128)(2,1)S(1)} %slice.70), channel_id=1, source_target_pairs={{0,4},{1,5},{2,6},{3,7},{4,0},{5,1},{6,2},{7,3},{8,12},{9,13},{10,... | collective-permute-start | bytes 921608 | tf_op jit(solution)/shard_map/ppermute | solution.py:73
  52.6 3.2 %collective-permute-done.4 = bf16[96,1408]{1,0:T(8,128)(2,1)S(1)} collective-permute-done((bf16[96,1408]{1,0:T(8,128)(2,1)S(1)}, bf16[96,1408]{1,0:T(8,128)(2,1)S(1)}, u32[]{:S(2)}, u32[]{:S(2)}) %collective-permute-start.4) | collective-permute-done | bytes 270368 | tf_op jit(solution)/shard_map/ppermute | solution.py:73
  55.8 1.9 %collective-permute-done.5 = bf16[192,768]{1,0:T(8,128)(2,1)S(1)} collective-permute-done((bf16[192,768]{1,0:T(8,128)(2,1)S(1)}, bf16[192,768]{1,0:T(8,128)(2,1)S(1)}, u32[]{:S(2)}, u32[]{:S(2)}) %collective-permute-start.5) | collective-permute-done | bytes 294944 | tf_op jit(solution)/shard_map/ppermute | solution.py:73
  57.8 1.6 %collective-permute-start.10 = (bf16[48,1408]{1,0:T(8,128)(2,1)S(1)}, bf16[48,1408]{1,0:T(8,128)(2,1)S(1)}, u32[]{:S(2)}, u32[]{:S(2)}) collective-permute-start(bf16[48,1408]{1,0:T(8,128)(2,1)S(1)} %slice.74), channel_id=1, source_target_pairs={{0,4},{1,5},{2,6},{3,7},{4,0},{5,1},{6,2},{7,3},{8,12},{9,13},{10,... | collective-permute-start | bytes 405512 | tf_op jit(solution)/shard_map/ppermute | solution.py:73
  59.4 0.6 collective-permute-start.13
  60.0 1.6 %collective-permute-start.6 = (bf16[256,384]{1,0:T(8,128)(2,1)S(1)}, bf16[256,384]{1,0:T(8,128)(2,1)S(1)}, u32[]{:S(2)}, u32[]{:S(2)}) collective-permute-start(bf16[256,384]{1,0:T(8,128)(2,1)S(1)} %get-tuple-element.132), channel_id=1, source_target_pairs={{0,16},{16,0},{1,17},{17,1},{2,18},{18,2},{3,19},{19,3},{4,20},{20... | collective-permute-start | bytes 589832 | tf_op jit(solution)/shard_map/ppermute | solution.py:73
  61.6 2.6 %collective-permute-start.8 = (bf16[24,3200]{1,0:T(8,128)(2,1)S(1)}, bf16[24,3200]{1,0:T(8,128)(2,1)S(1)}, u32[]{:S(2)}, u32[]{:S(2)}) collective-permute-start(bf16[24,3200]{1,0:T(8,128)(2,1)S(1)} %slice.84), channel_id=1, source_target_pairs={{0,8},{1,9},{2,10},{3,11},{4,12},{5,13},{6,14},{7,15},{8,0},{9,1},... | collective-permute-start | bytes 460808 | tf_op jit(solution)/shard_map/ppermute | solution.py:73
  64.3 2.8 %collective-permute-start.11 = (bf16[24,1408]{1,0:T(8,128)(2,1)S(1)}, bf16[24,1408]{1,0:T(8,128)(2,1)S(1)}, u32[]{:S(2)}, u32[]{:S(2)}) collective-permute-start(bf16[24,1408]{1,0:T(8,128)(2,1)S(1)} %slice.86), channel_id=1, source_target_pairs={{0,8},{1,9},{2,10},{3,11},{4,12},{5,13},{6,14},{7,15},{8,0},{9,1},... | collective-permute-start | bytes 202760 | tf_op jit(solution)/shard_map/ppermute | solution.py:73
  67.1 1.6 %collective-permute-start.14 = (bf16[48,768]{1,0:T(8,128)(2,1)S(1)}, bf16[48,768]{1,0:T(8,128)(2,1)S(1)}, u32[]{:S(2)}, u32[]{:S(2)}) collective-permute-start(bf16[48,768]{1,0:T(8,128)(2,1)S(1)} %slice.88), channel_id=1, source_target_pairs={{0,4},{1,5},{2,6},{3,7},{4,0},{5,1},{6,2},{7,3},{8,12},{9,13},{10,... | collective-permute-start | bytes 221192 | tf_op jit(solution)/shard_map/ppermute | solution.py:73
  68.7 3.0 %collective-permute-done.8 = bf16[24,3200]{1,0:T(8,128)(2,1)S(1)} collective-permute-done((bf16[24,3200]{1,0:T(8,128)(2,1)S(1)}, bf16[24,3200]{1,0:T(8,128)(2,1)S(1)}, u32[]{:S(2)}, u32[]{:S(2)}) %collective-permute-start.8) | collective-permute-done | bytes 153632 | tf_op jit(solution)/shard_map/ppermute | solution.py:73
  71.7 0.5 collective-permute-start.9
  72.2 1.2 %collective-permute-done.14 = bf16[48,768]{1,0:T(8,128)(2,1)S(1)} collective-permute-done((bf16[48,768]{1,0:T(8,128)(2,1)S(1)}, bf16[48,768]{1,0:T(8,128)(2,1)S(1)}, u32[]{:S(2)}, u32[]{:S(2)}) %collective-permute-start.14) | collective-permute-done | bytes 73760 | tf_op jit(solution)/shard_map/ppermute | solution.py:73
  73.6 0.6 collective-permute-start.12
  74.2 4.2 %collective-permute-done.15 = bf16[24,768]{1,0:T(8,128)(2,1)S(1)} collective-permute-done((bf16[24,768]{1,0:T(8,128)(2,1)S(1)}, bf16[24,768]{1,0:T(8,128)(2,1)S(1)}, u32[]{:S(2)}, u32[]{:S(2)}) %collective-permute-start.15) | collective-permute-done | bytes 36896 | tf_op jit(solution)/shard_map/ppermute | solution.py:73
  78.4 0.8 %collective-permute-start.16 = (bf16[24,768]{1,0:T(8,128)(2,1)S(1)}, bf16[24,768]{1,0:T(8,128)(2,1)S(1)}, u32[]{:S(2)}, u32[]{:S(2)}) collective-permute-start(bf16[24,768]{1,0:T(8,128)(2,1)S(1)} %slice_add_fusion.9.refs_4_), channel_id=1, source_target_pairs={{0,16},{16,0},{1,17},{17,1},{2,18},{18,2},{3,19},{19,3},{4,20},{20... | collective-permute-start | bytes 110600 | tf_op jit(solution)/shard_map/ppermute | solution.py:73
  79.3 0.8 fusion
  80.1 2.3 %collective-permute-done.16.refs_5_ = bf16[24,768]{1,0:T(8,128)(2,1)S(1)} collective-permute-done((bf16[24,768]{1,0:T(8,128)(2,1)S(1)}, bf16[24,768]{1,0:T(8,128)(2,1)S(1)}, u32[]{:S(2)}, u32[]{:S(2)}) %collective-permute-start.16) | collective-permute-done | bytes 36896 | tf_op jit(solution)/shard_map/ppermute | solution.py:73
  82.4 0.8 %final.1 = (f32[24,384]{1,0:T(8,128)}, f32[24,384]{1,0:T(8,128)}, f32[24,384]{1,0:T(8,128)}, f32[24,384]{1,0:T(8,128)}, f32[24,512]{1,0:T(8,128)}, /*index=5*/f3...) custom-call(bf16[24,3200]{1,0:T(8,128)(2,1)S(1)} %slice_add_fusion.4, ...), custom_call_target="tpu_custom_call" | custom-call | tf_op jit(solution)/shard_map/final/pallas_call | solution.py:890
  (64 shorter events, 1.9 us)
Async XLA Ops:
  1.6 7.9 %collective-permute-start = (bf16[256,384]{1,0:T(8,128)(2,1)S(1)}, bf16[256,384]{1,0:T(8,128)(2,1)S(1)}, u32[]{:S(2)}, u32[]{:S(2)}) collective-permute-start(bf16[256,384]{1,0:T(8,128)(2,1)S(1)} %dynamic-slice_bitcast_fusion), channel_id=1, source_target_pairs={{0,16},{16,0},{1,17},{17,1},{2,18},{18,2},{3,19},{19,3},{4,20},{20... | collective-permute-start | bytes 589832 | tf_op jit(solution)/shard_map/ppermute | solution.py:73
  4.6 4.9 %copy-start.1 = (bf16[384,384]{1,0:T(8,128)(2,1)S(1)}, bf16[384,384]{1,0:T(8,128)(2,1)}, u32[]{:S(2)}) copy-start(bf16[384,384]{1,0:T(8,128)(2,1)} %w_key.3) | copy-start | bytes 884740
  4.6 4.9 %copy-start.2 = (bf16[384,384]{1,0:T(8,128)(2,1)S(1)}, bf16[384,384]{1,0:T(8,128)(2,1)}, u32[]{:S(2)}) copy-start(bf16[384,384]{1,0:T(8,128)(2,1)} %w_value.3) | copy-start | bytes 884740
  4.6 4.9 %copy-start.8 = (bf16[4,384]{1,0:T(4,128)(2,1)S(1)}, bf16[4,384]{1,0:T(4,128)(2,1)}, u32[]{:S(2)}) copy-start(bf16[4,384]{1,0:T(4,128)(2,1)} %biases.3) | copy-start | bytes 9220
  4.6 13.7 %copy-start.6 = (bf16[1,512,384]{2,1,0:T(8,128)(2,1)S(1)}, bf16[1,512,384]{2,1,0:T(8,128)(2,1)}, u32[]{:S(2)}) copy-start(bf16[1,512,384]{2,1,0:T(8,128)(2,1)} %param.19) | copy-start | bytes 1179652
  4.6 13.7 %copy-start.7 = (bf16[384,384]{1,0:T(8,128)(2,1)S(1)}, bf16[384,384]{1,0:T(8,128)(2,1)}, u32[]{:S(2)}) copy-start(bf16[384,384]{1,0:T(8,128)(2,1)} %w_output.1) | copy-start | bytes 884740
  4.7 13.7 %copy-start.12 = (bf16[2,384]{1,0:T(2,128)(2,1)S(1)}, bf16[2,384]{1,0:T(2,128)(2,1)}, u32[]{:S(2)}) copy-start(bf16[2,384]{1,0:T(2,128)(2,1)} %shifts.1) | copy-start | bytes 4612
  9.6 8.8 %copy-start.3 = (bf16[1,512,384]{2,1,0:T(8,128)(2,1)S(1)}, bf16[1,512,384]{2,1,0:T(8,128)(2,1)}, u32[]{:S(2)}) copy-start(bf16[1,512,384]{2,1,0:T(8,128)(2,1)} %param.18) | copy-start | bytes 1179652
  9.6 8.8 %copy-start.4 = (bf16[384,1536]{1,0:T(8,128)(2,1)S(1)}, bf16[384,1536]{1,0:T(8,128)(2,1)}, u32[]{:S(2)}) copy-start(bf16[384,1536]{1,0:T(8,128)(2,1)} %w_inner.1) | copy-start | bytes 3538948
  9.6 8.8 %copy-start.5 = (bf16[1536,384]{1,0:T(8,128)(2,1)S(1)}, bf16[1536,384]{1,0:T(8,128)(2,1)}, u32[]{:S(2)}) copy-start(bf16[1536,384]{1,0:T(8,128)(2,1)} %w_outer.1) | copy-start | bytes 3538948
  9.6 8.8 %copy-start.9 = (bf16[1536]{0:T(1024)(128)(2,1)S(1)}, bf16[1536]{0:T(1024)(128)(2,1)}, u32[]{:S(2)}) copy-start(bf16[1536]{0:T(1024)(128)(2,1)} %inner_bias.1) | copy-start | bytes 9220
  9.6 8.8 %copy-start.10 = (s32[1,512]{1,0:T(1,128)S(1)}, s32[1,512]{1,0:T(1,128)}, u32[]{:S(2)}) copy-start(s32[1,512]{1,0:T(1,128)} %mask.1) | copy-start | bytes 6148
  9.6 8.8 %copy-start.11 = (bf16[2,384]{1,0:T(2,128)(2,1)S(1)}, bf16[2,384]{1,0:T(2,128)(2,1)}, u32[]{:S(2)}) copy-start(bf16[2,384]{1,0:T(2,128)(2,1)} %gains.1) | copy-start | bytes 4612
  9.6 8.8 %copy-start.13 = (bf16[384]{0:T(512)(128)(2,1)S(1)}, bf16[384]{0:T(512)(128)(2,1)}, u32[]{:S(2)}) copy-start(bf16[384]{0:T(512)(128)(2,1)} %outer_bias.1) | copy-start | bytes 2308
  26.5 14.1 %copy-start = (f32[512,384]{1,0:T(8,128)}, f32[512,384]{1,0:T(8,128)S(1)}, u32[]{:S(2)}) copy-start(f32[512,384]{1,0:T(8,128)S(1)} %get-tuple-element.124.d_first) | copy-start | bytes 2359300
  26.5 3.9 %collective-permute-start.1 = (bf16[192,3200]{1,0:T(8,128)(2,1)S(1)}, bf16[192,3200]{1,0:T(8,128)(2,1)S(1)}, u32[]{:S(2)}, u32[]{:S(2)}) collective-permute-start(bf16[192,3200]{1,0:T(8,128)(2,1)S(1)} %get-tuple-element.106), channel_id=1, source_target_pairs={{0,1},{1,0},{2,3},{3,2},{4,5},{5,4},{6,7},{7,6},{8,9},{9,8},{10,11... | collective-permute-start | bytes 3686408 | tf_op jit(solution)/shard_map/ppermute | solution.py:73
  30.8 16.3 %collective-permute-start.3 = (bf16[96,3200]{1,0:T(8,128)(2,1)S(1)}, bf16[96,3200]{1,0:T(8,128)(2,1)S(1)}, u32[]{:S(2)}, u32[]{:S(2)}) collective-permute-start(bf16[96,3200]{1,0:T(8,128)(2,1)S(1)} %slice.64), channel_id=1, source_target_pairs={{0,2},{1,3},{2,0},{3,1},{4,6},{5,7},{6,4},{7,5},{8,10},{9,11},{10,... | collective-permute-start | bytes 1843208 | tf_op jit(solution)/shard_map/ppermute | solution.py:73
  43.8 3.4 %collective-permute-start.2 = (bf16[192,2944]{1,0:T(8,128)(2,1)S(1)}, bf16[192,2944]{1,0:T(8,128)(2,1)S(1)}, u32[]{:S(2)}, u32[]{:S(2)}) collective-permute-start(bf16[192,2944]{1,0:T(8,128)(2,1)S(1)} %get-tuple-element.128), channel_id=1, source_target_pairs={{0,1},{1,0},{2,3},{3,2},{4,5},{5,4},{6,7},{7,6},{8,9},{9,8},{10,11... | collective-permute-start | bytes 3391496 | tf_op jit(solution)/shard_map/ppermute | solution.py:73
  47.5 8.3 %collective-permute-start.4 = (bf16[96,1408]{1,0:T(8,128)(2,1)S(1)}, bf16[96,1408]{1,0:T(8,128)(2,1)S(1)}, u32[]{:S(2)}, u32[]{:S(2)}) collective-permute-start(bf16[96,1408]{1,0:T(8,128)(2,1)S(1)} %slice.66), channel_id=1, source_target_pairs={{0,2},{1,3},{2,0},{3,1},{4,6},{5,7},{6,4},{7,5},{8,10},{9,11},{10,... | collective-permute-start | bytes 811016 | tf_op jit(solution)/shard_map/ppermute | solution.py:73
  49.3 8.4 %collective-permute-start.5 = (bf16[192,768]{1,0:T(8,128)(2,1)S(1)}, bf16[192,768]{1,0:T(8,128)(2,1)S(1)}, u32[]{:S(2)}, u32[]{:S(2)}) collective-permute-start(bf16[192,768]{1,0:T(8,128)(2,1)S(1)} %slice.68), channel_id=1, source_target_pairs={{0,16},{16,0},{1,17},{17,1},{2,18},{18,2},{3,19},{19,3},{4,20},{20... | collective-permute-start | bytes 884744 | tf_op jit(solution)/shard_map/ppermute | solution.py:73
  50.9 10.6 %collective-permute-start.7 = (bf16[48,3200]{1,0:T(8,128)(2,1)S(1)}, bf16[48,3200]{1,0:T(8,128)(2,1)S(1)}, u32[]{:S(2)}, u32[]{:S(2)}) collective-permute-start(bf16[48,3200]{1,0:T(8,128)(2,1)S(1)} %slice.70), channel_id=1, source_target_pairs={{0,4},{1,5},{2,6},{3,7},{4,0},{5,1},{6,2},{7,3},{8,12},{9,13},{10,... | collective-permute-start | bytes 921608 | tf_op jit(solution)/shard_map/ppermute | solution.py:73
  57.8 6.5 %collective-permute-start.10 = (bf16[48,1408]{1,0:T(8,128)(2,1)S(1)}, bf16[48,1408]{1,0:T(8,128)(2,1)S(1)}, u32[]{:S(2)}, u32[]{:S(2)}) collective-permute-start(bf16[48,1408]{1,0:T(8,128)(2,1)S(1)} %slice.74), channel_id=1, source_target_pairs={{0,4},{1,5},{2,6},{3,7},{4,0},{5,1},{6,2},{7,3},{8,12},{9,13},{10,... | collective-permute-start | bytes 405512 | tf_op jit(solution)/shard_map/ppermute | solution.py:73
  59.4 7.6 %collective-permute-start.13 = (bf16[96,768]{1,0:T(8,128)(2,1)S(1)}, bf16[96,768]{1,0:T(8,128)(2,1)S(1)}, u32[]{:S(2)}, u32[]{:S(2)}) collective-permute-start(bf16[96,768]{1,0:T(8,128)(2,1)S(1)} %slice.78), channel_id=1, source_target_pairs={{0,2},{1,3},{2,0},{3,1},{4,6},{5,7},{6,4},{7,5},{8,10},{9,11},{10,... | collective-permute-start | bytes 442376 | tf_op jit(solution)/shard_map/ppermute | solution.py:73
  60.0 12.2 %collective-permute-start.6 = (bf16[256,384]{1,0:T(8,128)(2,1)S(1)}, bf16[256,384]{1,0:T(8,128)(2,1)S(1)}, u32[]{:S(2)}, u32[]{:S(2)}) collective-permute-start(bf16[256,384]{1,0:T(8,128)(2,1)S(1)} %get-tuple-element.132), channel_id=1, source_target_pairs={{0,16},{16,0},{1,17},{17,1},{2,18},{18,2},{3,19},{19,3},{4,20},{20... | collective-permute-start | bytes 589832 | tf_op jit(solution)/shard_map/ppermute | solution.py:73
  61.6 10.0 %collective-permute-start.8 = (bf16[24,3200]{1,0:T(8,128)(2,1)S(1)}, bf16[24,3200]{1,0:T(8,128)(2,1)S(1)}, u32[]{:S(2)}, u32[]{:S(2)}) collective-permute-start(bf16[24,3200]{1,0:T(8,128)(2,1)S(1)} %slice.84), channel_id=1, source_target_pairs={{0,8},{1,9},{2,10},{3,11},{4,12},{5,13},{6,14},{7,15},{8,0},{9,1},... | collective-permute-start | bytes 460808 | tf_op jit(solution)/shard_map/ppermute | solution.py:73
  64.3 9.3 %collective-permute-start.11 = (bf16[24,1408]{1,0:T(8,128)(2,1)S(1)}, bf16[24,1408]{1,0:T(8,128)(2,1)S(1)}, u32[]{:S(2)}, u32[]{:S(2)}) collective-permute-start(bf16[24,1408]{1,0:T(8,128)(2,1)S(1)} %slice.86), channel_id=1, source_target_pairs={{0,8},{1,9},{2,10},{3,11},{4,12},{5,13},{6,14},{7,15},{8,0},{9,1},... | collective-permute-start | bytes 202760 | tf_op jit(solution)/shard_map/ppermute | solution.py:73
  67.1 6.3 %collective-permute-start.14 = (bf16[48,768]{1,0:T(8,128)(2,1)S(1)}, bf16[48,768]{1,0:T(8,128)(2,1)S(1)}, u32[]{:S(2)}, u32[]{:S(2)}) collective-permute-start(bf16[48,768]{1,0:T(8,128)(2,1)S(1)} %slice.88), channel_id=1, source_target_pairs={{0,4},{1,5},{2,6},{3,7},{4,0},{5,1},{6,2},{7,3},{8,12},{9,13},{10,... | collective-permute-start | bytes 221192 | tf_op jit(solution)/shard_map/ppermute | solution.py:73
  71.7 10.7 %collective-permute-start.9 = (bf16[24,3200]{1,0:T(8,128)(2,1)S(1)}, bf16[24,3200]{1,0:T(8,128)(2,1)S(1)}, u32[]{:S(2)}, u32[]{:S(2)}) collective-permute-start(bf16[24,3200]{1,0:T(8,128)(2,1)S(1)} %slice_add_fusion.4.refs_0_), channel_id=1, source_target_pairs={{0,16},{16,0},{1,17},{17,1},{2,18},{18,2},{3,19},{19,3},{4,20},{20... | collective-permute-start | bytes 460808 | tf_op jit(solution)/shard_map/ppermute | solution.py:73
  73.5 4.9 %collective-permute-start.15 = (bf16[24,768]{1,0:T(8,128)(2,1)S(1)}, bf16[24,768]{1,0:T(8,128)(2,1)S(1)}, u32[]{:S(2)}, u32[]{:S(2)}) collective-permute-start(bf16[24,768]{1,0:T(8,128)(2,1)S(1)} %slice.90), channel_id=1, source_target_pairs={{0,8},{1,9},{2,10},{3,11},{4,12},{5,13},{6,14},{7,15},{8,0},{9,1},... | collective-permute-start | bytes 110600 | tf_op jit(solution)/shard_map/ppermute | solution.py:73
  73.6 6.5 %collective-permute-start.12 = (bf16[24,1408]{1,0:T(8,128)(2,1)S(1)}, bf16[24,1408]{1,0:T(8,128)(2,1)S(1)}, u32[]{:S(2)}, u32[]{:S(2)}) collective-permute-start(bf16[24,1408]{1,0:T(8,128)(2,1)S(1)} %slice_add_fusion.8.refs_2_), channel_id=1, source_target_pairs={{0,16},{16,0},{1,17},{17,1},{2,18},{18,2},{3,19},{19,3},{4,20},{20... | collective-permute-start | bytes 202760 | tf_op jit(solution)/shard_map/ppermute | solution.py:73
  78.4 4.0 %collective-permute-start.16 = (bf16[24,768]{1,0:T(8,128)(2,1)S(1)}, bf16[24,768]{1,0:T(8,128)(2,1)S(1)}, u32[]{:S(2)}, u32[]{:S(2)}) collective-permute-start(bf16[24,768]{1,0:T(8,128)(2,1)S(1)} %slice_add_fusion.9.refs_4_), channel_id=1, source_target_pairs={{0,16},{16,0},{1,17},{17,1},{2,18},{18,2},{3,19},{19,3},{4,20},{20... | collective-permute-start | bytes 110600 | tf_op jit(solution)/shard_map/ppermute | solution.py:73
where the time goes:
time: 83.5 us; the launch traced here: 83.3 us
  Pallas kernels  39.7 us (48%)
  starting transfers between devices  23 us (28%)
  waiting for transfers between devices  16.7 us (20%)
  other arithmetic  1.68 us (2%)
  local copies, waits for them, and re-layouts  1.19 us (1%)
  between operations  1.16 us (1%)
    ppermute x17, starting transfers between devices, exchange(): return lax.ppermute(value, axis, [(i, i ^ bit) for i in range(count)])  23 us
    ppermute x17, waiting for transfers between devices, exchange(): return lax.ppermute(value, axis, [(i, i ^ bit) for i in range(count)])  16.7 us
    pallas_call x3, Pallas kernels, back(): pl.pallas_call(partial(attend_back_kernel, scale=scale, p=p), out_shape=(...  11.8 us
    pallas_call x1, Pallas kernels, local(): pl.pallas_call(partial(attend_kernel, scale=scale, n_seq=n_seq), out_shap...  8.68 us
    pallas_call x1, Pallas kernels, local(): pl.pallas_call(partial(middle_kernel, step=512, share=share), out_shape=(...  8.04 us
    pallas_call x1, Pallas kernels, local(): pl.pallas_call(project_kernel, out_shape=(shape((PAIRS, block, TILE), bf1...  4.52 us
    pallas_call x1, Pallas kernels, local(): pl.pallas_call(partial(weight_grad_kernel, n_seq=n_seq), out_shape=(shape...  3.26 us
    pallas_call x1, Pallas kernels, local(): pl.pallas_call(input_grad_kernel, out_shape=(shape((tokens, width), f32),...  2.53 us
  transfers between devices with their start and end apart: 17, of which 8 were waited for; matrix products, arithmetic and copies ran while one was open for 1% of the time, Pallas kernels for 27%

commit v1 on v0

--- a/solution.py
+++ b/solution.py
@@ -589,23 +589,21 @@
 
 def final_kernel(*refs, width, units, count):
     (g_q, g_k, g_v, g_o, g_rel, g_pk, g_pq, g_bias, g_gain, g_shift, g_in, g_out, g_ob, g_ib) = (
-        refs[6:]
+        refs[4:]
     )
     low = lax.axis_index("seq") % 2 == 0
 
-    def joined(one, one_other, two, two_other):
-        mine, other = two[...].astype(f32), two_other[...].astype(f32)
-        return jnp.concatenate(
-            [
-                one[...].astype(f32) + one_other[...].astype(f32),
-                jnp.where(low, mine, other),
-                jnp.where(low, other, mine),
-            ],
-            axis=1,
-        )
-
     mid = refs[0][...].astype(f32) + refs[1][...].astype(f32)
-    rest = joined(*refs[2:6])
+    cut, _ = column_cut(6 * width + count + TILE)
+    mine, other = refs[2][...].astype(f32), refs[3][...].astype(f32)
+    rest = jnp.concatenate(
+        [
+            mine[:, :cut] + other[:, :cut],
+            jnp.where(low, mine[:, cut:], other[:, cut:]),
+            jnp.where(low, other[:, cut:], mine[:, cut:]),
+        ],
+        axis=1,
+    )
     g_in[...] = mid[:, :units]
     g_out[...] = mid[:, units : 2 * units]
     g_ib[...] = mid[: units // TILE, 2 * units :]
@@ -810,15 +808,15 @@
         two = total[:, cut : cut + part] + exchange(total[:, cut + part :], "seq", 1)
         return one, two
 
-    def finished(one, two, first=2):
-        for step in range(first, row_bits + 1):
-            if step < row_bits:
-                one = row_step(one, step)
-            two = row_step(two, step - 1)
-        for step in range(seq_bits - 1):
-            one = seq_step(one, step)
-            two = seq_step(two, step + 1)
-        return one, exchange(one, "seq", 1 << (seq_bits - 1)), two, exchange(two, "seq", 1)
+    def finished(one, two):
+        for step in range(2, row_bits - 1):
+            one = row_step(one, step)
+        for step in range(2, row_bits - 1):
+            two = row_step(two, step)
+        both = row_step(jnp.concatenate([one, two], axis=1), row_bits - 1)
+        for step in range(1, seq_bits):
+            both = seq_step(both, step)
+        return both, exchange(both, "seq", 1)
 
     received = exchange(mid_send, "rows", 1)
     back0 = back(0, d_context)
@@ -860,7 +858,8 @@
     rest = rest_keep + exchange(rest_send, "rows", 1)
     rest, mid = tied(rest, mid)
     rest_one, rest_two = opened(rest)
-    rest_one, rest_two, edges = lax.optimization_barrier((rest_one, rest_two, edges))
+    rest_two = row_step(rest_two, 1)
+    rest_two, edges = tied(rest_two, edges)
     nothing = jnp.zeros((block - span, width), f32)
     if n_seq == 2:
         arrived = exchange(edges[0], "seq", 1).astype(f32)

time: 83.5 us -> 80.3 us (0.962)
  waiting for transfers between devices: 16.7 us -> 11.6 us
  starting transfers between devices: 23 us -> 24.8 us
    ppermute x17 -> x15, waiting for transfers between devices: 16.7 us -> 11.6 us  [exchange(): return lax.ppermute(value, axis, [(i, i ^ bit) for i in range(count)])]
    ppermute x17 -> x15, starting transfers between devices: 23 us -> 24.8 us  [exchange(): return lax.ppermute(value, axis, [(i, i ^ bit) for i in range(count)])]
  transfers between devices with their start and end apart: 17 -> 15, of which waited for: 8 -> 8; matrix products, arithmetic and copies ran while one was open for 1% -> 2% of each run, Pallas kernels for 27% -> 28%
where the time goes in v1:
time: 80.3 us; the launch traced here: 80.1 us
  Pallas kernels  39.7 us (49%)
  starting transfers between devices  24.8 us (31%)
  waiting for transfers between devices  11.6 us (14%)
  other arithmetic  1.7 us (2%)
  local copies, waits for them, and re-layouts  1.18 us (1%)
  between operations  1.14 us (1%)
    ppermute x15, starting transfers between devices, exchange(): return lax.ppermute(value, axis, [(i, i ^ bit) for i in range(count)])  24.8 us
    pallas_call x3, Pallas kernels, back(): pl.pallas_call(partial(attend_back_kernel, scale=scale, p=p), out_shape=(...  11.8 us
    ppermute x15, waiting for transfers between devices, exchange(): return lax.ppermute(value, axis, [(i, i ^ bit) for i in range(count)])  11.6 us
    pallas_call x1, Pallas kernels, local(): pl.pallas_call(partial(attend_kernel, scale=scale, n_seq=n_seq), out_shap...  8.68 us
    pallas_call x1, Pallas kernels, local(): pl.pallas_call(partial(middle_kernel, step=512, share=share), out_shape=(...  8.04 us
    pallas_call x1, Pallas kernels, local(): pl.pallas_call(project_kernel, out_shape=(shape((PAIRS, block, TILE), bf1...  4.52 us
    pallas_call x1, Pallas kernels, local(): pl.pallas_call(partial(weight_grad_kernel, n_seq=n_seq), out_shape=(shape...  3.26 us
    pallas_call x1, Pallas kernels, local(): pl.pallas_call(input_grad_kernel, out_shape=(shape((tokens, width), f32),...  2.53 us
  transfers between devices with their start and end apart: 15, of which 8 were waited for; matrix products, arithmetic and copies ran while one was open for 2% of the time, Pallas kernels for 28%

profile of v1, /device:TPU:0, one launch (start us, length us, event | category | flops | bytes accessed | tf_op | source)
XLA Modules:
  0.0 80.1 jit_solution(15398469722031357209)
XLA Ops:
  0.7 1.0 %dynamic-slice_bitcast_fusion = bf16[256,384]{1,0:T(8,128)(2,1)S(1)} fusion(bf16[1,512,384]{2,1,0:T(8,128)(2,1)} %param.18, s32[]{:T(128)S(6)} %select_n.11), kind=kLoop, calls=%fused_computation.8 | loop fusion | bytes 393220 | tf_op jit(solution)/shard_map/dynamic_slice | solution.py:667
  1.6 3.0 %collective-permute-start = (bf16[256,384]{1,0:T(8,128)(2,1)S(1)}, bf16[256,384]{1,0:T(8,128)(2,1)S(1)}, u32[]{:S(2)}, u32[]{:S(2)}) collective-permute-start(bf16[256,384]{1,0:T(8,128)(2,1)S(1)} %dynamic-slice_bitcast_fusion), channel_id=1, source_target_pairs={{0,16},{16,0},{1,17},{17,1},{2,18},{18,2},{3,19},{19,3},{4,20},{20... | collective-permute-start | bytes 589832 | tf_op jit(solution)/shard_map/ppermute | solution.py:73
  4.7 4.5 %project.1 = (bf16[3,512,128]{2,1,0:T(8,128)(2,1)S(1)}, bf16[3,512,128]{2,1,0:T(8,128)(2,1)S(1)}, bf16[3,512,128]{2,1,0:T(8,128)(2,1)S(1)}, bf16[3,512,128]{2,1,...) custom-call(s32[384,4]{1,0:T(8,128)} %constant.19.clone.refs_0_, ...), custom_call_target="tpu_custom_call" | custom-call | tf_op jit(solution)/shard_map/project/pallas_call | solution.py:689
  9.2 0.3 collective-permute-done.refs_0_
  9.6 8.7 %attend.1 = (bf16[512,384]{1,0:T(8,128)(2,1)S(1)}, bf16[3,2,4,128,640]{4,3,2,1,0:T(8,128)(2,1)S(1)}, bf16[3,1024,128]{2,1,0:T(8,128)(2,1)S(1)}, bf16[3,1024,128]{2,1,0:T(8,128)(2,1)S(1)}) custom-call(bf16[3,512,128]{2,1,0:T(8,128)(2,1)S(1)} %get-tuple-element.82.q, bf16[3,512,128]{2,1,0:T(8,128)(2,1)S(1)} %get-tuple-element.83.k_own, ...), custom_call_target="tpu_custom_call" | custom-call | tf_op jit(solution)/shard_map/attend/pallas_call | solution.py:711
  18.4 8.0 %middle.1 = (bf16[512,384]{1,0:T(8,128)(2,1)}, f32[512,384]{1,0:T(8,128)S(1)}, bf16[512,384]{1,0:T(8,128)(2,1)S(1)}, bf16[192,3200]{1,0:T(8,128)(2,1)S(1)}, bf16...) custom-call(bf16[512,384]{1,0:T(8,128)(2,1)S(1)} %bitcast.12, bf16[512,384]{1,0:T(8,128)(2,1)S(1)} %get-tuple-element.87.context, ...), custom_call_target="tpu_custom_call" | custom-call | tf_op jit(solution)/shard_map/middle/pallas_call | solution.py:728
  26.6 3.9 %attend_back.3 = (bf16[512,128]{1,0:T(8,128)(2,1)S(1)}, bf16[1024,128]{1,0:T(8,128)(2,1)S(1)}, bf16[1024,128]{1,0:T(8,128)(2,1)S(1)}, bf16[128,512]{1,0:T(8,128)(2,1)S(1)}, bf16[128,512]{1,0:T(8,128)(2,1)S(1)}) custom-call(bf16[3,512,128]{2,1,0:T(8,128)(2,1)S(1)} %get-tuple-element.82.q, bf16[3,1024,128]{2,1,0:T(8,128)(2,1)S(1)} %get-tuple-element.97.k, ...), custom_call_target="tpu_custom_call" | custom-call | flops 1000 | bytes 1000 | tf_op jit(solution)/shard_map/attend_back/pallas_call | solution.py:764
  30.4 0.3 add.44
  30.8 1.8 %collective-permute-start.3 = (bf16[96,3200]{1,0:T(8,128)(2,1)S(1)}, bf16[96,3200]{1,0:T(8,128)(2,1)S(1)}, u32[]{:S(2)}, u32[]{:S(2)}) collective-permute-start(bf16[96,3200]{1,0:T(8,128)(2,1)S(1)} %slice.58), channel_id=1, source_target_pairs={{0,2},{1,3},{2,0},{3,1},{4,6},{5,7},{6,4},{7,5},{8,10},{9,11},{10,... | collective-permute-start | bytes 1843208 | tf_op jit(solution)/shard_map/ppermute | solution.py:73
  32.6 4.1 %attend_back.5 = (bf16[512,128]{1,0:T(8,128)(2,1)S(1)}, bf16[1024,128]{1,0:T(8,128)(2,1)S(1)}, bf16[1024,128]{1,0:T(8,128)(2,1)S(1)}, bf16[128,512]{1,0:T(8,128)(2,1)S(1)}, bf16[128,512]{1,0:T(8,128)(2,1)S(1)}) custom-call(bf16[3,512,128]{2,1,0:T(8,128)(2,1)S(1)} %get-tuple-element.82.q, bf16[3,1024,128]{2,1,0:T(8,128)(2,1)S(1)} %get-tuple-element.97.k, ...), custom_call_target="tpu_custom_call" | custom-call | flops 1000 | bytes 1000 | tf_op jit(solution)/shard_map/attend_back/pallas_call | solution.py:764
  36.7 3.9 %attend_back.4 = (bf16[512,128]{1,0:T(8,128)(2,1)S(1)}, bf16[1024,128]{1,0:T(8,128)(2,1)S(1)}, bf16[1024,128]{1,0:T(8,128)(2,1)S(1)}, bf16[128,512]{1,0:T(8,128)(2,1)S(1)}, bf16[128,512]{1,0:T(8,128)(2,1)S(1)}) custom-call(bf16[3,512,128]{2,1,0:T(8,128)(2,1)S(1)} %get-tuple-element.82.q, bf16[3,1024,128]{2,1,0:T(8,128)(2,1)S(1)} %get-tuple-element.97.k, ...), custom_call_target="tpu_custom_call" | custom-call | flops 1000 | bytes 1000 | tf_op jit(solution)/shard_map/attend_back/pallas_call | solution.py:764
  40.6 3.3 %weight_grad.1 = (bf16[192,2944]{1,0:T(8,128)(2,1)S(1)}, bf16[192,2944]{1,0:T(8,128)(2,1)S(1)}) custom-call(bf16[384,512]{1,0:T(8,128)(2,1)S(1)} %get-tuple-element.90.x_t, bf16[384,512]{1,0:T(8,128)(2,1)S(1)} %get-tuple-element.91.rel_t, bf16[384,384]{1,0:T(8,128)(2,1)S(1)} %get-tuple-element.92.w_pk_t, bf16[384,384]{1,0:T(8,128)(2,1)S(1)} %get-tuple-element.93.w_pq_t, ...), custom_call_target="tpu_custom_call" | custom-call | flops 1000 | bytes 1000 | tf_op jit(solution)/shard_map/weight_grad/pallas_call | solution.py:836
  44.1 2.5 %input_grad.1 = (f32[512,384]{1,0:T(8,128)S(1)}, bf16[256,384]{1,0:T(8,128)(2,1)S(1)}) custom-call(bf16[512,128]{1,0:T(8,128)(2,1)S(1)} %get-tuple-element.103.refs_1_.dq0, bf16[512,128]{1,0:T(8,128)(2,1)S(1)} %get-tuple-element.107.refs_2_.dq1, bf16[512,128]{1,0:T(8,128)(2,1)S(1)} %get-tuple-element.108.refs_3_.dq2, ...), custom_call_target="tpu_custom_call" | custom-call | flops 1000 | bytes 1000 | tf_op jit(solution)/shard_map/input_grad/pallas_call | solution.py:850
  46.6 0.5 collective-permute-done.3
  47.5 1.8 %collective-permute-start.10 = (bf16[96,1408]{1,0:T(8,128)(2,1)S(1)}, bf16[96,1408]{1,0:T(8,128)(2,1)S(1)}, u32[]{:S(2)}, u32[]{:S(2)}) collective-permute-start(bf16[96,1408]{1,0:T(8,128)(2,1)S(1)} %slice.68), channel_id=1, source_target_pairs={{0,2},{1,3},{2,0},{3,1},{4,6},{5,7},{6,4},{7,5},{8,10},{9,11},{10,... | collective-permute-start | bytes 811016 | tf_op jit(solution)/shard_map/ppermute | solution.py:73
  49.3 1.6 %collective-permute-start.4 = (bf16[192,768]{1,0:T(8,128)(2,1)S(1)}, bf16[192,768]{1,0:T(8,128)(2,1)S(1)}, u32[]{:S(2)}, u32[]{:S(2)}) collective-permute-start(bf16[192,768]{1,0:T(8,128)(2,1)S(1)} %slice.60), channel_id=1, source_target_pairs={{0,16},{16,0},{1,17},{17,1},{2,18},{18,2},{3,19},{19,3},{4,20},{20... | collective-permute-start | bytes 884744 | tf_op jit(solution)/shard_map/ppermute | solution.py:73
  50.9 1.6 %collective-permute-start.7 = (bf16[48,3200]{1,0:T(8,128)(2,1)S(1)}, bf16[48,3200]{1,0:T(8,128)(2,1)S(1)}, u32[]{:S(2)}, u32[]{:S(2)}) collective-permute-start(bf16[48,3200]{1,0:T(8,128)(2,1)S(1)} %slice.64), channel_id=1, source_target_pairs={{0,4},{1,5},{2,6},{3,7},{4,0},{5,1},{6,2},{7,3},{8,12},{9,13},{10,... | collective-permute-start | bytes 921608 | tf_op jit(solution)/shard_map/ppermute | solution.py:73
  52.6 3.2 %collective-permute-done.10 = bf16[96,1408]{1,0:T(8,128)(2,1)S(1)} collective-permute-done((bf16[96,1408]{1,0:T(8,128)(2,1)S(1)}, bf16[96,1408]{1,0:T(8,128)(2,1)S(1)}, u32[]{:S(2)}, u32[]{:S(2)}) %collective-permute-start.10) | collective-permute-done | bytes 270368 | tf_op jit(solution)/shard_map/ppermute | solution.py:73
  55.9 1.7 %collective-permute-start.11 = (bf16[48,1408]{1,0:T(8,128)(2,1)S(1)}, bf16[48,1408]{1,0:T(8,128)(2,1)S(1)}, u32[]{:S(2)}, u32[]{:S(2)}) collective-permute-start(bf16[48,1408]{1,0:T(8,128)(2,1)S(1)} %slice.80), channel_id=1, source_target_pairs={{0,4},{1,5},{2,6},{3,7},{4,0},{5,1},{6,2},{7,3},{8,12},{9,13},{10,... | collective-permute-start | bytes 405512 | tf_op jit(solution)/shard_map/ppermute | solution.py:73
  57.8 1.4 %collective-permute-start.5 = (bf16[96,768]{1,0:T(8,128)(2,1)S(1)}, bf16[96,768]{1,0:T(8,128)(2,1)S(1)}, u32[]{:S(2)}, u32[]{:S(2)}) collective-permute-start(bf16[96,768]{1,0:T(8,128)(2,1)S(1)} %slice.76), channel_id=1, source_target_pairs={{0,2},{1,3},{2,0},{3,1},{4,6},{5,7},{6,4},{7,5},{8,10},{9,11},{10,... | collective-permute-start | bytes 442376 | tf_op jit(solution)/shard_map/ppermute | solution.py:73
  59.2 1.5 %collective-permute-done.7 = bf16[48,3200]{1,0:T(8,128)(2,1)S(1)} collective-permute-done((bf16[48,3200]{1,0:T(8,128)(2,1)S(1)}, bf16[48,3200]{1,0:T(8,128)(2,1)S(1)}, u32[]{:S(2)}, u32[]{:S(2)}) %collective-permute-start.7) | collective-permute-done | bytes 307232 | tf_op jit(solution)/shard_map/ppermute | solution.py:73
  60.8 3.1 %collective-permute-start.8 = (bf16[24,3200]{1,0:T(8,128)(2,1)S(1)}, bf16[24,3200]{1,0:T(8,128)(2,1)S(1)}, u32[]{:S(2)}, u32[]{:S(2)}) collective-permute-start(bf16[24,3200]{1,0:T(8,128)(2,1)S(1)} %slice.78), channel_id=1, source_target_pairs={{0,8},{1,9},{2,10},{3,11},{4,12},{5,13},{6,14},{7,15},{8,0},{9,1},... | collective-permute-start | bytes 460808 | tf_op jit(solution)/shard_map/ppermute | solution.py:73
  64.0 1.2 %collective-permute-start.12 = (bf16[48,768]{1,0:T(8,128)(2,1)S(1)}, bf16[48,768]{1,0:T(8,128)(2,1)S(1)}, u32[]{:S(2)}, u32[]{:S(2)}) collective-permute-start(bf16[48,768]{1,0:T(8,128)(2,1)S(1)} %slice.72), channel_id=1, source_target_pairs={{0,4},{1,5},{2,6},{3,7},{4,0},{5,1},{6,2},{7,3},{8,12},{9,13},{10,... | collective-permute-start | bytes 221192 | tf_op jit(solution)/shard_map/ppermute | solution.py:73
  65.2 1.1 %collective-permute-start.6 = (bf16[256,384]{1,0:T(8,128)(2,1)S(1)}, bf16[256,384]{1,0:T(8,128)(2,1)S(1)}, u32[]{:S(2)}, u32[]{:S(2)}) collective-permute-start(bf16[256,384]{1,0:T(8,128)(2,1)S(1)} %get-tuple-element.131), channel_id=1, source_target_pairs={{0,16},{16,0},{1,17},{17,1},{2,18},{18,2},{3,19},{19,3},{4,20},{20... | collective-permute-start | bytes 589832 | tf_op jit(solution)/shard_map/ppermute | solution.py:73
  66.3 2.1 %collective-permute-done.12 = bf16[48,768]{1,0:T(8,128)(2,1)S(1)} collective-permute-done((bf16[48,768]{1,0:T(8,128)(2,1)S(1)}, bf16[48,768]{1,0:T(8,128)(2,1)S(1)}, u32[]{:S(2)}, u32[]{:S(2)}) %collective-permute-start.12) | collective-permute-done | bytes 73760 | tf_op jit(solution)/shard_map/ppermute | solution.py:73
  68.4 2.1 %collective-permute-start.13 = (bf16[24,2176]{1,0:T(8,128)(2,1)S(1)}, bf16[24,2176]{1,0:T(8,128)(2,1)S(1)}, u32[]{:S(2)}, u32[]{:S(2)}) collective-permute-start(bf16[24,2176]{1,0:T(8,128)(2,1)S(1)} %pad_maximum_fusion), channel_id=1, source_target_pairs={{0,8},{1,9},{2,10},{3,11},{4,12},{5,13},{6,14},{7,15},{8,0},{9,1},... | collective-permute-start | bytes 313352 | tf_op jit(solution)/shard_map/ppermute | solution.py:73
  70.5 1.5 %collective-permute-start.9 = (bf16[24,3200]{1,0:T(8,128)(2,1)S(1)}, bf16[24,3200]{1,0:T(8,128)(2,1)S(1)}, u32[]{:S(2)}, u32[]{:S(2)}) collective-permute-start(bf16[24,3200]{1,0:T(8,128)(2,1)S(1)} %slice_add_fusion.4.refs_0_), channel_id=1, source_target_pairs={{0,16},{16,0},{1,17},{17,1},{2,18},{18,2},{3,19},{19,3},{4,20},{20... | collective-permute-start | bytes 460808 | tf_op jit(solution)/shard_map/ppermute | solution.py:73
  72.1 2.0 %collective-permute-done.13 = bf16[24,2176]{1,0:T(8,128)(2,1)S(1)} collective-permute-done((bf16[24,2176]{1,0:T(8,128)(2,1)S(1)}, bf16[24,2176]{1,0:T(8,128)(2,1)S(1)}, u32[]{:S(2)}, u32[]{:S(2)}) %collective-permute-start.13) | collective-permute-done | bytes 104480 | tf_op jit(solution)/shard_map/ppermute | solution.py:73
  74.1 2.4 %collective-permute-start.14 = (bf16[24,2176]{1,0:T(8,128)(2,1)S(1)}, bf16[24,2176]{1,0:T(8,128)(2,1)S(1)}, u32[]{:S(2)}, u32[]{:S(2)}) collective-permute-start(bf16[24,2176]{1,0:T(8,128)(2,1)S(1)} %fusion.2.refs_2_), channel_id=1, source_target_pairs={{0,16},{16,0},{1,17},{17,1},{2,18},{18,2},{3,19},{19,3},{4,20},{20... | collective-permute-start | bytes 313352 | tf_op jit(solution)/shard_map/ppermute | solution.py:73
  76.5 0.8 %fusion = bf16[1,512,384]{2,1,0:T(8,128)(2,1)} fusion(f32[512,384]{1,0:T(8,128)S(1)} %get-tuple-element.125, f32[256,384]{1,0:T(8,128)S(1)} %convert_element_type.6, pred[]{:T(512)S(6)} %eq.3), kind=kLoop, calls=%fused_computation.2 | loop fusion | flops 589824 | bytes 1572865 | tf_op jit(solution)/shard_map/reshape | solution.py:912
  77.4 1.8 %collective-permute-done.14.refs_3_ = bf16[24,2176]{1,0:T(8,128)(2,1)S(1)} collective-permute-done((bf16[24,2176]{1,0:T(8,128)(2,1)S(1)}, bf16[24,2176]{1,0:T(8,128)(2,1)S(1)}, u32[]{:S(2)}, u32[]{:S(2)}) %collective-permute-start.14) | collective-permute-done | bytes 104480 | tf_op jit(solution)/shard_map/ppermute | solution.py:73
  79.2 0.8 %final.1 = (f32[24,384]{1,0:T(8,128)}, f32[24,384]{1,0:T(8,128)}, f32[24,384]{1,0:T(8,128)}, f32[24,384]{1,0:T(8,128)}, f32[24,512]{1,0:T(8,128)}, /*index=5*/f3...) custom-call(bf16[24,3200]{1,0:T(8,128)(2,1)S(1)} %slice_add_fusion.4, ...), custom_call_target="tpu_custom_call" | custom-call | tf_op jit(solution)/shard_map/final/pallas_call | solution.py:889
  (58 shorter events, 1.3 us)
Async XLA Ops:
  1.6 7.9 %collective-permute-start = (bf16[256,384]{1,0:T(8,128)(2,1)S(1)}, bf16[256,384]{1,0:T(8,128)(2,1)S(1)}, u32[]{:S(2)}, u32[]{:S(2)}) collective-permute-start(bf16[256,384]{1,0:T(8,128)(2,1)S(1)} %dynamic-slice_bitcast_fusion), channel_id=1, source_target_pairs={{0,16},{16,0},{1,17},{17,1},{2,18},{18,2},{3,19},{19,3},{4,20},{20... | collective-permute-start | bytes 589832 | tf_op jit(solution)/shard_map/ppermute | solution.py:73
  4.6 4.9 %copy-start.1 = (bf16[384,384]{1,0:T(8,128)(2,1)S(1)}, bf16[384,384]{1,0:T(8,128)(2,1)}, u32[]{:S(2)}) copy-start(bf16[384,384]{1,0:T(8,128)(2,1)} %w_key.3) | copy-start | bytes 884740
  4.6 4.9 %copy-start.2 = (bf16[384,384]{1,0:T(8,128)(2,1)S(1)}, bf16[384,384]{1,0:T(8,128)(2,1)}, u32[]{:S(2)}) copy-start(bf16[384,384]{1,0:T(8,128)(2,1)} %w_value.3) | copy-start | bytes 884740
  4.6 4.9 %copy-start.8 = (bf16[4,384]{1,0:T(4,128)(2,1)S(1)}, bf16[4,384]{1,0:T(4,128)(2,1)}, u32[]{:S(2)}) copy-start(bf16[4,384]{1,0:T(4,128)(2,1)} %biases.3) | copy-start | bytes 9220
  4.6 13.7 %copy-start.6 = (bf16[1,512,384]{2,1,0:T(8,128)(2,1)S(1)}, bf16[1,512,384]{2,1,0:T(8,128)(2,1)}, u32[]{:S(2)}) copy-start(bf16[1,512,384]{2,1,0:T(8,128)(2,1)} %param.19) | copy-start | bytes 1179652
  4.6 13.7 %copy-start.7 = (bf16[384,384]{1,0:T(8,128)(2,1)S(1)}, bf16[384,384]{1,0:T(8,128)(2,1)}, u32[]{:S(2)}) copy-start(bf16[384,384]{1,0:T(8,128)(2,1)} %w_output.1) | copy-start | bytes 884740
  4.7 13.7 %copy-start.12 = (bf16[2,384]{1,0:T(2,128)(2,1)S(1)}, bf16[2,384]{1,0:T(2,128)(2,1)}, u32[]{:S(2)}) copy-start(bf16[2,384]{1,0:T(2,128)(2,1)} %shifts.1) | copy-start | bytes 4612
  9.6 8.8 %copy-start.3 = (bf16[1,512,384]{2,1,0:T(8,128)(2,1)S(1)}, bf16[1,512,384]{2,1,0:T(8,128)(2,1)}, u32[]{:S(2)}) copy-start(bf16[1,512,384]{2,1,0:T(8,128)(2,1)} %param.18) | copy-start | bytes 1179652
  9.6 8.8 %copy-start.4 = (bf16[384,1536]{1,0:T(8,128)(2,1)S(1)}, bf16[384,1536]{1,0:T(8,128)(2,1)}, u32[]{:S(2)}) copy-start(bf16[384,1536]{1,0:T(8,128)(2,1)} %w_inner.1) | copy-start | bytes 3538948
  9.6 8.8 %copy-start.5 = (bf16[1536,384]{1,0:T(8,128)(2,1)S(1)}, bf16[1536,384]{1,0:T(8,128)(2,1)}, u32[]{:S(2)}) copy-start(bf16[1536,384]{1,0:T(8,128)(2,1)} %w_outer.1) | copy-start | bytes 3538948
  9.6 8.8 %copy-start.9 = (bf16[1536]{0:T(1024)(128)(2,1)S(1)}, bf16[1536]{0:T(1024)(128)(2,1)}, u32[]{:S(2)}) copy-start(bf16[1536]{0:T(1024)(128)(2,1)} %inner_bias.1) | copy-start | bytes 9220
  9.6 8.8 %copy-start.10 = (s32[1,512]{1,0:T(1,128)S(1)}, s32[1,512]{1,0:T(1,128)}, u32[]{:S(2)}) copy-start(s32[1,512]{1,0:T(1,128)} %mask.1) | copy-start | bytes 6148
  9.6 8.8 %copy-start.11 = (bf16[2,384]{1,0:T(2,128)(2,1)S(1)}, bf16[2,384]{1,0:T(2,128)(2,1)}, u32[]{:S(2)}) copy-start(bf16[2,384]{1,0:T(2,128)(2,1)} %gains.1) | copy-start | bytes 4612
  9.6 8.8 %copy-start.13 = (bf16[384]{0:T(512)(128)(2,1)S(1)}, bf16[384]{0:T(512)(128)(2,1)}, u32[]{:S(2)}) copy-start(bf16[384]{0:T(512)(128)(2,1)} %outer_bias.1) | copy-start | bytes 2308
  26.5 14.1 %copy-start = (f32[512,384]{1,0:T(8,128)}, f32[512,384]{1,0:T(8,128)S(1)}, u32[]{:S(2)}) copy-start(f32[512,384]{1,0:T(8,128)S(1)} %get-tuple-element.123.d_first) | copy-start | bytes 2359300
  26.5 3.9 %collective-permute-start.1 = (bf16[192,3200]{1,0:T(8,128)(2,1)S(1)}, bf16[192,3200]{1,0:T(8,128)(2,1)S(1)}, u32[]{:S(2)}, u32[]{:S(2)}) collective-permute-start(bf16[192,3200]{1,0:T(8,128)(2,1)S(1)} %get-tuple-element.105), channel_id=1, source_target_pairs={{0,1},{1,0},{2,3},{3,2},{4,5},{5,4},{6,7},{7,6},{8,9},{9,8},{10,11... | collective-permute-start | bytes 3686408 | tf_op jit(solution)/shard_map/ppermute | solution.py:73
  30.8 16.3 %collective-permute-start.3 = (bf16[96,3200]{1,0:T(8,128)(2,1)S(1)}, bf16[96,3200]{1,0:T(8,128)(2,1)S(1)}, u32[]{:S(2)}, u32[]{:S(2)}) collective-permute-start(bf16[96,3200]{1,0:T(8,128)(2,1)S(1)} %slice.58), channel_id=1, source_target_pairs={{0,2},{1,3},{2,0},{3,1},{4,6},{5,7},{6,4},{7,5},{8,10},{9,11},{10,... | collective-permute-start | bytes 1843208 | tf_op jit(solution)/shard_map/ppermute | solution.py:73
  43.8 3.4 %collective-permute-start.2 = (bf16[192,2944]{1,0:T(8,128)(2,1)S(1)}, bf16[192,2944]{1,0:T(8,128)(2,1)S(1)}, u32[]{:S(2)}, u32[]{:S(2)}) collective-permute-start(bf16[192,2944]{1,0:T(8,128)(2,1)S(1)} %get-tuple-element.127), channel_id=1, source_target_pairs={{0,1},{1,0},{2,3},{3,2},{4,5},{5,4},{6,7},{7,6},{8,9},{9,8},{10,11... | collective-permute-start | bytes 3391496 | tf_op jit(solution)/shard_map/ppermute | solution.py:73
  47.5 8.3 %collective-permute-start.10 = (bf16[96,1408]{1,0:T(8,128)(2,1)S(1)}, bf16[96,1408]{1,0:T(8,128)(2,1)S(1)}, u32[]{:S(2)}, u32[]{:S(2)}) collective-permute-start(bf16[96,1408]{1,0:T(8,128)(2,1)S(1)} %slice.68), channel_id=1, source_target_pairs={{0,2},{1,3},{2,0},{3,1},{4,6},{5,7},{6,4},{7,5},{8,10},{9,11},{10,... | collective-permute-start | bytes 811016 | tf_op jit(solution)/shard_map/ppermute | solution.py:73
  49.3 8.4 %collective-permute-start.4 = (bf16[192,768]{1,0:T(8,128)(2,1)S(1)}, bf16[192,768]{1,0:T(8,128)(2,1)S(1)}, u32[]{:S(2)}, u32[]{:S(2)}) collective-permute-start(bf16[192,768]{1,0:T(8,128)(2,1)S(1)} %slice.60), channel_id=1, source_target_pairs={{0,16},{16,0},{1,17},{17,1},{2,18},{18,2},{3,19},{19,3},{4,20},{20... | collective-permute-start | bytes 884744 | tf_op jit(solution)/shard_map/ppermute | solution.py:73
  50.9 9.8 %collective-permute-start.7 = (bf16[48,3200]{1,0:T(8,128)(2,1)S(1)}, bf16[48,3200]{1,0:T(8,128)(2,1)S(1)}, u32[]{:S(2)}, u32[]{:S(2)}) collective-permute-start(bf16[48,3200]{1,0:T(8,128)(2,1)S(1)} %slice.64), channel_id=1, source_target_pairs={{0,4},{1,5},{2,6},{3,7},{4,0},{5,1},{6,2},{7,3},{8,12},{9,13},{10,... | collective-permute-start | bytes 921608 | tf_op jit(solution)/shard_map/ppermute | solution.py:73
  55.9 9.3 %collective-permute-start.11 = (bf16[48,1408]{1,0:T(8,128)(2,1)S(1)}, bf16[48,1408]{1,0:T(8,128)(2,1)S(1)}, u32[]{:S(2)}, u32[]{:S(2)}) collective-permute-start(bf16[48,1408]{1,0:T(8,128)(2,1)S(1)} %slice.80), channel_id=1, source_target_pairs={{0,4},{1,5},{2,6},{3,7},{4,0},{5,1},{6,2},{7,3},{8,12},{9,13},{10,... | collective-permute-start | bytes 405512 | tf_op jit(solution)/shard_map/ppermute | solution.py:73
  57.8 6.1 %collective-permute-start.5 = (bf16[96,768]{1,0:T(8,128)(2,1)S(1)}, bf16[96,768]{1,0:T(8,128)(2,1)S(1)}, u32[]{:S(2)}, u32[]{:S(2)}) collective-permute-start(bf16[96,768]{1,0:T(8,128)(2,1)S(1)} %slice.76), channel_id=1, source_target_pairs={{0,2},{1,3},{2,0},{3,1},{4,6},{5,7},{6,4},{7,5},{8,10},{9,11},{10,... | collective-permute-start | bytes 442376 | tf_op jit(solution)/shard_map/ppermute | solution.py:73
  60.8 9.7 %collective-permute-start.8 = (bf16[24,3200]{1,0:T(8,128)(2,1)S(1)}, bf16[24,3200]{1,0:T(8,128)(2,1)S(1)}, u32[]{:S(2)}, u32[]{:S(2)}) collective-permute-start(bf16[24,3200]{1,0:T(8,128)(2,1)S(1)} %slice.78), channel_id=1, source_target_pairs={{0,8},{1,9},{2,10},{3,11},{4,12},{5,13},{6,14},{7,15},{8,0},{9,1},... | collective-permute-start | bytes 460808 | tf_op jit(solution)/shard_map/ppermute | solution.py:73
  64.0 4.4 %collective-permute-start.12 = (bf16[48,768]{1,0:T(8,128)(2,1)S(1)}, bf16[48,768]{1,0:T(8,128)(2,1)S(1)}, u32[]{:S(2)}, u32[]{:S(2)}) collective-permute-start(bf16[48,768]{1,0:T(8,128)(2,1)S(1)} %slice.72), channel_id=1, source_target_pairs={{0,4},{1,5},{2,6},{3,7},{4,0},{5,1},{6,2},{7,3},{8,12},{9,13},{10,... | collective-permute-start | bytes 221192 | tf_op jit(solution)/shard_map/ppermute | solution.py:73
  65.2 11.3 %collective-permute-start.6 = (bf16[256,384]{1,0:T(8,128)(2,1)S(1)}, bf16[256,384]{1,0:T(8,128)(2,1)S(1)}, u32[]{:S(2)}, u32[]{:S(2)}) collective-permute-start(bf16[256,384]{1,0:T(8,128)(2,1)S(1)} %get-tuple-element.131), channel_id=1, source_target_pairs={{0,16},{16,0},{1,17},{17,1},{2,18},{18,2},{3,19},{19,3},{4,20},{20... | collective-permute-start | bytes 589832 | tf_op jit(solution)/shard_map/ppermute | solution.py:73
  68.4 5.7 %collective-permute-start.13 = (bf16[24,2176]{1,0:T(8,128)(2,1)S(1)}, bf16[24,2176]{1,0:T(8,128)(2,1)S(1)}, u32[]{:S(2)}, u32[]{:S(2)}) collective-permute-start(bf16[24,2176]{1,0:T(8,128)(2,1)S(1)} %pad_maximum_fusion), channel_id=1, source_target_pairs={{0,8},{1,9},{2,10},{3,11},{4,12},{5,13},{6,14},{7,15},{8,0},{9,1},... | collective-permute-start | bytes 313352 | tf_op jit(solution)/shard_map/ppermute | solution.py:73
  70.5 6.8 %collective-permute-start.9 = (bf16[24,3200]{1,0:T(8,128)(2,1)S(1)}, bf16[24,3200]{1,0:T(8,128)(2,1)S(1)}, u32[]{:S(2)}, u32[]{:S(2)}) collective-permute-start(bf16[24,3200]{1,0:T(8,128)(2,1)S(1)} %slice_add_fusion.4.refs_0_), channel_id=1, source_target_pairs={{0,16},{16,0},{1,17},{17,1},{2,18},{18,2},{3,19},{19,3},{4,20},{20... | collective-permute-start | bytes 460808 | tf_op jit(solution)/shard_map/ppermute | solution.py:73
  74.1 5.0 %collective-permute-start.14 = (bf16[24,2176]{1,0:T(8,128)(2,1)S(1)}, bf16[24,2176]{1,0:T(8,128)(2,1)S(1)}, u32[]{:S(2)}, u32[]{:S(2)}) collective-permute-start(bf16[24,2176]{1,0:T(8,128)(2,1)S(1)} %fusion.2.refs_2_), channel_id=1, source_target_pairs={{0,16},{16,0},{1,17},{17,1},{2,18},{18,2},{3,19},{19,3},{4,20},{20... | collective-permute-start | bytes 313352 | tf_op jit(solution)/shard_map/ppermute | solution.py:73

commit v2 on v1

--- a/solution.py
+++ b/solution.py
@@ -270,6 +270,7 @@
     turn_scr,
     shifted_scr,
     dv_scr,
+    dk_scr,
     *,
     scale,
     p,
@@ -302,7 +303,6 @@
         flat = value.astype(f32).T
         return [jnp.where(row_halves[h], flat, 0.0).astype(bf16) for h in range(2)]
 
-    stacked_q = [split_rows(q[p, part(it), :]) for it in range(tiles)]
     for it in range(tiles):
         dct = d_context[part(it), cols]
         overlap = dct.astype(f32) * context[part(it), cols].astype(f32)
@@ -333,17 +333,21 @@
     for it in range(tiles):
         for b in range(blocks):
             turn_scr[it, b] = nt(flip, ds_scr[it, :, part(b)]).astype(bf16)
+    reverse = nn(flip, jnp.concatenate([k[p, part(wb), :] for wb in range(keys)], axis=1))
+    reverse_t = [reverse[:, part(wb)].T for wb in range(keys)]
     for it in range(tiles):
-        both = slice(2 * it * TILE, 2 * (it + 1) * TILE)
-        total = nn(
-            jnp.concatenate([ds_scr[it], band_scr[both, :]], axis=1),
-            jnp.concatenate([k[p, window(it), :], pk[p]], axis=0),
-        )
-        dq_out[part(it), :] = jnp.where(halves[0], total[:TILE], total[TILE:]).astype(bf16)
+        left = jnp.concatenate([reverse_t[it + b].astype(bf16) for b in range(blocks)], axis=1)
+        direct = nn(left, jnp.concatenate([turn_scr[it, b] for b in range(blocks)], axis=0))
+        direct = jnp.where(row_halves[0], direct[:, :TILE], direct[:, TILE:]).T
+        total = nn(band_scr[2 * it * TILE : 2 * (it + 1) * TILE, :], pk[p])
+        total = jnp.where(halves[0], total[:TILE], total[TILE:])
+        dq_out[part(it), :] = (direct + total).astype(bf16)
     turned = [split_turned(q[p, part(it), :]) for it in range(tiles)]
     dpk_out[...] = nn(jnp.concatenate(sum(turned, []), axis=1), band_scr[...]).astype(bf16)
     dv_scr[...] = jnp.zeros_like(dv_scr)
+    dk_scr[...] = jnp.zeros_like(dk_scr)
     for it in range(tiles):
+        dk_scr[:, window(it)] += nn(jnp.concatenate(turned[it], axis=1), ds_scr[it])
         dv_scr[:, window(it)] += nn(
             jnp.concatenate(split_turned(d_context[part(it), cols]), axis=1),
             jnp.concatenate([probs[p, 0, it], probs[p, 1, it]], axis=0),
@@ -374,21 +378,21 @@
     for wb in range(keys):
         low, high, first, last = key_block_range(wb, blocks, tiles)
         left, right = [], []
-        for e in range(low, high + 1):
-            it, b = wb - (blocks - 1) + e, blocks - 1 - e
-            left.append(turn_scr[it, b])
-            right.append(stacked_q[it])
         span = slice(first * TILE, (last + 1) * TILE)
         for h in range(2):
             left.append(shifted_scr[part(2 * wb + h), span])
             right.append(tables[h][span])
         total = nn(jnp.concatenate(left, axis=1), jnp.concatenate(right, axis=0))
         lows.append(total.astype(bf16))
-    natural = nn(flip, jnp.concatenate(lows, axis=1)).astype(bf16)
+    natural = nn(flip, jnp.concatenate(lows, axis=1))
     for wb in range(keys):
-        dk_out[part(wb), :] = natural[:, part(wb)]
-    reverse = nn(flip, jnp.concatenate([k[p, part(wb), :] for wb in range(keys)], axis=1))
-    turned = sum([split_turned(reverse[:, part(wb)]) for wb in range(keys)], [])
+        direct = dk_scr[:, part(wb)].T
+        dk_out[part(wb), :] = (natural[:, part(wb)] + direct).astype(bf16)
+    turned = [
+        jnp.where(row_halves[h], reverse_t[wb], 0.0).astype(bf16)
+        for wb in range(keys)
+        for h in range(2)
+    ]
     dpq_out[...] = nn(jnp.concatenate(turned, axis=1), shifted_scr[...]).astype(bf16)
     for wb in range(keys):
         dv_out[part(wb), :] = dv_scr[:, part(wb)].T.astype(bf16)
@@ -427,6 +431,7 @@
     d_context,
     keep,
     send,
+    inner_out,
     rows_out,
     low_scr,
     active_scr,
@@ -435,7 +440,6 @@
     d_att_scr,
     *,
     step,
-    share,
 ):
     tokens, width = x.shape
     units = w_inner.shape[1]
@@ -502,18 +506,14 @@
 
     put(0, low_scr[...], d_inner_scr)
     put(units, d_outer_scr[...], active_scr)
-    line = nn(jnp.ones((8, tokens), bf16), d_inner_scr[...])[0:1]
-    lines = [line[:, c : c + TILE] for c in range(0, units, TILE)]
-    lines = jnp.concatenate(lines + [jnp.zeros((share - len(lines), TILE), f32)] * (share > len(lines)), axis=0)
-    lines = jnp.concatenate([lines] * (width // share), axis=0)
-    store_halves(keep, send, 2 * units, lines)
+    inner_out[...] = nn(jnp.ones((8, tokens), bf16), d_inner_scr[...])
     zero = jnp.zeros((1, width), f32)
     table = [zero, zero, zero, sums[5], sums[3], sums[0], sums[4], sums[1], sums[2]]
     rows_out[...] = jnp.concatenate(table + [zero] * (16 - len(table)), axis=0)
 
 
 def weight_grad_kernel(
-    x_t, rel_t, w_pk_t, w_pq_t, order, rows, context, d_first, *refs, n_seq
+    x_t, rel_t, w_pk_t, w_pq_t, order, rows, context, d_first, inner, *refs, n_seq, share
 ):
     edges = refs[: 1 if n_seq == 2 else 2]
     backs, (keep, send) = refs[len(edges) : -2], refs[-2:]
@@ -560,7 +560,21 @@
     known = jnp.where(place == 1, sum_v, known)
     known = jnp.where(place == 2, sum_p, known)
     padded = jnp.concatenate([known, jnp.zeros((TILE - known.shape[0], width), f32)], axis=0)
-    put(6 * width + count, nt(ord_, padded.astype(bf16)))
+    block = nt(ord_, padded.astype(bf16))
+    lines = [inner[0:1, c : c + TILE] for c in range(0, inner.shape[1], TILE)]
+    some = len(lines)
+    lines = jnp.concatenate(lines + [jnp.zeros((-some % 8, TILE), f32)] * (some % 8 > 0), axis=0)
+    if compact_bias(share, inner.shape[1]):
+        turned = pltpu.roll(lines, TILE // 2, 1)
+        picked = [t[j : j + 1] for j in range(some) for t in (turned, lines)]
+        picked += [jnp.zeros((share - 2 * some, TILE), f32)] * (share > 2 * some)
+        lines = jnp.concatenate(picked, axis=0)
+        lines = jnp.where(iota(lines.shape, 1) >= TILE // 2, lines, 0.0)
+        put(6 * width + count, block + jnp.concatenate([lines] * (width // share), axis=0))
+    else:
+        put(6 * width + count, block)
+        lines = [lines[:some]] + [jnp.zeros((share - some, TILE), f32)] * (share > some)
+        put(6 * width + count + TILE, jnp.concatenate(lines * (width // share), axis=0))
 
 
 def input_grad_kernel(
@@ -587,14 +601,18 @@
     own[...] = halo(slice(span, span + block)) + d_first[...] + nt(dq, w_query[...])
 
 
+def compact_bias(share, units):
+    return 2 * units // TILE <= share
+
+
 def final_kernel(*refs, width, units, count):
     (g_q, g_k, g_v, g_o, g_rel, g_pk, g_pq, g_bias, g_gain, g_shift, g_in, g_out, g_ob, g_ib) = (
         refs[4:]
     )
     low = lax.axis_index("seq") % 2 == 0
-
+    share = refs[0].shape[0]
     mid = refs[0][...].astype(f32) + refs[1][...].astype(f32)
-    cut, _ = column_cut(6 * width + count + TILE)
+    cut, _ = column_cut(6 * width + count + (1 if compact_bias(share, units) else 2) * TILE)
     mine, other = refs[2][...].astype(f32), refs[3][...].astype(f32)
     rest = jnp.concatenate(
         [
@@ -606,11 +624,23 @@
     )
     g_in[...] = mid[:, :units]
     g_out[...] = mid[:, units : 2 * units]
-    g_ib[...] = mid[: units // TILE, 2 * units :]
     for i, out in enumerate((g_q, g_k, g_v, g_pk, g_pq, g_o)):
         out[...] = rest[:, i * width : (i + 1) * width]
     g_rel[...] = rest[:, 6 * width : 6 * width + count]
-    lines = rest[:, 6 * width + count :].T
+    block = rest[:, 6 * width + count : 6 * width + count + TILE]
+    if compact_bias(share, units):
+        turned = pltpu.roll(block, TILE // 2, 1)
+        left = iota((1, TILE), 1) < TILE // 2
+        g_ib[...] = jnp.concatenate(
+            [
+                jnp.where(left, turned[2 * j : 2 * j + 1], block[2 * j + 1 : 2 * j + 2])
+                for j in range(units // TILE)
+            ],
+            axis=0,
+        )
+    else:
+        g_ib[...] = rest[: units // TILE, 6 * width + count + TILE :]
+    lines = block.T
     g_bias[...] = lines[0:4]
     g_gain[...] = lines[4:6]
     g_shift[...] = lines[6:8]
@@ -724,15 +754,16 @@
         name="attend",
     )(q3, k3, v3, pk_rev3, pq_rev3, w_key, w_value, attn_biases, *outside)
 
-    mid_cols = 2 * units + TILE
-    result, d_first, d_context, mid_keep, mid_send, rows = pl.pallas_call(
-        partial(middle_kernel, step=512, share=share),
+    mid_cols = 2 * units
+    result, d_first, d_context, mid_keep, mid_send, inner_sum, rows = pl.pallas_call(
+        partial(middle_kernel, step=512),
         out_shape=(
             shape((tokens, width), bf16),
             shape((tokens, width), f32),
             shape((tokens, width), bf16),
             shape((width // 2, mid_cols), bf16),
             shape((width // 2, mid_cols), bf16),
+            shape((8, units), f32),
             shape((16, width), f32),
         ),
         scratch_shapes=[
@@ -777,6 +808,7 @@
                 pltpu.VMEM((tiles, blocks, TILE, 2 * TILE), bf16),
                 pltpu.VMEM((2 * window, table), bf16),
                 pltpu.VMEM((TILE, window), f32),
+                pltpu.VMEM((TILE, window), f32),
             ],
             compiler_params=pltpu.CompilerParams(vmem_limit_bytes=20 * MiB),
             cost_estimate=pl.CostEstimate(
@@ -832,9 +864,9 @@
     dq = (dq0, dq1, dq2)
     dk, dv, dpk, dpq = ((back0[i], back1[i], back2[i]) for i in range(1, 5))
 
-    rest_cols = 6 * width + table + TILE
+    rest_cols = 6 * width + table + (1 if compact_bias(share, units) else 2) * TILE
     rest_keep, rest_send = pl.pallas_call(
-        partial(weight_grad_kernel, n_seq=n_seq),
+        partial(weight_grad_kernel, n_seq=n_seq, share=share),
         out_shape=(
             shape((width // 2, rest_cols), bf16),
             shape((width // 2, rest_cols), bf16),
@@ -842,7 +874,7 @@
         compiler_params=pltpu.CompilerParams(vmem_limit_bytes=20 * MiB),
         cost_estimate=pl.CostEstimate(flops=1000, bytes_accessed=1000, transcendentals=0),
         name="weight_grad",
-    )(x_t, rel_t, w_pk_t, w_pq_t, order, rows, context, d_first, *outside, *dq, *dk, *dv, *dpk, *dpq)
+    )(x_t, rel_t, w_pk_t, w_pq_t, order, rows, context, d_first, inner_sum, *outside, *dq, *dk, *dv, *dpk, *dpq)
 
     rest_send, d_first = tied(rest_send, d_first)
     edge = shape((span, width), bf16)

time: 80.3 us -> 79.7 us (level)
  waiting for transfers between devices: 11.6 us -> 9.69 us
  starting transfers between devices: 24.8 us -> 26.7 us
    ppermute x15, waiting for transfers between devices: 11.6 us -> 9.69 us  [exchange(): return lax.ppermute(value, axis, [(i, i ^ bit) for i in range(count)])]
    ppermute x15, starting transfers between devices: 24.8 us -> 26.7 us  [exchange(): return lax.ppermute(value, axis, [(i, i ^ bit) for i in range(count)])]
  transfers between devices with their start and end apart: 15 -> 15, of which waited for: 8 -> 8; matrix products, arithmetic and copies ran while one was open for 2% -> 2% of each run, Pallas kernels for 28% -> 27%
where the time goes in v2:
time: 79.7 us; the launch traced here: 79.5 us
  Pallas kernels  39 us (49%)
  starting transfers between devices  26.7 us (34%)
  waiting for transfers between devices  9.69 us (12%)
  other arithmetic  1.8 us (2%)
  local copies, waits for them, and re-layouts  1.17 us (1%)
  between operations  1.13 us (1%)
    ppermute x15, starting transfers between devices, exchange(): return lax.ppermute(value, axis, [(i, i ^ bit) for i in range(count)])  26.7 us
    pallas_call x3, Pallas kernels, back(): pl.pallas_call(partial(attend_back_kernel, scale=scale, p=p), out_shape=(...  11.2 us
    ppermute x15, waiting for transfers between devices, exchange(): return lax.ppermute(value, axis, [(i, i ^ bit) for i in range(count)])  9.69 us
    pallas_call x1, Pallas kernels, local(): pl.pallas_call(partial(attend_kernel, scale=scale, n_seq=n_seq), out_shap...  8.67 us
    pallas_call x1, Pallas kernels, local(): pl.pallas_call(partial(middle_kernel, step=512), out_shape=(shape((tokens...  8.03 us
    pallas_call x1, Pallas kernels, local(): pl.pallas_call(project_kernel, out_shape=(shape((PAIRS, block, TILE), bf1...  4.52 us
    pallas_call x1, Pallas kernels, local(): pl.pallas_call(partial(weight_grad_kernel, n_seq=n_seq, share=share), out...  3.25 us
    pallas_call x1, Pallas kernels, local(): pl.pallas_call(input_grad_kernel, out_shape=(shape((tokens, width), f32),...  2.53 us
  transfers between devices with their start and end apart: 15, of which 8 were waited for; matrix products, arithmetic and copies ran while one was open for 2% of the time, Pallas kernels for 27%

profile of v2, /device:TPU:0, one launch (start us, length us, event | category | flops | bytes accessed | tf_op | source)
XLA Modules:
  0.0 79.5 jit_solution(2418892224505934150)
XLA Ops:
  0.7 1.0 %dynamic-slice_bitcast_fusion = bf16[256,384]{1,0:T(8,128)(2,1)S(1)} fusion(bf16[1,512,384]{2,1,0:T(8,128)(2,1)} %param.18, s32[]{:T(128)S(6)} %select_n.11), kind=kLoop, calls=%fused_computation.8 | loop fusion | bytes 393220 | tf_op jit(solution)/shard_map/dynamic_slice | solution.py:697
  1.6 3.0 %collective-permute-start = (bf16[256,384]{1,0:T(8,128)(2,1)S(1)}, bf16[256,384]{1,0:T(8,128)(2,1)S(1)}, u32[]{:S(2)}, u32[]{:S(2)}) collective-permute-start(bf16[256,384]{1,0:T(8,128)(2,1)S(1)} %dynamic-slice_bitcast_fusion), channel_id=1, source_target_pairs={{0,16},{16,0},{1,17},{17,1},{2,18},{18,2},{3,19},{19,3},{4,20},{20... | collective-permute-start | bytes 589832 | tf_op jit(solution)/shard_map/ppermute | solution.py:73
  4.7 4.5 %project.1 = (bf16[3,512,128]{2,1,0:T(8,128)(2,1)S(1)}, bf16[3,512,128]{2,1,0:T(8,128)(2,1)S(1)}, bf16[3,512,128]{2,1,0:T(8,128)(2,1)S(1)}, bf16[3,512,128]{2,1,...) custom-call(s32[384,4]{1,0:T(8,128)} %constant.19.clone.refs_0_, ...), custom_call_target="tpu_custom_call" | custom-call | tf_op jit(solution)/shard_map/project/pallas_call | solution.py:719
  9.2 0.3 collective-permute-done.refs_0_
  9.6 8.7 %attend.1 = (bf16[512,384]{1,0:T(8,128)(2,1)S(1)}, bf16[3,2,4,128,640]{4,3,2,1,0:T(8,128)(2,1)S(1)}, bf16[3,1024,128]{2,1,0:T(8,128)(2,1)S(1)}, bf16[3,1024,128]{2,1,0:T(8,128)(2,1)S(1)}) custom-call(bf16[3,512,128]{2,1,0:T(8,128)(2,1)S(1)} %get-tuple-element.83.q, bf16[3,512,128]{2,1,0:T(8,128)(2,1)S(1)} %get-tuple-element.84.k_own, ...), custom_call_target="tpu_custom_call" | custom-call | tf_op jit(solution)/shard_map/attend/pallas_call | solution.py:741
  18.4 8.0 %middle.1 = (bf16[512,384]{1,0:T(8,128)(2,1)}, f32[512,384]{1,0:T(8,128)S(1)}, bf16[512,384]{1,0:T(8,128)(2,1)S(1)}, bf16[192,3072]{1,0:T(8,128)(2,1)S(1)}, bf16...) custom-call(bf16[512,384]{1,0:T(8,128)(2,1)S(1)} %bitcast.12, ...), custom_call_target="tpu_custom_call" | custom-call | tf_op jit(solution)/shard_map/middle/pallas_call | solution.py:758
  26.5 3.6 %attend_back.3 = (bf16[512,128]{1,0:T(8,128)(2,1)S(1)}, bf16[1024,128]{1,0:T(8,128)(2,1)S(1)}, bf16[1024,128]{1,0:T(8,128)(2,1)S(1)}, bf16[128,512]{1,0:T(8,128)(2,1)S(1)}, bf16[128,512]{1,0:T(8,128)(2,1)S(1)}) custom-call(bf16[3,512,128]{2,1,0:T(8,128)(2,1)S(1)} %get-tuple-element.83.q, bf16[3,1024,128]{2,1,0:T(8,128)(2,1)S(1)} %get-tuple-element.99.k, ...), custom_call_target="tpu_custom_call" | custom-call | flops 1000 | bytes 1000 | tf_op jit(solution)/shard_map/attend_back/pallas_call | solution.py:795
  30.2 0.4 add.44
  30.6 1.8 %collective-permute-start.3 = (bf16[96,3072]{1,0:T(8,128)(2,1)S(1)}, bf16[96,3072]{1,0:T(8,128)(2,1)S(1)}, u32[]{:S(2)}, u32[]{:S(2)}) collective-permute-start(bf16[96,3072]{1,0:T(8,128)(2,1)S(1)} %slice.58), channel_id=1, source_target_pairs={{0,2},{1,3},{2,0},{3,1},{4,6},{5,7},{6,4},{7,5},{8,10},{9,11},{10,... | collective-permute-start | bytes 1769480 | tf_op jit(solution)/shard_map/ppermute | solution.py:73
  32.4 3.9 %attend_back.5 = (bf16[512,128]{1,0:T(8,128)(2,1)S(1)}, bf16[1024,128]{1,0:T(8,128)(2,1)S(1)}, bf16[1024,128]{1,0:T(8,128)(2,1)S(1)}, bf16[128,512]{1,0:T(8,128)(2,1)S(1)}, bf16[128,512]{1,0:T(8,128)(2,1)S(1)}) custom-call(bf16[3,512,128]{2,1,0:T(8,128)(2,1)S(1)} %get-tuple-element.83.q, bf16[3,1024,128]{2,1,0:T(8,128)(2,1)S(1)} %get-tuple-element.99.k, ...), custom_call_target="tpu_custom_call" | custom-call | flops 1000 | bytes 1000 | tf_op jit(solution)/shard_map/attend_back/pallas_call | solution.py:795
  36.3 3.6 %attend_back.4 = (bf16[512,128]{1,0:T(8,128)(2,1)S(1)}, bf16[1024,128]{1,0:T(8,128)(2,1)S(1)}, bf16[1024,128]{1,0:T(8,128)(2,1)S(1)}, bf16[128,512]{1,0:T(8,128)(2,1)S(1)}, bf16[128,512]{1,0:T(8,128)(2,1)S(1)}) custom-call(bf16[3,512,128]{2,1,0:T(8,128)(2,1)S(1)} %get-tuple-element.83.q, bf16[3,1024,128]{2,1,0:T(8,128)(2,1)S(1)} %get-tuple-element.99.k, ...), custom_call_target="tpu_custom_call" | custom-call | flops 1000 | bytes 1000 | tf_op jit(solution)/shard_map/attend_back/pallas_call | solution.py:795
  40.0 3.3 %weight_grad.1 = (bf16[192,2944]{1,0:T(8,128)(2,1)S(1)}, bf16[192,2944]{1,0:T(8,128)(2,1)S(1)}) custom-call(bf16[384,512]{1,0:T(8,128)(2,1)S(1)} %get-tuple-element.91.x_t, bf16[384,512]{1,0:T(8,128)(2,1)S(1)} %get-tuple-element.92.rel_t, bf16[384,384]{1,0:T(8,128)(2,1)S(1)} %get-tuple-element.93.w_pk_t, bf16[384,384]{1,0:T(8,128)(2,1)S(1)} %get-tuple-element.94.w_pq_t, ...), custom_call_target="tpu_custom_call" | custom-call | flops 1000 | bytes 1000 | tf_op jit(solution)/shard_map/weight_grad/pallas_call | solution.py:868
  43.5 2.5 %input_grad.1 = (f32[512,384]{1,0:T(8,128)S(1)}, bf16[256,384]{1,0:T(8,128)(2,1)S(1)}) custom-call(bf16[512,128]{1,0:T(8,128)(2,1)S(1)} %get-tuple-element.105.refs_1_.dq0, bf16[512,128]{1,0:T(8,128)(2,1)S(1)} %get-tuple-element.109.refs_2_.dq1, bf16[512,128]{1,0:T(8,128)(2,1)S(1)} %get-tuple-element.110.refs_3_.dq2, ...), custom_call_target="tpu_custom_call" | custom-call | flops 1000 | bytes 1000 | tf_op jit(solution)/shard_map/input_grad/pallas_call | solution.py:882
  46.0 0.4 collective-permute-done.3
  46.8 1.8 %collective-permute-start.10 = (bf16[96,1408]{1,0:T(8,128)(2,1)S(1)}, bf16[96,1408]{1,0:T(8,128)(2,1)S(1)}, u32[]{:S(2)}, u32[]{:S(2)}) collective-permute-start(bf16[96,1408]{1,0:T(8,128)(2,1)S(1)} %slice.68), channel_id=1, source_target_pairs={{0,2},{1,3},{2,0},{3,1},{4,6},{5,7},{6,4},{7,5},{8,10},{9,11},{10,... | collective-permute-start | bytes 811016 | tf_op jit(solution)/shard_map/ppermute | solution.py:73
  48.6 1.6 %collective-permute-start.4 = (bf16[192,768]{1,0:T(8,128)(2,1)S(1)}, bf16[192,768]{1,0:T(8,128)(2,1)S(1)}, u32[]{:S(2)}, u32[]{:S(2)}) collective-permute-start(bf16[192,768]{1,0:T(8,128)(2,1)S(1)} %slice.60), channel_id=1, source_target_pairs={{0,16},{16,0},{1,17},{17,1},{2,18},{18,2},{3,19},{19,3},{4,20},{20... | collective-permute-start | bytes 884744 | tf_op jit(solution)/shard_map/ppermute | solution.py:73
  50.2 1.6 %collective-permute-start.7 = (bf16[48,3072]{1,0:T(8,128)(2,1)S(1)}, bf16[48,3072]{1,0:T(8,128)(2,1)S(1)}, u32[]{:S(2)}, u32[]{:S(2)}) collective-permute-start(bf16[48,3072]{1,0:T(8,128)(2,1)S(1)} %slice.64), channel_id=1, source_target_pairs={{0,4},{1,5},{2,6},{3,7},{4,0},{5,1},{6,2},{7,3},{8,12},{9,13},{10,... | collective-permute-start | bytes 884744 | tf_op jit(solution)/shard_map/ppermute | solution.py:73
  51.8 3.4 %collective-permute-done.10 = bf16[96,1408]{1,0:T(8,128)(2,1)S(1)} collective-permute-done((bf16[96,1408]{1,0:T(8,128)(2,1)S(1)}, bf16[96,1408]{1,0:T(8,128)(2,1)S(1)}, u32[]{:S(2)}, u32[]{:S(2)}) %collective-permute-start.10) | collective-permute-done | bytes 270368 | tf_op jit(solution)/shard_map/ppermute | solution.py:73
  55.2 1.6 %collective-permute-start.11 = (bf16[48,1408]{1,0:T(8,128)(2,1)S(1)}, bf16[48,1408]{1,0:T(8,128)(2,1)S(1)}, u32[]{:S(2)}, u32[]{:S(2)}) collective-permute-start(bf16[48,1408]{1,0:T(8,128)(2,1)S(1)} %slice.80), channel_id=1, source_target_pairs={{0,4},{1,5},{2,6},{3,7},{4,0},{5,1},{6,2},{7,3},{8,12},{9,13},{10,... | collective-permute-start | bytes 405512 | tf_op jit(solution)/shard_map/ppermute | solution.py:73
  57.1 1.4 %collective-permute-start.5 = (bf16[96,768]{1,0:T(8,128)(2,1)S(1)}, bf16[96,768]{1,0:T(8,128)(2,1)S(1)}, u32[]{:S(2)}, u32[]{:S(2)}) collective-permute-start(bf16[96,768]{1,0:T(8,128)(2,1)S(1)} %slice.76), channel_id=1, source_target_pairs={{0,2},{1,3},{2,0},{3,1},{4,6},{5,7},{6,4},{7,5},{8,10},{9,11},{10,... | collective-permute-start | bytes 442376 | tf_op jit(solution)/shard_map/ppermute | solution.py:73
  58.5 1.0 %collective-permute-done.7 = bf16[48,3072]{1,0:T(8,128)(2,1)S(1)} collective-permute-done((bf16[48,3072]{1,0:T(8,128)(2,1)S(1)}, bf16[48,3072]{1,0:T(8,128)(2,1)S(1)}, u32[]{:S(2)}, u32[]{:S(2)}) %collective-permute-start.7) | collective-permute-done | bytes 294944 | tf_op jit(solution)/shard_map/ppermute | solution.py:73
  59.5 2.9 %collective-permute-start.8 = (bf16[24,3072]{1,0:T(8,128)(2,1)S(1)}, bf16[24,3072]{1,0:T(8,128)(2,1)S(1)}, u32[]{:S(2)}, u32[]{:S(2)}) collective-permute-start(bf16[24,3072]{1,0:T(8,128)(2,1)S(1)} %slice.78), channel_id=1, source_target_pairs={{0,8},{1,9},{2,10},{3,11},{4,12},{5,13},{6,14},{7,15},{8,0},{9,1},... | collective-permute-start | bytes 442376 | tf_op jit(solution)/shard_map/ppermute | solution.py:73
  62.4 1.7 %collective-permute-start.12 = (bf16[48,768]{1,0:T(8,128)(2,1)S(1)}, bf16[48,768]{1,0:T(8,128)(2,1)S(1)}, u32[]{:S(2)}, u32[]{:S(2)}) collective-permute-start(bf16[48,768]{1,0:T(8,128)(2,1)S(1)} %slice.72), channel_id=1, source_target_pairs={{0,4},{1,5},{2,6},{3,7},{4,0},{5,1},{6,2},{7,3},{8,12},{9,13},{10,... | collective-permute-start | bytes 221192 | tf_op jit(solution)/shard_map/ppermute | solution.py:73
  64.1 1.4 %collective-permute-start.6 = (bf16[256,384]{1,0:T(8,128)(2,1)S(1)}, bf16[256,384]{1,0:T(8,128)(2,1)S(1)}, u32[]{:S(2)}, u32[]{:S(2)}) collective-permute-start(bf16[256,384]{1,0:T(8,128)(2,1)S(1)} %get-tuple-element.133), channel_id=1, source_target_pairs={{0,16},{16,0},{1,17},{17,1},{2,18},{18,2},{3,19},{19,3},{4,20},{20... | collective-permute-start | bytes 589832 | tf_op jit(solution)/shard_map/ppermute | solution.py:73
  65.6 1.3 %collective-permute-done.12 = bf16[48,768]{1,0:T(8,128)(2,1)S(1)} collective-permute-done((bf16[48,768]{1,0:T(8,128)(2,1)S(1)}, bf16[48,768]{1,0:T(8,128)(2,1)S(1)}, u32[]{:S(2)}, u32[]{:S(2)}) %collective-permute-start.12) | collective-permute-done | bytes 73760 | tf_op jit(solution)/shard_map/ppermute | solution.py:73
  66.9 3.0 %collective-permute-start.13 = (bf16[24,2176]{1,0:T(8,128)(2,1)S(1)}, bf16[24,2176]{1,0:T(8,128)(2,1)S(1)}, u32[]{:S(2)}, u32[]{:S(2)}) collective-permute-start(bf16[24,2176]{1,0:T(8,128)(2,1)S(1)} %pad_maximum_fusion), channel_id=1, source_target_pairs={{0,8},{1,9},{2,10},{3,11},{4,12},{5,13},{6,14},{7,15},{8,0},{9,1},... | collective-permute-start | bytes 313352 | tf_op jit(solution)/shard_map/ppermute | solution.py:73
  69.9 1.3 %collective-permute-start.9 = (bf16[24,3072]{1,0:T(8,128)(2,1)S(1)}, bf16[24,3072]{1,0:T(8,128)(2,1)S(1)}, u32[]{:S(2)}, u32[]{:S(2)}) collective-permute-start(bf16[24,3072]{1,0:T(8,128)(2,1)S(1)} %slice_add_fusion.4.refs_0_), channel_id=1, source_target_pairs={{0,16},{16,0},{1,17},{17,1},{2,18},{18,2},{3,19},{19,3},{4,20},{20... | collective-permute-start | bytes 442376 | tf_op jit(solution)/shard_map/ppermute | solution.py:73
  71.2 1.4 %collective-permute-done.13 = bf16[24,2176]{1,0:T(8,128)(2,1)S(1)} collective-permute-done((bf16[24,2176]{1,0:T(8,128)(2,1)S(1)}, bf16[24,2176]{1,0:T(8,128)(2,1)S(1)}, u32[]{:S(2)}, u32[]{:S(2)}) %collective-permute-start.13) | collective-permute-done | bytes 104480 | tf_op jit(solution)/shard_map/ppermute | solution.py:73
  72.6 3.3 %collective-permute-start.14 = (bf16[24,2176]{1,0:T(8,128)(2,1)S(1)}, bf16[24,2176]{1,0:T(8,128)(2,1)S(1)}, u32[]{:S(2)}, u32[]{:S(2)}) collective-permute-start(bf16[24,2176]{1,0:T(8,128)(2,1)S(1)} %fusion.2.refs_2_), channel_id=1, source_target_pairs={{0,16},{16,0},{1,17},{17,1},{2,18},{18,2},{3,19},{19,3},{4,20},{20... | collective-permute-start | bytes 313352 | tf_op jit(solution)/shard_map/ppermute | solution.py:73
  75.9 0.8 %fusion = bf16[1,512,384]{2,1,0:T(8,128)(2,1)} fusion(f32[512,384]{1,0:T(8,128)S(1)} %get-tuple-element.127, f32[256,384]{1,0:T(8,128)S(1)} %convert_element_type.6, pred[]{:T(512)S(6)} %eq.3), kind=kLoop, calls=%fused_computation.2 | loop fusion | flops 589824 | bytes 1572865 | tf_op jit(solution)/shard_map/reshape | solution.py:944
  76.8 1.8 %collective-permute-done.14.refs_3_ = bf16[24,2176]{1,0:T(8,128)(2,1)S(1)} collective-permute-done((bf16[24,2176]{1,0:T(8,128)(2,1)S(1)}, bf16[24,2176]{1,0:T(8,128)(2,1)S(1)}, u32[]{:S(2)}, u32[]{:S(2)}) %collective-permute-start.14) | collective-permute-done | bytes 104480 | tf_op jit(solution)/shard_map/ppermute | solution.py:73
  78.6 0.8 %final.1 = (f32[24,384]{1,0:T(8,128)}, f32[24,384]{1,0:T(8,128)}, f32[24,384]{1,0:T(8,128)}, f32[24,384]{1,0:T(8,128)}, f32[24,512]{1,0:T(8,128)}, /*index=5*/f3...) custom-call(bf16[24,3072]{1,0:T(8,128)(2,1)S(1)} %slice_add_fusion.4, ...), custom_call_target="tpu_custom_call" | custom-call | tf_op jit(solution)/shard_map/final/pallas_call | solution.py:921
  (58 shorter events, 1.3 us)
Async XLA Ops:
  1.6 7.9 %collective-permute-start = (bf16[256,384]{1,0:T(8,128)(2,1)S(1)}, bf16[256,384]{1,0:T(8,128)(2,1)S(1)}, u32[]{:S(2)}, u32[]{:S(2)}) collective-permute-start(bf16[256,384]{1,0:T(8,128)(2,1)S(1)} %dynamic-slice_bitcast_fusion), channel_id=1, source_target_pairs={{0,16},{16,0},{1,17},{17,1},{2,18},{18,2},{3,19},{19,3},{4,20},{20... | collective-permute-start | bytes 589832 | tf_op jit(solution)/shard_map/ppermute | solution.py:73
  4.6 4.9 %copy-start.1 = (bf16[384,384]{1,0:T(8,128)(2,1)S(1)}, bf16[384,384]{1,0:T(8,128)(2,1)}, u32[]{:S(2)}) copy-start(bf16[384,384]{1,0:T(8,128)(2,1)} %w_key.3) | copy-start | bytes 884740
  4.6 4.9 %copy-start.2 = (bf16[384,384]{1,0:T(8,128)(2,1)S(1)}, bf16[384,384]{1,0:T(8,128)(2,1)}, u32[]{:S(2)}) copy-start(bf16[384,384]{1,0:T(8,128)(2,1)} %w_value.3) | copy-start | bytes 884740
  4.6 4.9 %copy-start.8 = (bf16[4,384]{1,0:T(4,128)(2,1)S(1)}, bf16[4,384]{1,0:T(4,128)(2,1)}, u32[]{:S(2)}) copy-start(bf16[4,384]{1,0:T(4,128)(2,1)} %biases.3) | copy-start | bytes 9220
  4.6 13.7 %copy-start.6 = (bf16[1,512,384]{2,1,0:T(8,128)(2,1)S(1)}, bf16[1,512,384]{2,1,0:T(8,128)(2,1)}, u32[]{:S(2)}) copy-start(bf16[1,512,384]{2,1,0:T(8,128)(2,1)} %param.19) | copy-start | bytes 1179652
  4.6 13.7 %copy-start.7 = (bf16[384,384]{1,0:T(8,128)(2,1)S(1)}, bf16[384,384]{1,0:T(8,128)(2,1)}, u32[]{:S(2)}) copy-start(bf16[384,384]{1,0:T(8,128)(2,1)} %w_output.1) | copy-start | bytes 884740
  4.7 13.7 %copy-start.12 = (bf16[2,384]{1,0:T(2,128)(2,1)S(1)}, bf16[2,384]{1,0:T(2,128)(2,1)}, u32[]{:S(2)}) copy-start(bf16[2,384]{1,0:T(2,128)(2,1)} %shifts.1) | copy-start | bytes 4612
  9.6 8.8 %copy-start.3 = (bf16[1,512,384]{2,1,0:T(8,128)(2,1)S(1)}, bf16[1,512,384]{2,1,0:T(8,128)(2,1)}, u32[]{:S(2)}) copy-start(bf16[1,512,384]{2,1,0:T(8,128)(2,1)} %param.18) | copy-start | bytes 1179652
  9.6 8.8 %copy-start.4 = (bf16[384,1536]{1,0:T(8,128)(2,1)S(1)}, bf16[384,1536]{1,0:T(8,128)(2,1)}, u32[]{:S(2)}) copy-start(bf16[384,1536]{1,0:T(8,128)(2,1)} %w_inner.1) | copy-start | bytes 3538948
  9.6 8.8 %copy-start.5 = (bf16[1536,384]{1,0:T(8,128)(2,1)S(1)}, bf16[1536,384]{1,0:T(8,128)(2,1)}, u32[]{:S(2)}) copy-start(bf16[1536,384]{1,0:T(8,128)(2,1)} %w_outer.1) | copy-start | bytes 3538948
  9.6 8.8 %copy-start.9 = (bf16[1536]{0:T(1024)(128)(2,1)S(1)}, bf16[1536]{0:T(1024)(128)(2,1)}, u32[]{:S(2)}) copy-start(bf16[1536]{0:T(1024)(128)(2,1)} %inner_bias.1) | copy-start | bytes 9220
  9.6 8.8 %copy-start.10 = (s32[1,512]{1,0:T(1,128)S(1)}, s32[1,512]{1,0:T(1,128)}, u32[]{:S(2)}) copy-start(s32[1,512]{1,0:T(1,128)} %mask.1) | copy-start | bytes 6148
  9.6 8.8 %copy-start.11 = (bf16[2,384]{1,0:T(2,128)(2,1)S(1)}, bf16[2,384]{1,0:T(2,128)(2,1)}, u32[]{:S(2)}) copy-start(bf16[2,384]{1,0:T(2,128)(2,1)} %gains.1) | copy-start | bytes 4612
  9.6 8.8 %copy-start.13 = (bf16[384]{0:T(512)(128)(2,1)S(1)}, bf16[384]{0:T(512)(128)(2,1)}, u32[]{:S(2)}) copy-start(bf16[384]{0:T(512)(128)(2,1)} %outer_bias.1) | copy-start | bytes 2308
  26.4 13.5 %copy-start = (f32[512,384]{1,0:T(8,128)}, f32[512,384]{1,0:T(8,128)S(1)}, u32[]{:S(2)}) copy-start(f32[512,384]{1,0:T(8,128)S(1)} %get-tuple-element.125.d_first) | copy-start | bytes 2359300
  26.4 3.7 %collective-permute-start.1 = (bf16[192,3072]{1,0:T(8,128)(2,1)S(1)}, bf16[192,3072]{1,0:T(8,128)(2,1)S(1)}, u32[]{:S(2)}, u32[]{:S(2)}) collective-permute-start(bf16[192,3072]{1,0:T(8,128)(2,1)S(1)} %get-tuple-element.107), channel_id=1, source_target_pairs={{0,1},{1,0},{2,3},{3,2},{4,5},{5,4},{6,7},{7,6},{8,9},{9,8},{10,11... | collective-permute-start | bytes 3538952 | tf_op jit(solution)/shard_map/ppermute | solution.py:73
  30.6 15.8 %collective-permute-start.3 = (bf16[96,3072]{1,0:T(8,128)(2,1)S(1)}, bf16[96,3072]{1,0:T(8,128)(2,1)S(1)}, u32[]{:S(2)}, u32[]{:S(2)}) collective-permute-start(bf16[96,3072]{1,0:T(8,128)(2,1)S(1)} %slice.58), channel_id=1, source_target_pairs={{0,2},{1,3},{2,0},{3,1},{4,6},{5,7},{6,4},{7,5},{8,10},{9,11},{10,... | collective-permute-start | bytes 1769480 | tf_op jit(solution)/shard_map/ppermute | solution.py:73
  43.2 3.3 %collective-permute-start.2 = (bf16[192,2944]{1,0:T(8,128)(2,1)S(1)}, bf16[192,2944]{1,0:T(8,128)(2,1)S(1)}, u32[]{:S(2)}, u32[]{:S(2)}) collective-permute-start(bf16[192,2944]{1,0:T(8,128)(2,1)S(1)} %get-tuple-element.129), channel_id=1, source_target_pairs={{0,1},{1,0},{2,3},{3,2},{4,5},{5,4},{6,7},{7,6},{8,9},{9,8},{10,11... | collective-permute-start | bytes 3391496 | tf_op jit(solution)/shard_map/ppermute | solution.py:73
  46.8 8.4 %collective-permute-start.10 = (bf16[96,1408]{1,0:T(8,128)(2,1)S(1)}, bf16[96,1408]{1,0:T(8,128)(2,1)S(1)}, u32[]{:S(2)}, u32[]{:S(2)}) collective-permute-start(bf16[96,1408]{1,0:T(8,128)(2,1)S(1)} %slice.68), channel_id=1, source_target_pairs={{0,2},{1,3},{2,0},{3,1},{4,6},{5,7},{6,4},{7,5},{8,10},{9,11},{10,... | collective-permute-start | bytes 811016 | tf_op jit(solution)/shard_map/ppermute | solution.py:73
  48.6 8.4 %collective-permute-start.4 = (bf16[192,768]{1,0:T(8,128)(2,1)S(1)}, bf16[192,768]{1,0:T(8,128)(2,1)S(1)}, u32[]{:S(2)}, u32[]{:S(2)}) collective-permute-start(bf16[192,768]{1,0:T(8,128)(2,1)S(1)} %slice.60), channel_id=1, source_target_pairs={{0,16},{16,0},{1,17},{17,1},{2,18},{18,2},{3,19},{19,3},{4,20},{20... | collective-permute-start | bytes 884744 | tf_op jit(solution)/shard_map/ppermute | solution.py:73
  50.2 9.3 %collective-permute-start.7 = (bf16[48,3072]{1,0:T(8,128)(2,1)S(1)}, bf16[48,3072]{1,0:T(8,128)(2,1)S(1)}, u32[]{:S(2)}, u32[]{:S(2)}) collective-permute-start(bf16[48,3072]{1,0:T(8,128)(2,1)S(1)} %slice.64), channel_id=1, source_target_pairs={{0,4},{1,5},{2,6},{3,7},{4,0},{5,1},{6,2},{7,3},{8,12},{9,13},{10,... | collective-permute-start | bytes 884744 | tf_op jit(solution)/shard_map/ppermute | solution.py:73
  55.2 8.9 %collective-permute-start.11 = (bf16[48,1408]{1,0:T(8,128)(2,1)S(1)}, bf16[48,1408]{1,0:T(8,128)(2,1)S(1)}, u32[]{:S(2)}, u32[]{:S(2)}) collective-permute-start(bf16[48,1408]{1,0:T(8,128)(2,1)S(1)} %slice.80), channel_id=1, source_target_pairs={{0,4},{1,5},{2,6},{3,7},{4,0},{5,1},{6,2},{7,3},{8,12},{9,13},{10,... | collective-permute-start | bytes 405512 | tf_op jit(solution)/shard_map/ppermute | solution.py:73
  57.1 5.3 %collective-permute-start.5 = (bf16[96,768]{1,0:T(8,128)(2,1)S(1)}, bf16[96,768]{1,0:T(8,128)(2,1)S(1)}, u32[]{:S(2)}, u32[]{:S(2)}) collective-permute-start(bf16[96,768]{1,0:T(8,128)(2,1)S(1)} %slice.76), channel_id=1, source_target_pairs={{0,2},{1,3},{2,0},{3,1},{4,6},{5,7},{6,4},{7,5},{8,10},{9,11},{10,... | collective-permute-start | bytes 442376 | tf_op jit(solution)/shard_map/ppermute | solution.py:73
  59.5 10.4 %collective-permute-start.8 = (bf16[24,3072]{1,0:T(8,128)(2,1)S(1)}, bf16[24,3072]{1,0:T(8,128)(2,1)S(1)}, u32[]{:S(2)}, u32[]{:S(2)}) collective-permute-start(bf16[24,3072]{1,0:T(8,128)(2,1)S(1)} %slice.78), channel_id=1, source_target_pairs={{0,8},{1,9},{2,10},{3,11},{4,12},{5,13},{6,14},{7,15},{8,0},{9,1},... | collective-permute-start | bytes 442376 | tf_op jit(solution)/shard_map/ppermute | solution.py:73
  62.4 4.4 %collective-permute-start.12 = (bf16[48,768]{1,0:T(8,128)(2,1)S(1)}, bf16[48,768]{1,0:T(8,128)(2,1)S(1)}, u32[]{:S(2)}, u32[]{:S(2)}) collective-permute-start(bf16[48,768]{1,0:T(8,128)(2,1)S(1)} %slice.72), channel_id=1, source_target_pairs={{0,4},{1,5},{2,6},{3,7},{4,0},{5,1},{6,2},{7,3},{8,12},{9,13},{10,... | collective-permute-start | bytes 221192 | tf_op jit(solution)/shard_map/ppermute | solution.py:73
  64.1 11.7 %collective-permute-start.6 = (bf16[256,384]{1,0:T(8,128)(2,1)S(1)}, bf16[256,384]{1,0:T(8,128)(2,1)S(1)}, u32[]{:S(2)}, u32[]{:S(2)}) collective-permute-start(bf16[256,384]{1,0:T(8,128)(2,1)S(1)} %get-tuple-element.133), channel_id=1, source_target_pairs={{0,16},{16,0},{1,17},{17,1},{2,18},{18,2},{3,19},{19,3},{4,20},{20... | collective-permute-start | bytes 589832 | tf_op jit(solution)/shard_map/ppermute | solution.py:73
  66.9 5.6 %collective-permute-start.13 = (bf16[24,2176]{1,0:T(8,128)(2,1)S(1)}, bf16[24,2176]{1,0:T(8,128)(2,1)S(1)}, u32[]{:S(2)}, u32[]{:S(2)}) collective-permute-start(bf16[24,2176]{1,0:T(8,128)(2,1)S(1)} %pad_maximum_fusion), channel_id=1, source_target_pairs={{0,8},{1,9},{2,10},{3,11},{4,12},{5,13},{6,14},{7,15},{8,0},{9,1},... | collective-permute-start | bytes 313352 | tf_op jit(solution)/shard_map/ppermute | solution.py:73
  69.9 6.8 %collective-permute-start.9 = (bf16[24,3072]{1,0:T(8,128)(2,1)S(1)}, bf16[24,3072]{1,0:T(8,128)(2,1)S(1)}, u32[]{:S(2)}, u32[]{:S(2)}) collective-permute-start(bf16[24,3072]{1,0:T(8,128)(2,1)S(1)} %slice_add_fusion.4.refs_0_), channel_id=1, source_target_pairs={{0,16},{16,0},{1,17},{17,1},{2,18},{18,2},{3,19},{19,3},{4,20},{20... | collective-permute-start | bytes 442376 | tf_op jit(solution)/shard_map/ppermute | solution.py:73
  72.6 6.0 %collective-permute-start.14 = (bf16[24,2176]{1,0:T(8,128)(2,1)S(1)}, bf16[24,2176]{1,0:T(8,128)(2,1)S(1)}, u32[]{:S(2)}, u32[]{:S(2)}) collective-permute-start(bf16[24,2176]{1,0:T(8,128)(2,1)S(1)} %fusion.2.refs_2_), channel_id=1, source_target_pairs={{0,16},{16,0},{1,17},{17,1},{2,18},{18,2},{3,19},{19,3},{4,20},{20... | collective-permute-start | bytes 313352 | tf_op jit(solution)/shard_map/ppermute | solution.py:73

commit v3 on v2

--- a/solution.py
+++ b/solution.py
@@ -121,66 +121,38 @@
 
 
 def attend_kernel(q, k_own, v_own, pk_rev, pq_rev, w_key, w_value, biases, *refs, scale, n_seq):
-    edges, refs = refs[:-6], refs[-6:]
-
-    def one_pair(p, carry):
-        attend_pair(
-            p, q, k_own, v_own, pk_rev, pq_rev, w_key, w_value, biases, edges, *refs, scale, n_seq
-        )
-        return carry
-
-    lax.fori_loop(0, PAIRS, one_pair, 0)
-
-
-def attend_pair(
-    p,
-    q,
-    k_own,
-    v_own,
-    pk_rev,
-    pq_rev,
-    w_key,
-    w_value,
-    biases,
-    edges,
-    context,
-    probs,
-    k,
-    v,
-    from_scr,
-    score_scr,
-    scale,
-    n_seq,
-):
+    edges, (context, probs, k, v, from_scr, score_scr) = refs[:-6], refs[-6:]
     me_seq = lax.axis_index("seq")
-    cols = pl.ds(pl.multiple_of(p * TILE, TILE), TILE)
     span, block = edges[0].shape[0], k_own.shape[1]
-    k[p, span : span + block, :] = k_own[p]
-    v[p, span : span + block, :] = v_own[p]
-    bias = biases[1:2, cols].astype(f32)
-    both = jnp.concatenate([w_key[:, cols], w_value[:, cols]], axis=1)
-    sides = ((0, span + block),) if len(edges) == 1 else ((0,), (span + block,))
-    for firsts, source in zip(sides, edges):
-        product = nn(source[...], both)
-        for first in firsts:
-            k[p, first : first + span, :] = product[:, :TILE].astype(bf16)
-            v[p, first : first + span, :] = (product[:, TILE:] + bias).astype(bf16)
     row, lane = iota((TILE, TILE), 0), iota((TILE, TILE), 1)
     eye = jnp.where(row == lane, 1.0, 0.0).astype(bf16)
     halves = (lane < TILE // 2, lane >= TILE // 2)
     tiles = q.shape[1] // TILE
     blocks = pk_rev.shape[1] // TILE + 1
     side = blocks // 2
-    tables = []
-    for h in range(2):
+    bias = biases[1:2, :].astype(f32)
+    sides = ((0, span + block),) if len(edges) == 1 else ((0,), (span + block,))
+    for firsts, source in zip(sides, edges):
+        new_keys = nn(source[...], w_key[...]).astype(bf16)
+        new_values = (nn(source[...], w_value[...]) + bias).astype(bf16)
+        for p in range(PAIRS):
+            for first in firsts:
+                k[p, first : first + span, :] = new_keys[:, p * TILE : (p + 1) * TILE]
+                v[p, first : first + span, :] = new_values[:, p * TILE : (p + 1) * TILE]
+    for p in range(PAIRS):
+        k[p, span : span + block, :] = k_own[p]
+        v[p, span : span + block, :] = v_own[p]
+
+    def masked_tables(p):
         table = pq_rev[p].astype(f32)
-        half = iota((table.shape[0], TILE), 1) // (TILE // 2) == h
-        tables.append(jnp.where(half, table, 0.0).astype(bf16))
-    for wb in range(tiles + blocks - 1):
+        half = iota((table.shape[0], TILE), 1) // (TILE // 2)
+        return [jnp.where(half == h, table, 0.0).astype(bf16) for h in range(2)]
+
+    def from_terms(p, slot, tables, wb):
         low, high, first, last = key_block_range(wb, blocks, tiles)
         kb = k[p, wb * TILE : (wb + 1) * TILE, :]
-        span = slice(first * TILE, (last + 1) * TILE)
-        product = nt(kb, jnp.concatenate([tables[0][span], tables[1][span]], axis=0))
+        rows = slice(first * TILE, (last + 1) * TILE)
+        product = nt(kb, jnp.concatenate([tables[0][rows], tables[1][rows]], axis=0))
         for h in range(2):
             turned = {}
             for a in range(first, last + 1):
@@ -194,60 +166,78 @@
                 else:
                     term = jnp.where(lane >= row, turned[e], turned[e - 1])
                 it, b = wb - (blocks - 1) + e, blocks - 1 - e
-                from_scr[h, it, b * TILE : (b + 1) * TILE, :] = term.astype(bf16)
+                from_scr[slot, h, it, b * TILE : (b + 1) * TILE, :] = term.astype(bf16)
+
     before = jnp.where(me_seq == 0, masked_score, 0.0)
     after = jnp.where(me_seq == n_seq - 1, masked_score, 0.0)
     rate = scale * math.log2(math.e)
-    chains = [(it, h) for it in range(tiles) for h in range(2)]
-    stacked = jnp.concatenate(
-        [where_bf16(halves[h], q[p, it * TILE : (it + 1) * TILE, :]) for it, h in chains], axis=0
-    )
-    product = nt(stacked, pk_rev[p])
-    tops = []
-    for n, (it, h) in enumerate(chains):
-        rows = slice(n * TILE, (n + 1) * TILE)
-        turned = [
-            skew(product[rows, b * TILE : (b + 1) * TILE], 1) for b in range(blocks - 1)
-        ]
-        left = jnp.concatenate([stacked[rows], eye], axis=1)
-        right = jnp.concatenate(
-            [k[p, it * TILE : (it + blocks) * TILE, :], from_scr[h, it]], axis=1
+    keys = tiles + blocks - 1
+    tables = masked_tables(0)
+    for wb in range(keys):
+        from_terms(0, 0, tables, wb)
+
+    def one_pair(p, carry):
+        attend_pair(p, p % 2)
+        return carry
+
+    def attend_pair(p, slot):
+        cols = pl.ds(pl.multiple_of(p * TILE, TILE), TILE)
+        following = jnp.minimum(p + 1, PAIRS - 1)
+        tables = masked_tables(following)
+        chains = [(it, h) for it in range(tiles) for h in range(2)]
+        stacked = jnp.concatenate(
+            [where_bf16(halves[h], q[p, it * TILE : (it + 1) * TILE, :]) for it, h in chains], axis=0
         )
-        content = nt(left, right)
-        largest = None
-        for b in range(blocks):
-            score = content[:, b * TILE : (b + 1) * TILE]
-            if b == 0:
-                score = jnp.where(lane > row, score + turned[0], masked_score)
-            elif b == blocks - 1:
-                score = jnp.where(lane <= row, score + turned[b - 1], masked_score)
-            else:
-                score = score + jnp.where(lane > row, turned[b], turned[b - 1])
-            if it + b < side:
-                score = score + before
-            if it + b >= side + tiles:
-                score = score + after
-            score_scr[n, :, b * TILE : (b + 1) * TILE] = score
-            largest = score if largest is None else jnp.maximum(largest, score)
-        tops.append(largest)
-    tops = [jnp.max(top, axis=1, keepdims=True) for top in tops]
-    totals = []
-    for n in range(len(chains)):
-        weight = jnp.exp2((score_scr[n] - tops[n]) * rate)
-        score_scr[n] = weight
-        total = weight[:, :TILE]
-        for b in range(1, blocks):
-            total = total + weight[:, b * TILE : (b + 1) * TILE]
-        totals.append(total)
-    inverses = [1.0 / jnp.sum(total, axis=1, keepdims=True) for total in totals]
-    for n, (it, h) in enumerate(chains):
-        probs[p, h, it] = (score_scr[n] * inverses[n]).astype(bf16)
-    for it in range(tiles):
-        both = jnp.concatenate([probs[p, 0, it], probs[p, 1, it]], axis=0)
-        part = nn(both, v[p, it * TILE : (it + blocks) * TILE, :])
-        context[it * TILE : (it + 1) * TILE, cols] = jnp.where(
-            halves[0], part[:TILE], part[TILE:]
-        ).astype(bf16)
+        product = nt(stacked, pk_rev[p])
+        tops = []
+        for n, (it, h) in enumerate(chains):
+            rows = slice(n * TILE, (n + 1) * TILE)
+            turned = [
+                skew(product[rows, b * TILE : (b + 1) * TILE], 1) for b in range(blocks - 1)
+            ]
+            left = jnp.concatenate([stacked[rows], eye], axis=1)
+            right = jnp.concatenate(
+                [k[p, it * TILE : (it + blocks) * TILE, :], from_scr[slot, h, it]], axis=1
+            )
+            content = nt(left, right)
+            largest = None
+            for b in range(blocks):
+                score = content[:, b * TILE : (b + 1) * TILE]
+                if b == 0:
+                    score = jnp.where(lane > row, score + turned[0], masked_score)
+                elif b == blocks - 1:
+                    score = jnp.where(lane <= row, score + turned[b - 1], masked_score)
+                else:
+                    score = score + jnp.where(lane > row, turned[b], turned[b - 1])
+                if it + b < side:
+                    score = score + before
+                if it + b >= side + tiles:
+                    score = score + after
+                score_scr[n, :, b * TILE : (b + 1) * TILE] = score
+                largest = score if largest is None else jnp.maximum(largest, score)
+            tops.append(largest)
+        tops = [jnp.max(top, axis=1, keepdims=True) for top in tops]
+        totals = []
+        for n in range(len(chains)):
+            weight = jnp.exp2((score_scr[n] - tops[n]) * rate)
+            score_scr[n] = weight
+            total = weight[:, :TILE]
+            for b in range(1, blocks):
+                total = total + weight[:, b * TILE : (b + 1) * TILE]
+            totals.append(total)
+            for wb in range(n * keys // len(chains), (n + 1) * keys // len(chains)):
+                from_terms(following, 1 - slot, tables, wb)
+        inverses = [1.0 / jnp.sum(total, axis=1, keepdims=True) for total in totals]
+        for n, (it, h) in enumerate(chains):
+            probs[p, h, it] = (score_scr[n] * inverses[n]).astype(bf16)
+        for it in range(tiles):
+            both = jnp.concatenate([probs[p, 0, it], probs[p, 1, it]], axis=0)
+            part = nn(both, v[p, it * TILE : (it + blocks) * TILE, :])
+            context[it * TILE : (it + 1) * TILE, cols] = jnp.where(
+                halves[0], part[:TILE], part[TILE:]
+            ).astype(bf16)
+
+    lax.fori_loop(0, PAIRS, one_pair, 0)
 
 
 def attend_back_kernel(
@@ -747,7 +737,7 @@
             shape((PAIRS, window, TILE), bf16),
         ),
         scratch_shapes=[
-            pltpu.VMEM((2, tiles, blocks * TILE, TILE), bf16),
+            pltpu.VMEM((2, 2, tiles, blocks * TILE, TILE), bf16),
             pltpu.VMEM((2 * tiles, TILE, blocks * TILE), f32),
         ],
         compiler_params=pltpu.CompilerParams(vmem_limit_bytes=20 * MiB),

time: 79.7 us -> 79.4 us (level)
  no operation moved by 1% of the time
where the time goes in v3:
time: 79.4 us; the launch traced here: 79.2 us
  Pallas kernels  38.7 us (49%)
  starting transfers between devices  26.6 us (34%)
  waiting for transfers between devices  9.82 us (12%)
  other arithmetic  1.8 us (2%)
  local copies, waits for them, and re-layouts  1.17 us (1%)
  between operations  1.13 us (1%)
    ppermute x15, starting transfers between devices, exchange(): return lax.ppermute(value, axis, [(i, i ^ bit) for i in range(count)])  26.6 us
    pallas_call x3, Pallas kernels, back(): pl.pallas_call(partial(attend_back_kernel, scale=scale, p=p), out_shape=(...  11.2 us
    ppermute x15, waiting for transfers between devices, exchange(): return lax.ppermute(value, axis, [(i, i ^ bit) for i in range(count)])  9.82 us
    pallas_call x1, Pallas kernels, local(): pl.pallas_call(partial(attend_kernel, scale=scale, n_seq=n_seq), out_shap...  8.38 us
    pallas_call x1, Pallas kernels, local(): pl.pallas_call(partial(middle_kernel, step=512), out_shape=(shape((tokens...  8.05 us
    pallas_call x1, Pallas kernels, local(): pl.pallas_call(project_kernel, out_shape=(shape((PAIRS, block, TILE), bf1...  4.52 us
    pallas_call x1, Pallas kernels, local(): pl.pallas_call(partial(weight_grad_kernel, n_seq=n_seq, share=share), out...  3.25 us
    pallas_call x1, Pallas kernels, local(): pl.pallas_call(input_grad_kernel, out_shape=(shape((tokens, width), f32),...  2.53 us
  transfers between devices with their start and end apart: 15, of which 8 were waited for; matrix products, arithmetic and copies ran while one was open for 2% of the time, Pallas kernels for 27%

profile of v3, /device:TPU:0, one launch (start us, length us, event | category | flops | bytes accessed | tf_op | source)
XLA Modules:
  0.0 79.2 jit_solution(4046123442837966129)
XLA Ops:
  0.7 1.0 %dynamic-slice_bitcast_fusion = bf16[256,384]{1,0:T(8,128)(2,1)S(1)} fusion(bf16[1,512,384]{2,1,0:T(8,128)(2,1)} %param.18, s32[]{:T(128)S(6)} %select_n.11), kind=kLoop, calls=%fused_computation.8 | loop fusion | bytes 393220 | tf_op jit(solution)/shard_map/dynamic_slice | solution.py:687
  1.6 3.0 %collective-permute-start = (bf16[256,384]{1,0:T(8,128)(2,1)S(1)}, bf16[256,384]{1,0:T(8,128)(2,1)S(1)}, u32[]{:S(2)}, u32[]{:S(2)}) collective-permute-start(bf16[256,384]{1,0:T(8,128)(2,1)S(1)} %dynamic-slice_bitcast_fusion), channel_id=1, source_target_pairs={{0,16},{16,0},{1,17},{17,1},{2,18},{18,2},{3,19},{19,3},{4,20},{20... | collective-permute-start | bytes 589832 | tf_op jit(solution)/shard_map/ppermute | solution.py:73
  4.7 4.5 %project.1 = (bf16[3,512,128]{2,1,0:T(8,128)(2,1)S(1)}, bf16[3,512,128]{2,1,0:T(8,128)(2,1)S(1)}, bf16[3,512,128]{2,1,0:T(8,128)(2,1)S(1)}, bf16[3,512,128]{2,1,...) custom-call(s32[384,4]{1,0:T(8,128)} %constant.19.clone.refs_0_, ...), custom_call_target="tpu_custom_call" | custom-call | tf_op jit(solution)/shard_map/project/pallas_call | solution.py:709
  9.2 0.3 collective-permute-done.refs_0_
  9.6 8.4 %attend.1 = (bf16[512,384]{1,0:T(8,128)(2,1)S(1)}, bf16[3,2,4,128,640]{4,3,2,1,0:T(8,128)(2,1)S(1)}, bf16[3,1024,128]{2,1,0:T(8,128)(2,1)S(1)}, bf16[3,1024,128]{2,1,0:T(8,128)(2,1)S(1)}) custom-call(bf16[3,512,128]{2,1,0:T(8,128)(2,1)S(1)} %get-tuple-element.83.q, bf16[3,512,128]{2,1,0:T(8,128)(2,1)S(1)} %get-tuple-element.84.k_own, ...), custom_call_target="tpu_custom_call" | custom-call | tf_op jit(solution)/shard_map/attend/pallas_call | solution.py:731
  18.1 8.1 %middle.1 = (bf16[512,384]{1,0:T(8,128)(2,1)}, f32[512,384]{1,0:T(8,128)S(1)}, bf16[512,384]{1,0:T(8,128)(2,1)S(1)}, bf16[192,3072]{1,0:T(8,128)(2,1)S(1)}, bf16...) custom-call(bf16[512,384]{1,0:T(8,128)(2,1)S(1)} %bitcast.12, ...), custom_call_target="tpu_custom_call" | custom-call | tf_op jit(solution)/shard_map/middle/pallas_call | solution.py:748
  26.2 3.6 %attend_back.3 = (bf16[512,128]{1,0:T(8,128)(2,1)S(1)}, bf16[1024,128]{1,0:T(8,128)(2,1)S(1)}, bf16[1024,128]{1,0:T(8,128)(2,1)S(1)}, bf16[128,512]{1,0:T(8,128)(2,1)S(1)}, bf16[128,512]{1,0:T(8,128)(2,1)S(1)}) custom-call(bf16[3,512,128]{2,1,0:T(8,128)(2,1)S(1)} %get-tuple-element.83.q, bf16[3,1024,128]{2,1,0:T(8,128)(2,1)S(1)} %get-tuple-element.99.k, ...), custom_call_target="tpu_custom_call" | custom-call | flops 1000 | bytes 1000 | tf_op jit(solution)/shard_map/attend_back/pallas_call | solution.py:785
  29.9 0.4 add.44
  30.3 1.8 %collective-permute-start.3 = (bf16[96,3072]{1,0:T(8,128)(2,1)S(1)}, bf16[96,3072]{1,0:T(8,128)(2,1)S(1)}, u32[]{:S(2)}, u32[]{:S(2)}) collective-permute-start(bf16[96,3072]{1,0:T(8,128)(2,1)S(1)} %slice.58), channel_id=1, source_target_pairs={{0,2},{1,3},{2,0},{3,1},{4,6},{5,7},{6,4},{7,5},{8,10},{9,11},{10,... | collective-permute-start | bytes 1769480 | tf_op jit(solution)/shard_map/ppermute | solution.py:73
  32.1 3.9 %attend_back.5 = (bf16[512,128]{1,0:T(8,128)(2,1)S(1)}, bf16[1024,128]{1,0:T(8,128)(2,1)S(1)}, bf16[1024,128]{1,0:T(8,128)(2,1)S(1)}, bf16[128,512]{1,0:T(8,128)(2,1)S(1)}, bf16[128,512]{1,0:T(8,128)(2,1)S(1)}) custom-call(bf16[3,512,128]{2,1,0:T(8,128)(2,1)S(1)} %get-tuple-element.83.q, bf16[3,1024,128]{2,1,0:T(8,128)(2,1)S(1)} %get-tuple-element.99.k, ...), custom_call_target="tpu_custom_call" | custom-call | flops 1000 | bytes 1000 | tf_op jit(solution)/shard_map/attend_back/pallas_call | solution.py:785
  36.0 3.6 %attend_back.4 = (bf16[512,128]{1,0:T(8,128)(2,1)S(1)}, bf16[1024,128]{1,0:T(8,128)(2,1)S(1)}, bf16[1024,128]{1,0:T(8,128)(2,1)S(1)}, bf16[128,512]{1,0:T(8,128)(2,1)S(1)}, bf16[128,512]{1,0:T(8,128)(2,1)S(1)}) custom-call(bf16[3,512,128]{2,1,0:T(8,128)(2,1)S(1)} %get-tuple-element.83.q, bf16[3,1024,128]{2,1,0:T(8,128)(2,1)S(1)} %get-tuple-element.99.k, ...), custom_call_target="tpu_custom_call" | custom-call | flops 1000 | bytes 1000 | tf_op jit(solution)/shard_map/attend_back/pallas_call | solution.py:785
  39.7 3.3 %weight_grad.1 = (bf16[192,2944]{1,0:T(8,128)(2,1)S(1)}, bf16[192,2944]{1,0:T(8,128)(2,1)S(1)}) custom-call(bf16[384,512]{1,0:T(8,128)(2,1)S(1)} %get-tuple-element.91.x_t, bf16[384,512]{1,0:T(8,128)(2,1)S(1)} %get-tuple-element.92.rel_t, bf16[384,384]{1,0:T(8,128)(2,1)S(1)} %get-tuple-element.93.w_pk_t, bf16[384,384]{1,0:T(8,128)(2,1)S(1)} %get-tuple-element.94.w_pq_t, ...), custom_call_target="tpu_custom_call" | custom-call | flops 1000 | bytes 1000 | tf_op jit(solution)/shard_map/weight_grad/pallas_call | solution.py:858
  43.2 2.5 %input_grad.1 = (f32[512,384]{1,0:T(8,128)S(1)}, bf16[256,384]{1,0:T(8,128)(2,1)S(1)}) custom-call(bf16[512,128]{1,0:T(8,128)(2,1)S(1)} %get-tuple-element.105.refs_1_.dq0, bf16[512,128]{1,0:T(8,128)(2,1)S(1)} %get-tuple-element.109.refs_2_.dq1, bf16[512,128]{1,0:T(8,128)(2,1)S(1)} %get-tuple-element.110.refs_3_.dq2, ...), custom_call_target="tpu_custom_call" | custom-call | flops 1000 | bytes 1000 | tf_op jit(solution)/shard_map/input_grad/pallas_call | solution.py:872
  45.8 0.4 collective-permute-done.3
  46.5 1.8 %collective-permute-start.10 = (bf16[96,1408]{1,0:T(8,128)(2,1)S(1)}, bf16[96,1408]{1,0:T(8,128)(2,1)S(1)}, u32[]{:S(2)}, u32[]{:S(2)}) collective-permute-start(bf16[96,1408]{1,0:T(8,128)(2,1)S(1)} %slice.68), channel_id=1, source_target_pairs={{0,2},{1,3},{2,0},{3,1},{4,6},{5,7},{6,4},{7,5},{8,10},{9,11},{10,... | collective-permute-start | bytes 811016 | tf_op jit(solution)/shard_map/ppermute | solution.py:73
  48.3 1.6 %collective-permute-start.4 = (bf16[192,768]{1,0:T(8,128)(2,1)S(1)}, bf16[192,768]{1,0:T(8,128)(2,1)S(1)}, u32[]{:S(2)}, u32[]{:S(2)}) collective-permute-start(bf16[192,768]{1,0:T(8,128)(2,1)S(1)} %slice.60), channel_id=1, source_target_pairs={{0,16},{16,0},{1,17},{17,1},{2,18},{18,2},{3,19},{19,3},{4,20},{20... | collective-permute-start | bytes 884744 | tf_op jit(solution)/shard_map/ppermute | solution.py:73
  49.9 1.6 %collective-permute-start.7 = (bf16[48,3072]{1,0:T(8,128)(2,1)S(1)}, bf16[48,3072]{1,0:T(8,128)(2,1)S(1)}, u32[]{:S(2)}, u32[]{:S(2)}) collective-permute-start(bf16[48,3072]{1,0:T(8,128)(2,1)S(1)} %slice.64), channel_id=1, source_target_pairs={{0,4},{1,5},{2,6},{3,7},{4,0},{5,1},{6,2},{7,3},{8,12},{9,13},{10,... | collective-permute-start | bytes 884744 | tf_op jit(solution)/shard_map/ppermute | solution.py:73
  51.5 3.4 %collective-permute-done.10 = bf16[96,1408]{1,0:T(8,128)(2,1)S(1)} collective-permute-done((bf16[96,1408]{1,0:T(8,128)(2,1)S(1)}, bf16[96,1408]{1,0:T(8,128)(2,1)S(1)}, u32[]{:S(2)}, u32[]{:S(2)}) %collective-permute-start.10) | collective-permute-done | bytes 270368 | tf_op jit(solution)/shard_map/ppermute | solution.py:73
  54.9 1.7 %collective-permute-start.11 = (bf16[48,1408]{1,0:T(8,128)(2,1)S(1)}, bf16[48,1408]{1,0:T(8,128)(2,1)S(1)}, u32[]{:S(2)}, u32[]{:S(2)}) collective-permute-start(bf16[48,1408]{1,0:T(8,128)(2,1)S(1)} %slice.80), channel_id=1, source_target_pairs={{0,4},{1,5},{2,6},{3,7},{4,0},{5,1},{6,2},{7,3},{8,12},{9,13},{10,... | collective-permute-start | bytes 405512 | tf_op jit(solution)/shard_map/ppermute | solution.py:73
  56.8 1.4 %collective-permute-start.5 = (bf16[96,768]{1,0:T(8,128)(2,1)S(1)}, bf16[96,768]{1,0:T(8,128)(2,1)S(1)}, u32[]{:S(2)}, u32[]{:S(2)}) collective-permute-start(bf16[96,768]{1,0:T(8,128)(2,1)S(1)} %slice.76), channel_id=1, source_target_pairs={{0,2},{1,3},{2,0},{3,1},{4,6},{5,7},{6,4},{7,5},{8,10},{9,11},{10,... | collective-permute-start | bytes 442376 | tf_op jit(solution)/shard_map/ppermute | solution.py:73
  58.2 1.0 %collective-permute-done.7 = bf16[48,3072]{1,0:T(8,128)(2,1)S(1)} collective-permute-done((bf16[48,3072]{1,0:T(8,128)(2,1)S(1)}, bf16[48,3072]{1,0:T(8,128)(2,1)S(1)}, u32[]{:S(2)}, u32[]{:S(2)}) %collective-permute-start.7) | collective-permute-done | bytes 294944 | tf_op jit(solution)/shard_map/ppermute | solution.py:73
  59.3 2.9 %collective-permute-start.8 = (bf16[24,3072]{1,0:T(8,128)(2,1)S(1)}, bf16[24,3072]{1,0:T(8,128)(2,1)S(1)}, u32[]{:S(2)}, u32[]{:S(2)}) collective-permute-start(bf16[24,3072]{1,0:T(8,128)(2,1)S(1)} %slice.78), channel_id=1, source_target_pairs={{0,8},{1,9},{2,10},{3,11},{4,12},{5,13},{6,14},{7,15},{8,0},{9,1},... | collective-permute-start | bytes 442376 | tf_op jit(solution)/shard_map/ppermute | solution.py:73
  62.3 1.6 %collective-permute-start.12 = (bf16[48,768]{1,0:T(8,128)(2,1)S(1)}, bf16[48,768]{1,0:T(8,128)(2,1)S(1)}, u32[]{:S(2)}, u32[]{:S(2)}) collective-permute-start(bf16[48,768]{1,0:T(8,128)(2,1)S(1)} %slice.72), channel_id=1, source_target_pairs={{0,4},{1,5},{2,6},{3,7},{4,0},{5,1},{6,2},{7,3},{8,12},{9,13},{10,... | collective-permute-start | bytes 221192 | tf_op jit(solution)/shard_map/ppermute | solution.py:73
  63.9 1.5 %collective-permute-start.6 = (bf16[256,384]{1,0:T(8,128)(2,1)S(1)}, bf16[256,384]{1,0:T(8,128)(2,1)S(1)}, u32[]{:S(2)}, u32[]{:S(2)}) collective-permute-start(bf16[256,384]{1,0:T(8,128)(2,1)S(1)} %get-tuple-element.133), channel_id=1, source_target_pairs={{0,16},{16,0},{1,17},{17,1},{2,18},{18,2},{3,19},{19,3},{4,20},{20... | collective-permute-start | bytes 589832 | tf_op jit(solution)/shard_map/ppermute | solution.py:73
  65.3 1.4 %collective-permute-done.12 = bf16[48,768]{1,0:T(8,128)(2,1)S(1)} collective-permute-done((bf16[48,768]{1,0:T(8,128)(2,1)S(1)}, bf16[48,768]{1,0:T(8,128)(2,1)S(1)}, u32[]{:S(2)}, u32[]{:S(2)}) %collective-permute-start.12) | collective-permute-done | bytes 73760 | tf_op jit(solution)/shard_map/ppermute | solution.py:73
  66.7 2.9 %collective-permute-start.13 = (bf16[24,2176]{1,0:T(8,128)(2,1)S(1)}, bf16[24,2176]{1,0:T(8,128)(2,1)S(1)}, u32[]{:S(2)}, u32[]{:S(2)}) collective-permute-start(bf16[24,2176]{1,0:T(8,128)(2,1)S(1)} %pad_maximum_fusion), channel_id=1, source_target_pairs={{0,8},{1,9},{2,10},{3,11},{4,12},{5,13},{6,14},{7,15},{8,0},{9,1},... | collective-permute-start | bytes 313352 | tf_op jit(solution)/shard_map/ppermute | solution.py:73
  69.6 1.3 %collective-permute-start.9 = (bf16[24,3072]{1,0:T(8,128)(2,1)S(1)}, bf16[24,3072]{1,0:T(8,128)(2,1)S(1)}, u32[]{:S(2)}, u32[]{:S(2)}) collective-permute-start(bf16[24,3072]{1,0:T(8,128)(2,1)S(1)} %slice_add_fusion.4.refs_0_), channel_id=1, source_target_pairs={{0,16},{16,0},{1,17},{17,1},{2,18},{18,2},{3,19},{19,3},{4,20},{20... | collective-permute-start | bytes 442376 | tf_op jit(solution)/shard_map/ppermute | solution.py:73
  70.9 1.4 %collective-permute-done.13 = bf16[24,2176]{1,0:T(8,128)(2,1)S(1)} collective-permute-done((bf16[24,2176]{1,0:T(8,128)(2,1)S(1)}, bf16[24,2176]{1,0:T(8,128)(2,1)S(1)}, u32[]{:S(2)}, u32[]{:S(2)}) %collective-permute-start.13) | collective-permute-done | bytes 104480 | tf_op jit(solution)/shard_map/ppermute | solution.py:73
  72.4 3.2 %collective-permute-start.14 = (bf16[24,2176]{1,0:T(8,128)(2,1)S(1)}, bf16[24,2176]{1,0:T(8,128)(2,1)S(1)}, u32[]{:S(2)}, u32[]{:S(2)}) collective-permute-start(bf16[24,2176]{1,0:T(8,128)(2,1)S(1)} %fusion.2.refs_2_), channel_id=1, source_target_pairs={{0,16},{16,0},{1,17},{17,1},{2,18},{18,2},{3,19},{19,3},{4,20},{20... | collective-permute-start | bytes 313352 | tf_op jit(solution)/shard_map/ppermute | solution.py:73
  75.7 0.8 %fusion = bf16[1,512,384]{2,1,0:T(8,128)(2,1)} fusion(f32[512,384]{1,0:T(8,128)S(1)} %get-tuple-element.127, f32[256,384]{1,0:T(8,128)S(1)} %convert_element_type.6, pred[]{:T(512)S(6)} %eq.3), kind=kLoop, calls=%fused_computation.2 | loop fusion | flops 589824 | bytes 1572865 | tf_op jit(solution)/shard_map/reshape | solution.py:934
  76.5 1.8 %collective-permute-done.14.refs_3_ = bf16[24,2176]{1,0:T(8,128)(2,1)S(1)} collective-permute-done((bf16[24,2176]{1,0:T(8,128)(2,1)S(1)}, bf16[24,2176]{1,0:T(8,128)(2,1)S(1)}, u32[]{:S(2)}, u32[]{:S(2)}) %collective-permute-start.14) | collective-permute-done | bytes 104480 | tf_op jit(solution)/shard_map/ppermute | solution.py:73
  78.3 0.8 %final.1 = (f32[24,384]{1,0:T(8,128)}, f32[24,384]{1,0:T(8,128)}, f32[24,384]{1,0:T(8,128)}, f32[24,384]{1,0:T(8,128)}, f32[24,512]{1,0:T(8,128)}, /*index=5*/f3...) custom-call(bf16[24,3072]{1,0:T(8,128)(2,1)S(1)} %slice_add_fusion.4, ...), custom_call_target="tpu_custom_call" | custom-call | tf_op jit(solution)/shard_map/final/pallas_call | solution.py:911
  (58 shorter events, 1.3 us)
Async XLA Ops:
  1.6 7.9 %collective-permute-start = (bf16[256,384]{1,0:T(8,128)(2,1)S(1)}, bf16[256,384]{1,0:T(8,128)(2,1)S(1)}, u32[]{:S(2)}, u32[]{:S(2)}) collective-permute-start(bf16[256,384]{1,0:T(8,128)(2,1)S(1)} %dynamic-slice_bitcast_fusion), channel_id=1, source_target_pairs={{0,16},{16,0},{1,17},{17,1},{2,18},{18,2},{3,19},{19,3},{4,20},{20... | collective-permute-start | bytes 589832 | tf_op jit(solution)/shard_map/ppermute | solution.py:73
  4.6 4.9 %copy-start.1 = (bf16[384,384]{1,0:T(8,128)(2,1)S(1)}, bf16[384,384]{1,0:T(8,128)(2,1)}, u32[]{:S(2)}) copy-start(bf16[384,384]{1,0:T(8,128)(2,1)} %w_key.3) | copy-start | bytes 884740
  4.6 4.9 %copy-start.2 = (bf16[384,384]{1,0:T(8,128)(2,1)S(1)}, bf16[384,384]{1,0:T(8,128)(2,1)}, u32[]{:S(2)}) copy-start(bf16[384,384]{1,0:T(8,128)(2,1)} %w_value.3) | copy-start | bytes 884740
  4.6 4.9 %copy-start.8 = (bf16[4,384]{1,0:T(4,128)(2,1)S(1)}, bf16[4,384]{1,0:T(4,128)(2,1)}, u32[]{:S(2)}) copy-start(bf16[4,384]{1,0:T(4,128)(2,1)} %biases.3) | copy-start | bytes 9220
  4.6 13.4 %copy-start.6 = (bf16[1,512,384]{2,1,0:T(8,128)(2,1)S(1)}, bf16[1,512,384]{2,1,0:T(8,128)(2,1)}, u32[]{:S(2)}) copy-start(bf16[1,512,384]{2,1,0:T(8,128)(2,1)} %param.19) | copy-start | bytes 1179652
  4.6 13.4 %copy-start.7 = (bf16[384,384]{1,0:T(8,128)(2,1)S(1)}, bf16[384,384]{1,0:T(8,128)(2,1)}, u32[]{:S(2)}) copy-start(bf16[384,384]{1,0:T(8,128)(2,1)} %w_output.1) | copy-start | bytes 884740
  4.7 13.4 %copy-start.12 = (bf16[2,384]{1,0:T(2,128)(2,1)S(1)}, bf16[2,384]{1,0:T(2,128)(2,1)}, u32[]{:S(2)}) copy-start(bf16[2,384]{1,0:T(2,128)(2,1)} %shifts.1) | copy-start | bytes 4612
  9.6 8.5 %copy-start.3 = (bf16[1,512,384]{2,1,0:T(8,128)(2,1)S(1)}, bf16[1,512,384]{2,1,0:T(8,128)(2,1)}, u32[]{:S(2)}) copy-start(bf16[1,512,384]{2,1,0:T(8,128)(2,1)} %param.18) | copy-start | bytes 1179652
  9.6 8.5 %copy-start.4 = (bf16[384,1536]{1,0:T(8,128)(2,1)S(1)}, bf16[384,1536]{1,0:T(8,128)(2,1)}, u32[]{:S(2)}) copy-start(bf16[384,1536]{1,0:T(8,128)(2,1)} %w_inner.1) | copy-start | bytes 3538948
  9.6 8.5 %copy-start.5 = (bf16[1536,384]{1,0:T(8,128)(2,1)S(1)}, bf16[1536,384]{1,0:T(8,128)(2,1)}, u32[]{:S(2)}) copy-start(bf16[1536,384]{1,0:T(8,128)(2,1)} %w_outer.1) | copy-start | bytes 3538948
  9.6 8.5 %copy-start.9 = (bf16[1536]{0:T(1024)(128)(2,1)S(1)}, bf16[1536]{0:T(1024)(128)(2,1)}, u32[]{:S(2)}) copy-start(bf16[1536]{0:T(1024)(128)(2,1)} %inner_bias.1) | copy-start | bytes 9220
  9.6 8.5 %copy-start.10 = (s32[1,512]{1,0:T(1,128)S(1)}, s32[1,512]{1,0:T(1,128)}, u32[]{:S(2)}) copy-start(s32[1,512]{1,0:T(1,128)} %mask.1) | copy-start | bytes 6148
  9.6 8.5 %copy-start.11 = (bf16[2,384]{1,0:T(2,128)(2,1)S(1)}, bf16[2,384]{1,0:T(2,128)(2,1)}, u32[]{:S(2)}) copy-start(bf16[2,384]{1,0:T(2,128)(2,1)} %gains.1) | copy-start | bytes 4612
  9.6 8.5 %copy-start.13 = (bf16[384]{0:T(512)(128)(2,1)S(1)}, bf16[384]{0:T(512)(128)(2,1)}, u32[]{:S(2)}) copy-start(bf16[384]{0:T(512)(128)(2,1)} %outer_bias.1) | copy-start | bytes 2308
  26.2 13.5 %copy-start = (f32[512,384]{1,0:T(8,128)}, f32[512,384]{1,0:T(8,128)S(1)}, u32[]{:S(2)}) copy-start(f32[512,384]{1,0:T(8,128)S(1)} %get-tuple-element.125.d_first) | copy-start | bytes 2359300
  26.2 3.7 %collective-permute-start.1 = (bf16[192,3072]{1,0:T(8,128)(2,1)S(1)}, bf16[192,3072]{1,0:T(8,128)(2,1)S(1)}, u32[]{:S(2)}, u32[]{:S(2)}) collective-permute-start(bf16[192,3072]{1,0:T(8,128)(2,1)S(1)} %get-tuple-element.107), channel_id=1, source_target_pairs={{0,1},{1,0},{2,3},{3,2},{4,5},{5,4},{6,7},{7,6},{8,9},{9,8},{10,11... | collective-permute-start | bytes 3538952 | tf_op jit(solution)/shard_map/ppermute | solution.py:73
  30.3 15.8 %collective-permute-start.3 = (bf16[96,3072]{1,0:T(8,128)(2,1)S(1)}, bf16[96,3072]{1,0:T(8,128)(2,1)S(1)}, u32[]{:S(2)}, u32[]{:S(2)}) collective-permute-start(bf16[96,3072]{1,0:T(8,128)(2,1)S(1)} %slice.58), channel_id=1, source_target_pairs={{0,2},{1,3},{2,0},{3,1},{4,6},{5,7},{6,4},{7,5},{8,10},{9,11},{10,... | collective-permute-start | bytes 1769480 | tf_op jit(solution)/shard_map/ppermute | solution.py:73
  42.9 3.3 %collective-permute-start.2 = (bf16[192,2944]{1,0:T(8,128)(2,1)S(1)}, bf16[192,2944]{1,0:T(8,128)(2,1)S(1)}, u32[]{:S(2)}, u32[]{:S(2)}) collective-permute-start(bf16[192,2944]{1,0:T(8,128)(2,1)S(1)} %get-tuple-element.129), channel_id=1, source_target_pairs={{0,1},{1,0},{2,3},{3,2},{4,5},{5,4},{6,7},{7,6},{8,9},{9,8},{10,11... | collective-permute-start | bytes 3391496 | tf_op jit(solution)/shard_map/ppermute | solution.py:73
  46.5 8.4 %collective-permute-start.10 = (bf16[96,1408]{1,0:T(8,128)(2,1)S(1)}, bf16[96,1408]{1,0:T(8,128)(2,1)S(1)}, u32[]{:S(2)}, u32[]{:S(2)}) collective-permute-start(bf16[96,1408]{1,0:T(8,128)(2,1)S(1)} %slice.68), channel_id=1, source_target_pairs={{0,2},{1,3},{2,0},{3,1},{4,6},{5,7},{6,4},{7,5},{8,10},{9,11},{10,... | collective-permute-start | bytes 811016 | tf_op jit(solution)/shard_map/ppermute | solution.py:73
  48.3 8.4 %collective-permute-start.4 = (bf16[192,768]{1,0:T(8,128)(2,1)S(1)}, bf16[192,768]{1,0:T(8,128)(2,1)S(1)}, u32[]{:S(2)}, u32[]{:S(2)}) collective-permute-start(bf16[192,768]{1,0:T(8,128)(2,1)S(1)} %slice.60), channel_id=1, source_target_pairs={{0,16},{16,0},{1,17},{17,1},{2,18},{18,2},{3,19},{19,3},{4,20},{20... | collective-permute-start | bytes 884744 | tf_op jit(solution)/shard_map/ppermute | solution.py:73
  49.9 9.3 %collective-permute-start.7 = (bf16[48,3072]{1,0:T(8,128)(2,1)S(1)}, bf16[48,3072]{1,0:T(8,128)(2,1)S(1)}, u32[]{:S(2)}, u32[]{:S(2)}) collective-permute-start(bf16[48,3072]{1,0:T(8,128)(2,1)S(1)} %slice.64), channel_id=1, source_target_pairs={{0,4},{1,5},{2,6},{3,7},{4,0},{5,1},{6,2},{7,3},{8,12},{9,13},{10,... | collective-permute-start | bytes 884744 | tf_op jit(solution)/shard_map/ppermute | solution.py:73
  54.9 8.9 %collective-permute-start.11 = (bf16[48,1408]{1,0:T(8,128)(2,1)S(1)}, bf16[48,1408]{1,0:T(8,128)(2,1)S(1)}, u32[]{:S(2)}, u32[]{:S(2)}) collective-permute-start(bf16[48,1408]{1,0:T(8,128)(2,1)S(1)} %slice.80), channel_id=1, source_target_pairs={{0,4},{1,5},{2,6},{3,7},{4,0},{5,1},{6,2},{7,3},{8,12},{9,13},{10,... | collective-permute-start | bytes 405512 | tf_op jit(solution)/shard_map/ppermute | solution.py:73
  56.8 5.4 %collective-permute-start.5 = (bf16[96,768]{1,0:T(8,128)(2,1)S(1)}, bf16[96,768]{1,0:T(8,128)(2,1)S(1)}, u32[]{:S(2)}, u32[]{:S(2)}) collective-permute-start(bf16[96,768]{1,0:T(8,128)(2,1)S(1)} %slice.76), channel_id=1, source_target_pairs={{0,2},{1,3},{2,0},{3,1},{4,6},{5,7},{6,4},{7,5},{8,10},{9,11},{10,... | collective-permute-start | bytes 442376 | tf_op jit(solution)/shard_map/ppermute | solution.py:73
  59.3 10.3 %collective-permute-start.8 = (bf16[24,3072]{1,0:T(8,128)(2,1)S(1)}, bf16[24,3072]{1,0:T(8,128)(2,1)S(1)}, u32[]{:S(2)}, u32[]{:S(2)}) collective-permute-start(bf16[24,3072]{1,0:T(8,128)(2,1)S(1)} %slice.78), channel_id=1, source_target_pairs={{0,8},{1,9},{2,10},{3,11},{4,12},{5,13},{6,14},{7,15},{8,0},{9,1},... | collective-permute-start | bytes 442376 | tf_op jit(solution)/shard_map/ppermute | solution.py:73
  62.3 4.4 %collective-permute-start.12 = (bf16[48,768]{1,0:T(8,128)(2,1)S(1)}, bf16[48,768]{1,0:T(8,128)(2,1)S(1)}, u32[]{:S(2)}, u32[]{:S(2)}) collective-permute-start(bf16[48,768]{1,0:T(8,128)(2,1)S(1)} %slice.72), channel_id=1, source_target_pairs={{0,4},{1,5},{2,6},{3,7},{4,0},{5,1},{6,2},{7,3},{8,12},{9,13},{10,... | collective-permute-start | bytes 221192 | tf_op jit(solution)/shard_map/ppermute | solution.py:73
  63.9 11.8 %collective-permute-start.6 = (bf16[256,384]{1,0:T(8,128)(2,1)S(1)}, bf16[256,384]{1,0:T(8,128)(2,1)S(1)}, u32[]{:S(2)}, u32[]{:S(2)}) collective-permute-start(bf16[256,384]{1,0:T(8,128)(2,1)S(1)} %get-tuple-element.133), channel_id=1, source_target_pairs={{0,16},{16,0},{1,17},{17,1},{2,18},{18,2},{3,19},{19,3},{4,20},{20... | collective-permute-start | bytes 589832 | tf_op jit(solution)/shard_map/ppermute | solution.py:73
  66.7 5.6 %collective-permute-start.13 = (bf16[24,2176]{1,0:T(8,128)(2,1)S(1)}, bf16[24,2176]{1,0:T(8,128)(2,1)S(1)}, u32[]{:S(2)}, u32[]{:S(2)}) collective-permute-start(bf16[24,2176]{1,0:T(8,128)(2,1)S(1)} %pad_maximum_fusion), channel_id=1, source_target_pairs={{0,8},{1,9},{2,10},{3,11},{4,12},{5,13},{6,14},{7,15},{8,0},{9,1},... | collective-permute-start | bytes 313352 | tf_op jit(solution)/shard_map/ppermute | solution.py:73
  69.6 6.9 %collective-permute-start.9 = (bf16[24,3072]{1,0:T(8,128)(2,1)S(1)}, bf16[24,3072]{1,0:T(8,128)(2,1)S(1)}, u32[]{:S(2)}, u32[]{:S(2)}) collective-permute-start(bf16[24,3072]{1,0:T(8,128)(2,1)S(1)} %slice_add_fusion.4.refs_0_), channel_id=1, source_target_pairs={{0,16},{16,0},{1,17},{17,1},{2,18},{18,2},{3,19},{19,3},{4,20},{20... | collective-permute-start | bytes 442376 | tf_op jit(solution)/shard_map/ppermute | solution.py:73
  72.4 5.9 %collective-permute-start.14 = (bf16[24,2176]{1,0:T(8,128)(2,1)S(1)}, bf16[24,2176]{1,0:T(8,128)(2,1)S(1)}, u32[]{:S(2)}, u32[]{:S(2)}) collective-permute-start(bf16[24,2176]{1,0:T(8,128)(2,1)S(1)} %fusion.2.refs_2_), channel_id=1, source_target_pairs={{0,16},{16,0},{1,17},{17,1},{2,18},{18,2},{3,19},{19,3},{4,20},{20... | collective-permute-start | bytes 313352 | tf_op jit(solution)/shard_map/ppermute | solution.py:73
